TPU v7x, 256 devices: a whole 4x4x8 slice. The times are simulated.
256 devices in a mesh: bunch: 64 (over z, y_lo, x), dom: 4 (over y_hi, core).
Axes of the slice: x: 4, y: 4 (y_hi: 2, y_lo: 2; y = y_hi * 2 + y_lo), z: 8, core: 2. Of those that a mesh axis runs over, the one named last changes fastest.
Arguments:
- positions: float32 [2, 2, 128, 4096], P(None, None, 'bunch', 'dom'), may hold values from 0 to 127
- momenta: float32 [2, 2, 128, 4096], P(None, None, 'bunch', 'dom'), may hold values from -6 to 6
- kernel_hat: float32 [2, 2, 256, 256], replicated, may hold values from -1.2 to 1.2
- partners: int32 [2, 128, 16], P(None, 'bunch'), may hold values from 0 to 127, as said below
- offsets: int32 [2, 2, 128, 16], P(None, None, 'bunch'), may hold values from -32 to 32
- counts: int32 [2, 128], P(None, 'bunch'), may hold values from 1 to 16, as said below
Outputs:
- kicked: float32 [2, 2, 128, 4096], P(None, None, 'bunch', 'dom')
Inputs may be any that keep to these rules, and one draw needn't show every extreme that they name: partners[e, b, s] // 2 lies at most 2 from b // 2, counted around a cycle of 64 blocks. `counts`: the first bunch of each block of 2 bunches has all 16 slots live.
All inputs are finite; a program needn't handle non-finite values.
Results may differ from a plain program's by a relative error of at most 0.0003.
Values sent between devices are 32-bit elements; how exact they have to be, the bound alone decides.
No kernel may reach another device: no remote copies, remote signals or barrier semaphores. Data moves between devices by JAX's collectives and lax.ppermute only.
A program may use at most 64 MiB of HBM per device.

v0:
```python
import math

import jax
import jax.numpy as jnp
from jax import lax
from jax.sharding import PartitionSpec as P

HOPS = 2


HIGH = lax.Precision.HIGHEST


def passed_along(x, axis, by):
    peers = lax.axis_size(axis)
    return lax.ppermute(x, axis, [(i, (i + by) % peers) for i in range(peers)])


def split_up(x, dim, peers):
    lengths = x.shape
    tiles = x.reshape(*lengths[:dim], peers, lengths[dim] // peers, *lengths[dim + 1 :])
    return jnp.moveaxis(tiles, dim, 0)


def summed_on_arrival(x, axis, dim):
    tiles = split_up(x, dim, lax.axis_size(axis))
    arrived = lax.all_to_all(tiles, axis, split_axis=0, concat_axis=0, tiled=True)
    return arrived.sum(axis=0)


def copy_for_each(x, axis):
    copies = jnp.broadcast_to(x, (lax.axis_size(axis), *x.shape))
    return lax.all_to_all(copies, axis, split_axis=0, concat_axis=0, tiled=True)


def in_order(tiles, dim):
    tiles = jnp.moveaxis(tiles, 0, dim)
    lengths = tiles.shape
    return tiles.reshape(*lengths[:dim], lengths[dim] * lengths[dim + 1], *lengths[dim + 2 :])


def gathered_copies(x, axis, dim):
    tiles = copy_for_each(x, axis)
    return in_order(tiles, dim)


def hat_table(coord, cells):
    centres = jnp.arange(cells, dtype=jnp.float32)
    return jnp.maximum(0.0, 1.0 - jnp.abs(coord[:, None] - centres[None, :]))


def product(left, right):
    return jnp.dot(left, right, precision=HIGH, preferred_element_type=jnp.float32)


def deposit(coords, cells):
    weight_x = hat_table(coords[0], cells)
    weight_y = hat_table(coords[1], cells)
    return product(weight_x.T, weight_y)


def kick(coords, fields, moments, cells):
    weight_x = hat_table(coords[0], cells)
    weight_y = hat_table(coords[1], cells)
    field_x = jnp.sum(product(weight_x, fields[0]) * weight_y, axis=1)
    field_y = jnp.sum(product(weight_x, fields[1]) * weight_y, axis=1)
    return moments + jnp.stack([field_x, field_y])


def transform_fields(summed, kernel, cosine, sine, cells):
    padded_cells = cosine.shape[0]
    real_rows = product(cosine, summed)
    imag_rows = -product(sine, summed)
    spec_real = product(real_rows, cosine) + product(imag_rows, sine)
    spec_imag = product(imag_rows, cosine) - product(real_rows, sine)
    cos_rows = cosine[:cells]
    sin_rows = sine[:cells]
    cos_cols = cosine[:, :cells]
    sin_cols = sine[:, :cells]
    results = []
    for component in range(2):
        kernel_real = kernel[component, 0]
        kernel_imag = kernel[component, 1]
        prod_real = kernel_real * spec_real - kernel_imag * spec_imag
        prod_imag = kernel_real * spec_imag + kernel_imag * spec_real
        half_real = product(cos_rows, prod_real) - product(sin_rows, prod_imag)
        half_imag = product(cos_rows, prod_imag) + product(sin_rows, prod_real)
        result = product(half_real, cos_cols) - product(half_imag, sin_cols)
        results.append(result / float(padded_cells * padded_cells))
    return jnp.stack(results)


def window_of(grids):
    pieces = []
    for step in range(-HOPS, HOPS + 1):
        if step == 0:
            pieces.append(grids)
        else:
            pieces.append(passed_along(grids, "bunch", -step))
    return jnp.stack(pieces)


def per_device(positions, momenta, kernel_hat, partners, offsets, counts):
    bpb = positions.shape[2]
    local = 2 * bpb
    parts = positions.shape[3]
    padded_cells = kernel_hat.shape[-1]
    cells = padded_cells // 2
    slots = partners.shape[-1]
    device = lax.axis_index("bunch")
    ndev = lax.axis_size("bunch")
    coords = jnp.transpose(positions.reshape(2, local, parts), (1, 0, 2))
    partial_value = lax.map(lambda item: deposit(item, cells), coords)
    shares = summed_on_arrival(partial_value, "dom", 0)
    window_part = window_of(shares)
    window = gathered_copies(window_part, "dom", 1)
    share_len = local // lax.axis_size("dom")
    targets = lax.axis_index("dom") * share_len + jnp.arange(share_len, dtype=jnp.int32)
    flat = window.reshape(-1, cells, cells)
    indices = jnp.arange(padded_cells, dtype=jnp.int32)
    angle = (indices[:, None] * indices[None, :] % padded_cells).astype(jnp.float32) * (
        2.0 * math.pi / padded_cells
    )
    cosine = jnp.cos(angle)
    sine = jnp.sin(angle)
    grid_cells = jnp.arange(cells, dtype=jnp.int32)
    slot_ids = jnp.arange(slots, dtype=jnp.int32)

    def field_of(target):
        beam = target // bpb
        member = target % bpb
        row = partners[beam, member]
        shift_x = offsets[0, beam, member]
        shift_y = offsets[1, beam, member]
        live_count = counts[beam, member]
        other = (1 - beam) * bpb
        relative = (row // bpb - device + HOPS) % ndev
        chosen_rows = relative * local + other + row % bpb
        chosen = jnp.take(flat, chosen_rows, axis=0)
        live = (slot_ids < live_count).astype(jnp.float32)
        target_x = (grid_cells[None, None, :] + shift_x[:, None, None]) % padded_cells
        target_y = (grid_cells[None, None, :] + shift_y[:, None, None]) % padded_cells
        place_x = (indices[None, :, None] == target_x).astype(jnp.float32) * live[:, None, None]
        place_y = (indices[None, :, None] == target_y).astype(jnp.float32)
        moved = jnp.einsum(
            "sri,sij->srj", place_x, chosen, precision=HIGH, preferred_element_type=jnp.float32
        )
        summed = jnp.einsum(
            "srj,sqj->rq", moved, place_y, precision=HIGH, preferred_element_type=jnp.float32
        )
        return transform_fields(summed, kernel_hat, cosine, sine, cells)

    fields = lax.map(field_of, targets)
    fields = jax.tree.map(lambda part: gathered_copies(part, "dom", 0), fields)
    moments = jnp.transpose(momenta.reshape(2, local, parts), (1, 0, 2))
    kicked = lax.map(lambda item: kick(item[0], item[1], item[2], cells), (coords, fields, moments))
    return jnp.transpose(kicked, (1, 0, 2)).reshape(2, 2, bpb, parts)


def solution(mesh):
    in_specs = (
        P(None, None, "bunch", "dom"),
        P(None, None, "bunch", "dom"),
        P(),
        P(None, "bunch", None),
        P(None, None, "bunch", None),
        P(None, "bunch"),
    )
    out_specs = P(None, None, "bunch", "dom")
    return jax.shard_map(
        per_device, mesh=mesh, in_specs=in_specs, out_specs=out_specs, check_vma=False
    )
```

profile of v0, /device:TPU:1, one launch (start us, length us, event | category | flops | bytes accessed | tf_op | source)
XLA Modules:
  0.0 96.7 jit_solution(2971377880383530361)
XLA Ops:
  0.0 0.8 copy.18
  0.8 5.4 %while.24 = (s32[]{:T(128)}, f32[4,128,128]{2,1,0:T(8,128)S(1)}, f32[4,2,1024]{2,1,0:T(2,128)S(1)}, s32[]{:T(128)}, s32[]{:T(128)}, /*index=5*/s32[]{}) while((s32[]{:T(128)}, f32[4,128,128]{2,1,0:T(8,128)S(1)}, f32[4,2,1024]{2,1,0:T(2,128)S(1)}, s32[]{:T(128)}, s32[]{:T(128)}, /*index=5*/s32[]{}) %tuple.52), condition=%wide.region_1.2_spmd, body=%wide.region_0.1_spmd.sunk | while | flops 202375168 | bytes 90205 | solution.py:113
  0.8 1.3 %fusion.158 = f32[4,128,128]{2,1,0:T(8,128)S(1)} fusion(f32[4,128,128]{2,1,0:T(8,128)S(1)} %get-tuple-element.188, s32[]{:T(128)} %get-tuple-element.187, f32[1024]{0:T(1024)S(1)} %bitcast.170, f32[1024]{0:T(1024)S(1)} %bitcast.169), kind=kOutput, calls=%fused_computation.2.clone.1 | convolution fusion | flops 202375168 | bytes 73732 | tf_op jit(solution)/shard_map/while/body/eval_jaxpr/dot_general | solution.py:53
  2.2 1.3 %fusion.158 = f32[4,128,128]{2,1,0:T(8,128)S(1)} fusion(f32[4,128,128]{2,1,0:T(8,128)S(1)} %get-tuple-element.188, s32[]{:T(128)} %get-tuple-element.187, f32[1024]{0:T(1024)S(1)} %bitcast.170, f32[1024]{0:T(1024)S(1)} %bitcast.169), kind=kOutput, calls=%fused_computation.2.clone.1 | convolution fusion | flops 202375168 | bytes 73732 | tf_op jit(solution)/shard_map/while/body/eval_jaxpr/dot_general | solution.py:53
  3.5 1.3 %fusion.158 = f32[4,128,128]{2,1,0:T(8,128)S(1)} fusion(f32[4,128,128]{2,1,0:T(8,128)S(1)} %get-tuple-element.188, s32[]{:T(128)} %get-tuple-element.187, f32[1024]{0:T(1024)S(1)} %bitcast.170, f32[1024]{0:T(1024)S(1)} %bitcast.169), kind=kOutput, calls=%fused_computation.2.clone.1 | convolution fusion | flops 202375168 | bytes 73732 | tf_op jit(solution)/shard_map/while/body/eval_jaxpr/dot_general | solution.py:53
  4.9 1.3 %fusion.158 = f32[4,128,128]{2,1,0:T(8,128)S(1)} fusion(f32[4,128,128]{2,1,0:T(8,128)S(1)} %get-tuple-element.188, s32[]{:T(128)} %get-tuple-element.187, f32[1024]{0:T(1024)S(1)} %bitcast.170, f32[1024]{0:T(1024)S(1)} %bitcast.169), kind=kOutput, calls=%fused_computation.2.clone.1 | convolution fusion | flops 202375168 | bytes 73732 | tf_op jit(solution)/shard_map/while/body/eval_jaxpr/dot_general | solution.py:53
  6.2 12.3 %all_to_all.15 = f32[4,1,128,128]{3,2,1,0:T(8,128)S(1)} all-to-all(f32[4,1,128,128]{3,2,1,0:T(8,128)S(1)} %bitcast.166), channel_id=1, replica_groups=mesh['bunch'=64,'dom'=4] {'dom'}, dimensions={0} | all-to-all | bytes 524288 | tf_op jit(solution)/shard_map/all_to_all | solution.py:27
  18.5 2.8 %collective-permute-start = (f32[1,128,128]{2,1,0:T(8,128)S(1)}, f32[1,128,128]{2,1,0:T(8,128)S(1)}, u32[]{:S(2)}, u32[]{:S(2)}) collective-permute-start(f32[1,128,128]{2,1,0:T(8,128)S(1)} %bitcast.162), channel_id=1, source_target_pairs={{0,8},{4,12},{8,16},{12,20},{16,24},{20,28},{24,32},{28,36},{32,40... | collective-permute-start | bytes 196616 | tf_op jit(solution)/shard_map/ppermute | solution.py:16
  21.3 0.3 collective-permute-start.1
  21.6 5.4 %collective-permute-start.2 = (f32[1,128,128]{2,1,0:T(8,128)S(1)}, f32[1,128,128]{2,1,0:T(8,128)S(1)}, u32[]{:S(2)}, u32[]{:S(2)}) collective-permute-start(f32[1,128,128]{2,1,0:T(8,128)S(1)} %bitcast.164), channel_id=1, source_target_pairs={{0,252},{4,0},{8,4},{12,8},{16,12},{20,16},{24,20},{28,24},{32,28}... | collective-permute-start | bytes 196616 | tf_op jit(solution)/shard_map/ppermute | solution.py:16
  27.0 1.8 %collective-permute-start.3 = (f32[1,128,128]{2,1,0:T(8,128)S(1)}, f32[1,128,128]{2,1,0:T(8,128)S(1)}, u32[]{:S(2)}, u32[]{:S(2)}) collective-permute-start(f32[1,128,128]{2,1,0:T(8,128)S(1)} %bitcast.165), channel_id=1, source_target_pairs={{0,248},{4,252},{8,0},{12,4},{16,8},{20,12},{24,16},{28,20},{32,24... | collective-permute-start | bytes 196616 | tf_op jit(solution)/shard_map/ppermute | solution.py:16
  28.8 0.4 collective-permute-done.1
  29.3 2.3 %collective-permute-done.3 = f32[1,128,128]{2,1,0:T(8,128)S(1)} collective-permute-done((f32[1,128,128]{2,1,0:T(8,128)S(1)}, f32[1,128,128]{2,1,0:T(8,128)S(1)}, u32[]{:S(2)}, u32[]{:S(2)}) %collective-permute-start.3) | collective-permute-done | bytes 65568 | tf_op jit(solution)/shard_map/ppermute | solution.py:16
  31.6 1.2 %broadcast_in_dim.52 = f32[4,5,1,128,128]{4,3,1,2,0:T(8,128)} broadcast(f32[5,128,128]{2,1,0:T(8,128)S(1)} %bitcast.160), dimensions={1,3,4} | broadcast | bytes 1638400 | tf_op jit(solution)/shard_map/broadcast_in_dim | solution.py:32
  32.9 6.5 %all-to-all-start.1 = ((f32[4,5,1,128,128]{4,3,1,2,0:T(8,128)}), f32[4,5,1,128,128]{4,3,1,2,0:T(8,128)S(1)}, u32[]{:S(2)}, u32[]{:S(2)}) async-start(f32[4,5,1,128,128]{4,3,1,2,0:T(8,128)} %broadcast_in_dim.52), calls=%async_computation.1 | async-start | bytes 2621440 | tf_op jit(solution)/shard_map/all_to_all | solution.py:33
  39.4 0.6 dynamic_slice.34
  40.0 0.7 compare_and_fusion
  40.7 0.7 fusion.103
  41.4 1.0 fusion.58
  42.4 1.0 %fusion.57 = f32[256,256]{1,0:T(8,128)S(1)} fusion(), kind=kLoop, calls=%fused_computation.93 | loop fusion | flops 917504 | bytes 262144 | tf_op jit(solution)/shard_map/sin | solution.py:125
  43.4 13.9 %all-to-all-done.1 = f32[4,5,1,128,128]{4,3,1,2,0:T(8,128)S(1)} async-done(((f32[4,5,1,128,128]{4,3,1,2,0:T(8,128)}), f32[4,5,1,128,128]{4,3,1,2,0:T(8,128)S(1)}, u32[]{:S(2)}, u32[]{:S(2)}) %all-to-all-start.1) | async-done | bytes 1310752 | tf_op jit(solution)/shard_map/all_to_all | solution.py:33
  57.4 0.6 gather_fusion
  58.1 2.3 %fusion.32 = f32[16,256,128]{2,1,0:T(8,128)S(1)} fusion(f32[16,128,128]{2,1,0:T(8,128)S(1)} %gather_fusion, f32[16]{0:T(128)S(1)} %get-tuple-element.122, s32[16,128]{1,0:T(8,128)S(1)} %get-tuple-element.120, pred[16]{0:T(512)(128)(4,1)S(1)} %get-tuple-element.121), kind=kOutput, calls=%fused_computation.46 | convolution fusion | flops 806617088 | bytes 3154000 | tf_op jit(solution)/shard_map/while/body/eval_jaxpr/sri,sij->srj/dot_general | solution.py:145
  60.3 1.4 %fusion.35 = f32[256,256]{1,0:T(8,128)S(1)} fusion(f32[16,256,128]{2,1,0:T(8,128)S(1)} %fusion.32, s32[16,128]{1,0:T(8,128)S(1)} %get-tuple-element.119), kind=kOutput, calls=%fused_computation.53 | convolution fusion | flops 1611137024 | bytes 2367488 | tf_op jit(solution)/shard_map/while/body/eval_jaxpr/srj,sqj->rq/dot_general | solution.py:148
  61.7 1.6 %convolution_negate_fusion = f32[256,256]{1,0:T(8,128)S(1)} fusion(f32[256,256]{1,0:T(8,128)S(1)} %fusion.35), kind=kOutput, calls=%fused_computation.52 | convolution fusion | flops 202309632 | bytes 524288 | tf_op jit(solution)/shard_map/while/body/eval_jaxpr/dot_general | solution.py:53
  63.3 1.8 %fusion.63 = f32[256,256]{1,0:T(8,128)S(1)} fusion(f32[256,256]{1,0:T(8,128)S(1)} %fusion.35), kind=kOutput, calls=%fused_computation.97 | convolution fusion | flops 202244096 | bytes 524288 | tf_op jit(solution)/shard_map/while/body/eval_jaxpr/dot_general | solution.py:53
  65.2 1.3 %fusion.59 = f32[256,256]{1,0:T(8,128)S(1)} fusion(f32[256,256]{1,0:T(8,128)S(1)} %convolution_negate_fusion), kind=kOutput, calls=%fused_computation.95 | convolution fusion | flops 202244096 | bytes 524288 | tf_op jit(solution)/shard_map/while/body/eval_jaxpr/dot_general | solution.py:53
  66.5 1.3 %fusion.61 = f32[256,256]{1,0:T(8,128)S(1)} fusion(f32[256,256]{1,0:T(8,128)S(1)} %fusion.63), kind=kOutput, calls=%fused_computation.96 | convolution fusion | flops 202244096 | bytes 524288 | tf_op jit(solution)/shard_map/while/body/eval_jaxpr/dot_general | solution.py:53
  67.9 1.4 %convolution_subtract_fusion = f32[256,256]{1,0:T(8,128)S(1)} fusion(f32[256,256]{1,0:T(8,128)S(1)} %fusion.59, f32[256,256]{1,0:T(8,128)S(1)} %fusion.63), kind=kOutput, calls=%fused_computation.50 | convolution fusion | flops 202309632 | bytes 786432 | tf_op jit(solution)/shard_map/while/body/eval_jaxpr/dot_general | solution.py:53
  69.2 2.6 %fusion.53 = (f32[256,256]{1,0:T(8,128)S(1)}, f32[256,256]{1,0:T(8,128)S(1)}, f32[256,256]{1,0:T(8,128)S(1)}, f32[256,256]{1,0:T(8,128)S(1)}) fusion(f32[256,256]{1,0:T(8,128)S(1)} %convolution_subtract_fusion, f32[2,2,256,256]{3,2,1,0:T(8,128)} %param.12, f32[256,256]{1,0:T(8,128)S(1)} %fusion.61, f32[256,256]{1,0:T(8,128)S(1)} %convolution_negate_fusion), kind=kOutput, calls=%fused_computation.86 | convolution fusion | flops 203096064 | bytes 2883584 | tf_op jit(solution)/shard_map/while/body/eval_jaxpr/dot_general | solution.py:53
  71.9 0.3 fusion.82
  72.5 0.3 convolution_add_fusion.2
  72.8 0.3 convolution_subtract_fusion.2
  73.3 0.3 fusion.78
  73.9 0.3 convolution_add_fusion.1
  75.3 0.8 broadcast_in_dim.54
  76.2 4.3 %all-to-all-start.2 = ((f32[4,1,2,128,128]{4,3,2,1,0:T(8,128)}), f32[4,1,2,128,128]{4,3,2,1,0:T(8,128)S(1)}, u32[]{:S(2)}, u32[]{:S(2)}) async-start(f32[4,1,2,128,128]{4,3,2,1,0:T(8,128)} %broadcast_in_dim.54), calls=%async_computation.2 | async-start | bytes 1048576 | tf_op jit(solution)/shard_map/all_to_all | solution.py:33
  80.5 9.4 %all-to-all-done.2 = f32[4,1,2,128,128]{4,3,2,1,0:T(8,128)S(1)} async-done(((f32[4,1,2,128,128]{4,3,2,1,0:T(8,128)}), f32[4,1,2,128,128]{4,3,2,1,0:T(8,128)S(1)}, u32[]{:S(2)}, u32[]{:S(2)}) %all-to-all-start.2) | async-done | bytes 524320 | tf_op jit(solution)/shard_map/all_to_all | solution.py:33
  90.0 6.1 %while.25 = (s32[]{:T(128)}, f32[4,2,1024]{2,1,0:T(2,128)S(1)}, f32[4,2,1024]{2,1,0:T(2,128)S(1)}, f32[4,2,1024]{2,1,0:T(2,128)S(1)}, f32[4,2,128,128]{3,2,1,0:T(8,128)S(1)}, /*index=5*/s32[]{:T(128)}, s32[]{:T(128)}, s32[]{}) while((s32[]{:T(128)}, f32[4,2,1024]{2,1,0:T(2,128)S(1)}, f32[4,2,1024]{2,1,0:T(2,128)S(1)}, ...), condition=%wide.region_6.7_spmd, body=%wide.region_3.6_spmd.sunk | while | flops 405276672 | bytes 196729 | solution.py:156
  90.0 0.7 fusion.159
  90.7 0.7 fusion.160
  91.5 0.7 fusion.159
  92.2 0.7 fusion.160
  93.1 0.7 fusion.159
  93.8 0.7 fusion.160
  94.6 0.7 fusion.159
  95.3 0.7 fusion.160
  96.1 0.6 copy.25
  (41 shorter events, 2.5 us)
Async XLA Ops:
  18.5 10.3 %collective-permute-start = (f32[1,128,128]{2,1,0:T(8,128)S(1)}, f32[1,128,128]{2,1,0:T(8,128)S(1)}, u32[]{:S(2)}, u32[]{:S(2)}) collective-permute-start(f32[1,128,128]{2,1,0:T(8,128)S(1)} %bitcast.162), channel_id=1, source_target_pairs={{0,8},{4,12},{8,16},{12,20},{16,24},{20,28},{24,32},{28,36},{32,40... | collective-permute-start | bytes 196616 | tf_op jit(solution)/shard_map/ppermute | solution.py:16
  21.3 7.9 %collective-permute-start.1 = (f32[1,128,128]{2,1,0:T(8,128)S(1)}, f32[1,128,128]{2,1,0:T(8,128)S(1)}, u32[]{:S(2)}, u32[]{:S(2)}) collective-permute-start(f32[1,128,128]{2,1,0:T(8,128)S(1)} %bitcast.163), channel_id=1, source_target_pairs={{0,4},{4,8},{8,12},{12,16},{16,20},{20,24},{24,28},{28,32},{32,36}... | collective-permute-start | bytes 196616 | tf_op jit(solution)/shard_map/ppermute | solution.py:16
  21.6 7.7 %collective-permute-start.2 = (f32[1,128,128]{2,1,0:T(8,128)S(1)}, f32[1,128,128]{2,1,0:T(8,128)S(1)}, u32[]{:S(2)}, u32[]{:S(2)}) collective-permute-start(f32[1,128,128]{2,1,0:T(8,128)S(1)} %bitcast.164), channel_id=1, source_target_pairs={{0,252},{4,0},{8,4},{12,8},{16,12},{20,16},{24,20},{28,24},{32,28}... | collective-permute-start | bytes 196616 | tf_op jit(solution)/shard_map/ppermute | solution.py:16
  27.0 4.6 %collective-permute-start.3 = (f32[1,128,128]{2,1,0:T(8,128)S(1)}, f32[1,128,128]{2,1,0:T(8,128)S(1)}, u32[]{:S(2)}, u32[]{:S(2)}) collective-permute-start(f32[1,128,128]{2,1,0:T(8,128)S(1)} %bitcast.165), channel_id=1, source_target_pairs={{0,248},{4,252},{8,0},{12,4},{16,8},{20,12},{24,16},{28,20},{32,24... | collective-permute-start | bytes 196616 | tf_op jit(solution)/shard_map/ppermute | solution.py:16
  31.6 7.8 %copy-start.2 = (s32[2,2]{1,0:T(2,128)S(1)}, s32[2,2]{1,0:T(2,128)}, u32[]{:S(2)}) copy-start(s32[2,2]{1,0:T(2,128)} %param.15) | copy-start | bytes 52
  31.6 8.4 %copy-start.1 = (s32[2,2,16]{2,1,0:T(2,128)S(1)}, s32[2,2,16]{2,1,0:T(2,128)}, u32[]{:S(2)}) copy-start(s32[2,2,16]{2,1,0:T(2,128)} %param.13) | copy-start | bytes 772
  32.9 24.4 %all-to-all-start.1 = ((f32[4,5,1,128,128]{4,3,1,2,0:T(8,128)}), f32[4,5,1,128,128]{4,3,1,2,0:T(8,128)S(1)}, u32[]{:S(2)}, u32[]{:S(2)}) async-start(f32[4,5,1,128,128]{4,3,1,2,0:T(8,128)} %broadcast_in_dim.52), calls=%async_computation.1 | async-start | bytes 2621440 | tf_op jit(solution)/shard_map/all_to_all | solution.py:33
  73.9 6.6 %copy-start = (f32[2,2,2,1024]{3,2,1,0:T(2,128)S(1)}, f32[2,2,2,1024]{3,2,1,0:T(2,128)}, u32[]{:S(2)}) copy-start(f32[2,2,2,1024]{3,2,1,0:T(2,128)} %param.11) | copy-start | bytes 98308
  76.2 13.8 %all-to-all-start.2 = ((f32[4,1,2,128,128]{4,3,2,1,0:T(8,128)}), f32[4,1,2,128,128]{4,3,2,1,0:T(8,128)S(1)}, u32[]{:S(2)}, u32[]{:S(2)}) async-start(f32[4,1,2,128,128]{4,3,2,1,0:T(8,128)} %broadcast_in_dim.54), calls=%async_computation.2 | async-start | bytes 1048576 | tf_op jit(solution)/shard_map/all_to_all | solution.py:33
where the time goes:
time: 97.1 us; the launch traced here: 96.7 us
  matrix products  28.2 us (29%)
  waiting for transfers between devices  26.1 us (27%)
  starting transfers between devices  21.2 us (22%)
  blocking collectives  12.3 us (13%)
  local copies, waits for them, and re-layouts  5.69 us (6%)
  other arithmetic  2.85 us (3%)
    dot_general x30, matrix products, product(): jnp.dot(left, right, precision=HIGH, preferred_element_type=jnp.float32)  24.5 us
    all_to_all x2, waiting for transfers between devices, copy_for_each(): return lax.all_to_all(copies, axis, split_axis=0, concat_axis=0, tiled=True)  23.3 us
    all_to_all x1, blocking collectives, summed_on_arrival(): lax.all_to_all(tiles, axis, split_axis=0, concat_axis=0, tiled=True)  12.3 us
    all_to_all x2, starting transfers between devices, copy_for_each(): return lax.all_to_all(copies, axis, split_axis=0, concat_axis=0, tiled=True)  10.8 us
    ppermute x4, starting transfers between devices, passed_along(): return lax.ppermute(x, axis, [(i, (i + by) % peers) for i in range(peers)])  10.3 us
    ppermute x4, waiting for transfers between devices, passed_along(): return lax.ppermute(x, axis, [(i, (i + by) % peers) for i in range(peers)])  2.75 us
    dot_general x1, matrix products, field_of(): jnp.einsum('sri,sij->srj', place_x, chosen, precision=HIGH, preferred_ele...  2.25 us
    broadcast_in_dim x2, local copies, waits for them, and re-layouts, copy_for_each(): copies = jnp.broadcast_to(x, (lax.axis_size(axis), *x.shape))  2.06 us
  transfers between devices with their start and end apart: 6, of which 4 were waited for; matrix products, arithmetic and copies ran while one was open for 4% of the time, Pallas kernels for 0%

commit v1 on v0

v1 whole, which is shorter than its diff:
```python
import jax
import jax.numpy as jnp
import numpy as np
from jax import lax
from jax.experimental import pallas as pl
from jax.experimental.pallas import tpu as pltpu
from jax.sharding import PartitionSpec as P

GRID = 128
PAD = 256
OFFSET = 32
SPAN = GRID + 2 * OFFSET
BF = jnp.bfloat16
F32 = jnp.float32


def split_const(m):
    hi = m.astype(BF)
    lo = (m - hi.astype(np.float64)).astype(BF)
    return np.asarray(hi), np.asarray(lo)


def dft_tables():
    k = np.arange(PAD)
    w = 2.0 * np.pi / PAD
    r = np.arange(SPAN) - OFFSET
    ang = w * ((k[:, None] * r[None, :]) % PAD)
    hi, lo = split_const(np.concatenate([np.cos(ang), -np.sin(ang)], 0))
    rows = np.concatenate([hi, hi, lo], 1)
    r = np.arange(PAD) - OFFSET
    ang = w * ((r[:, None] * k[None, :]) % PAD)
    hi, lo = split_const(np.concatenate([np.cos(ang), np.sin(ang)], 1))
    cols = np.concatenate([hi, hi, lo], 0)
    j = np.arange(GRID)
    ang = w * ((k[:, None] * j[None, :]) % PAD)
    hi, lo = split_const(np.concatenate([np.cos(ang), np.sin(ang)], 1))
    back_cols = np.concatenate([hi, hi, lo], 0)
    ang = ang.T
    hi, lo = split_const(np.concatenate([np.cos(ang), -np.sin(ang)], 1) / (PAD * PAD))
    back_rows = np.concatenate([hi, hi, lo], 1)
    return rows, cols, back_cols, back_rows


def hilo(v):
    hi = v.astype(BF)
    lo = (v - hi.astype(F32)).astype(BF)
    return hi, lo


def dot(a, b):
    return jnp.dot(a, b, preferred_element_type=F32)


def hat(coord, lanes):
    cells = lax.broadcasted_iota(jnp.int32, (GRID, lanes), 0).astype(F32)
    return jnp.maximum(0.0, 1.0 - jnp.abs(coord - cells))


def deposit_body(where_ref, a_ref, b_ref, *rest):
    if len(rest) == 4:
        prev_ref, out_ref, tx, ty = rest
    else:
        prev_ref = None
        out_ref, tx, ty = rest
    e = 1 - where_ref[1]
    n = a_ref.shape[-1]
    for m in range(2):
        for i, ref in enumerate((a_ref, b_ref)):
            for coord, table in ((0, tx), (1, ty)):
                hi, lo = hilo(hat(ref[coord, e, pl.ds(m, 1), :], n))
                table[m, 0:GRID, i * n : (i + 1) * n] = hi
                table[m, GRID:, i * n : (i + 1) * n] = lo
        acc = lax.dot_general(
            tx[m], ty[m], (((1,), (1,)), ((), ())), preferred_element_type=F32
        )
        total = (acc[:GRID, :GRID] + acc[GRID:, GRID:]) + (acc[:GRID, GRID:] + acc[GRID:, :GRID])
        if prev_ref is not None:
            total = total + prev_ref[m]
        out_ref[m] = total


def deposit(where, a, b, prev=None):
    n = a.shape[-1]
    vm = pl.BlockSpec(memory_space=pltpu.VMEM)
    args = [where, a, b] + ([] if prev is None else [prev])
    return pl.pallas_call(
        deposit_body,
        out_shape=jax.ShapeDtypeStruct((2, GRID, GRID), F32),
        in_specs=[pl.BlockSpec(memory_space=pltpu.SMEM)] + [vm] * (len(args) - 1),
        out_specs=vm,
        scratch_shapes=[pltpu.VMEM((2, 2 * GRID, 2 * n), BF)] * 2,
        compiler_params=pltpu.CompilerParams(vmem_limit_bytes=16 * 1024 * 1024),
        name="deposit_first" if prev is None else "deposit_second",
    )(*args)


def field_body(
    where_ref, partners_ref, offsets_ref, counts_ref,
    own_ref, r1_ref, r2_ref, s1_ref, s2_ref,
    kernel_hbm, rows_hbm, cols_hbm, bcols_hbm, brows_hbm,
    pa_ref, pc_ref, py_ref, pyc_ref,
    near_ref, far_ref,
    grids, source, rows_ref, cols_ref, kern, bcols_ref, brows_ref, gsem, ksem,
):
    b = where_ref[0]
    h = where_ref[1]
    c = where_ref[2]
    ndev = where_ref[3]
    places = (2, 1 + 2 * c, 4 * c, 3 - 2 * c, 4 - 4 * c)
    copies = [
        pltpu.make_async_copy(ref, grids.at[place], gsem.at[i])
        for i, (ref, place) in enumerate(zip((own_ref, r1_ref, r2_ref, s1_ref, s2_ref), places))
    ]
    fixed = [
        pltpu.make_async_copy(src, dst, ksem.at[i])
        for i, (src, dst) in enumerate((
            (rows_hbm, rows_ref), (cols_hbm, cols_ref), (kernel_hbm, kern),
            (bcols_hbm, bcols_ref), (brows_hbm, brows_ref),
        ))
    ]
    for copy in copies + fixed:
        copy.start()
    source[...] = jnp.zeros_like(source)
    lane = lax.broadcasted_iota(jnp.int32, (GRID, GRID), 1)
    for copy in copies:
        copy.wait()

    def add_slot(s, carry):
        p = partners_ref[h, c, s]
        rel = lax.rem(p // 2 - b + 2 + 2 * ndev, ndev)
        r0 = offsets_ref[0, h, c, s] + OFFSET
        c0 = offsets_ref[1, h, c, s] + OFFSET
        grid = grids[rel, p % 2]
        turned = pltpu.roll(grid, c0, 1)
        low = jnp.where(lane >= c0, turned, 0.0)
        high = jnp.where(lane >= c0, 0.0, turned)
        source[0, pl.ds(r0, GRID), :] += low
        source[1, pl.ds(r0, GRID), :] += high
        return carry

    lax.fori_loop(0, counts_ref[h, c], add_slot, 0)
    hi, lo = hilo(jnp.concatenate([source[0, 0:SPAN, :], source[1, 0:SPAN, :]], 1))
    fixed[0].wait()
    half = dot(rows_ref[...], jnp.concatenate([hi, lo, hi], 0))
    hi, lo = hilo(half)
    fixed[1].wait()
    spec = dot(jnp.concatenate([hi, lo, hi], 1), cols_ref[...])
    spec_r = spec[:PAD, :PAD] + spec[PAD:, PAD:]
    spec_i = spec[PAD:, :PAD] - spec[:PAD, PAD:]
    fixed[2].wait()
    fixed[3].wait()
    back = []
    for comp in range(2):
        kr = kern[comp, 0]
        ki = kern[comp, 1]
        prod = jnp.concatenate([kr * spec_r - ki * spec_i, kr * spec_i + ki * spec_r], 0)
        hi, lo = hilo(prod)
        t = dot(jnp.concatenate([hi, lo, hi], 1), bcols_ref[...])
        re = t[:PAD, :GRID] - t[PAD:, GRID:]
        im = t[:PAD, GRID:] + t[PAD:, :GRID]
        back.append(jnp.concatenate([re, im], 0))
    hi, lo = hilo(jnp.concatenate(back, 1))
    fixed[4].wait()
    field = dot(brows_ref[...], jnp.concatenate([hi, lo, hi], 0))
    field = jnp.concatenate([field[:, :GRID], field[:, GRID:]], 0)
    hi, lo = hilo(field)
    maps = jnp.concatenate([hi, lo, hi], 1)
    n = pa_ref.shape[-1]
    chunk = 512
    for ref, out_ref, place in (
        (pa_ref, near_ref, 0), (pc_ref, near_ref, 1), (py_ref, far_ref, 0), (pyc_ref, far_ref, 1)
    ):
        for start in range(0, n, chunk):
            both = ref[0, h, :, start : start + chunk]
            x = jnp.where(c == 0, both[0:1], both[1:2])
            both = ref[1, h, :, start : start + chunk]
            y = jnp.where(c == 0, both[0:1], both[1:2])
            hi, lo = hilo(hat(y, chunk))
            t = dot(maps, jnp.concatenate([hi, hi, lo], 0))
            wx = hat(x, chunk)
            kx = jnp.sum(t[:GRID] * wx, axis=0, keepdims=True)
            ky = jnp.sum(t[GRID:] * wx, axis=0, keepdims=True)
            out_ref[place, 0:1, start : start + chunk] = kx
            out_ref[place, 1:2, start : start + chunk] = ky


def field_and_kick(where, partners, offsets, counts, grids, kernel_hat, tables, places):
    n = places[0].shape[-1]
    sm = pl.BlockSpec(memory_space=pltpu.SMEM)
    vm = pl.BlockSpec(memory_space=pltpu.VMEM)
    anyspace = pl.BlockSpec(memory_space=pl.ANY)
    hbm = pl.BlockSpec(memory_space=pltpu.HBM)
    return pl.pallas_call(
        field_body,
        out_shape=[jax.ShapeDtypeStruct((2, 2, n), F32)] * 2,
        in_specs=[sm] * 4 + [anyspace] * 5 + [hbm] * 5 + [vm] * 4,
        out_specs=[vm, vm],
        scratch_shapes=[
            pltpu.VMEM((5, 2, GRID, GRID), F32),
            pltpu.VMEM((2, SPAN + 8, GRID), F32),
            pltpu.VMEM(tables[0].shape, BF),
            pltpu.VMEM(tables[1].shape, BF),
            pltpu.VMEM((2, 2, PAD, PAD), F32),
            pltpu.VMEM(tables[2].shape, BF),
            pltpu.VMEM(tables[3].shape, BF),
            pltpu.SemaphoreType.DMA((5,)),
            pltpu.SemaphoreType.DMA((5,)),
        ],
        compiler_params=pltpu.CompilerParams(vmem_limit_bytes=24 * 1024 * 1024),
        name="field_and_kick",
    )(where, partners, offsets, counts, *grids, kernel_hat, *tables, *places)


def finish_body(where_ref, near_ref, far_ref, nearc_ref, farc_ref, momenta_ref, out_ref):
    h = where_ref[1]
    c = where_ref[2]
    for coord in range(2):
        near = near_ref[0, coord : coord + 1, :]
        nearc = nearc_ref[1, coord : coord + 1, :]
        far = far_ref[0, coord : coord + 1, :]
        farc = farc_ref[1, coord : coord + 1, :]
        for beam in range(2):
            mine = jnp.where(h == beam, near, far)
            other = jnp.where(h == beam, nearc, farc)
            both = jnp.concatenate(
                [jnp.where(c == 0, mine, other), jnp.where(c == 0, other, mine)], 0
            )
            out_ref[coord, beam] = momenta_ref[coord, beam] + both


def finish(where, near, far, nearc, farc, momenta):
    vm = pl.BlockSpec(memory_space=pltpu.VMEM)
    return pl.pallas_call(
        finish_body,
        out_shape=jax.ShapeDtypeStruct(momenta.shape, F32),
        in_specs=[pl.BlockSpec(memory_space=pltpu.SMEM)] + [vm] * 5,
        out_specs=vm,
        compiler_params=pltpu.CompilerParams(vmem_limit_bytes=4 * 1024 * 1024),
        name="finish",
    )(where, near, far, nearc, farc, momenta)


def per_device(positions, momenta, kernel_hat, partners, offsets, counts):
    blocks = lax.axis_size("bunch")
    doms = lax.axis_size("dom")
    b = lax.axis_index("bunch")
    d = lax.axis_index("dom")
    where = jnp.stack([b, d // 2, d % 2, jnp.int32(blocks)]).astype(jnp.int32)

    def across_cores(x):
        return lax.ppermute(x, "dom", [(i, i ^ 1) for i in range(doms)])

    def across_chips(x):
        return lax.ppermute(x, "dom", [(i, i ^ 2) for i in range(doms)])

    def along_blocks(x, by):
        pairs = []
        for i in range(blocks):
            for j in range(doms):
                to = (i + (by if j % 2 == 0 else -by)) % blocks
                pairs.append((i * doms + j, to * doms + j))
        return lax.ppermute(x, ("bunch", "dom"), pairs)

    pos_y = across_chips(positions)
    pos_c = across_cores(positions)
    first = deposit(where, positions, pos_c)
    pos_yc = across_cores(pos_y)
    own = deposit(where, pos_y, pos_yc, first)
    r1 = along_blocks(own, 1)
    r2 = along_blocks(own, 2)
    s1 = across_cores(r1)
    s2 = across_cores(r2)
    tables = [jnp.asarray(t) for t in dft_tables()]
    near, far = field_and_kick(
        where, partners, offsets, counts, (own, r1, r2, s1, s2), kernel_hat, tables,
        (positions, pos_c, pos_y, pos_yc),
    )
    far = across_chips(far)
    nearc = across_cores(near)
    farc = across_cores(far)
    return finish(where, near, far, nearc, farc, momenta)


def solution(mesh):
    in_specs = (
        P(None, None, "bunch", "dom"),
        P(None, None, "bunch", "dom"),
        P(),
        P(None, "bunch", None),
        P(None, None, "bunch", None),
        P(None, "bunch"),
    )
    out_specs = P(None, None, "bunch", "dom")
    return jax.shard_map(
        per_device, mesh=mesh, in_specs=in_specs, out_specs=out_specs, check_vma=False
    )
```

time: 97.1 us -> 46.8 us (0.48)
  matrix products: 28.2 us -> 0 us
  waiting for transfers between devices: 26.1 us -> 3.96 us
  blocking collectives: 12.3 us -> 0 us
  Pallas kernels: 0 us -> 11.8 us
  starting transfers between devices: 21.2 us -> 25.3 us
  other arithmetic: 2.85 us -> 0.08 us
    dot_general x32 -> x0, matrix products: 28.2 us -> none  [the longest x30 24.5 us: product(): jnp.dot(left, right, precision=HIGH, preferred_element_type=jnp.float32)]
    all_to_all x2 -> x0, waiting for transfers between devices: 23.3 us -> none  [copy_for_each(): return lax.all_to_all(copies, axis, split_axis=0, concat_axis=0, tiled=True)]
    ppermute x4 -> x10, starting transfers between devices: 10.3 us -> 25.3 us  [the longest x6 11 us: across_cores(): return lax.ppermute(x, 'dom', [(i, i ^ 1) for i in range(doms)])]
    all_to_all x1 -> x0, blocking collectives: 12.3 us -> none  [summed_on_arrival(): lax.all_to_all(tiles, axis, split_axis=0, concat_axis=0, tiled=True)]
    pallas_call x0 -> x4, Pallas kernels: none -> 11.8 us  [the longest x1 7.34 us: field_and_kick(): pl.pallas_call(field_body, out_shape=[jax.ShapeDtypeStruct((2, 2, n), F32...]
    all_to_all x2 -> x0, starting transfers between devices: 10.8 us -> none  [copy_for_each(): return lax.all_to_all(copies, axis, split_axis=0, concat_axis=0, tiled=True)]
    unnamed x12 -> x22, local copies, waits for them, and re-layouts: 0.85 us -> 5.23 us
    broadcast_in_dim x2 -> x0, local copies, waits for them, and re-layouts: 2.06 us -> none  [copy_for_each(): copies = jnp.broadcast_to(x, (lax.axis_size(axis), *x.shape))]
  transfers between devices with their start and end apart: 6 -> 10, of which waited for: 4 -> 5; matrix products, arithmetic and copies ran while one was open for 4% -> 0% of each run, Pallas kernels for 0% -> 4%
where the time goes in v1:
time: 46.8 us; the launch traced here: 46.5 us
  starting transfers between devices  25.3 us (54%)
  Pallas kernels  11.8 us (25%)
  local copies, waits for them, and re-layouts  5.23 us (11%)
  waiting for transfers between devices  3.96 us (8%)
    ppermute x6, starting transfers between devices, across_cores(): return lax.ppermute(x, 'dom', [(i, i ^ 1) for i in range(doms)])  11 us
    ppermute x2, starting transfers between devices, along_blocks(): return lax.ppermute(x, ('bunch', 'dom'), pairs)  8.25 us
    pallas_call x1, Pallas kernels, field_and_kick(): pl.pallas_call(field_body, out_shape=[jax.ShapeDtypeStruct((2, 2, n), F32...  7.34 us
    ppermute x2, starting transfers between devices, across_chips(): return lax.ppermute(x, 'dom', [(i, i ^ 2) for i in range(doms)])  6.05 us
    unnamed x22, local copies, waits for them, and re-layouts  5.23 us
    pallas_call x2, Pallas kernels, deposit(): pl.pallas_call(deposit_body, out_shape=jax.ShapeDtypeStruct((2, GRID, GRI...  3.29 us
    ppermute x6, waiting for transfers between devices, across_cores(): return lax.ppermute(x, 'dom', [(i, i ^ 1) for i in range(doms)])  1.83 us
    ppermute x2, waiting for transfers between devices, along_blocks(): return lax.ppermute(x, ('bunch', 'dom'), pairs)  1.57 us
  transfers between devices with their start and end apart: 10, of which 5 were waited for; matrix products, arithmetic and copies ran while one was open for 0% of the time, Pallas kernels for 4%

profile of v1, /device:TPU:1, one launch (start us, length us, event | category | flops | bytes accessed | tf_op | source)
XLA Modules:
  0.0 46.5 jit_solution(17334716029751569770)
XLA Ops:
  0.0 0.0 copy-start.3
  0.0 3.7 %collective-permute-start = (f32[2,2,2,1024]{3,2,1,0:T(2,128)}, f32[2,2,2,1024]{3,2,1,0:T(2,128)S(1)}, u32[]{:S(2)}, u32[]{:S(2)}) collective-permute-start(f32[2,2,2,1024]{3,2,1,0:T(2,128)} %pa_ref.1), channel_id=1, source_target_pairs={{0,2},{1,3},{2,0},{3,1},{4,6},{5,7},{6,4},{7,5},{8,10},{9,11},{10,... | collective-permute-start | bytes 98312 | tf_op jit(solution)/shard_map/ppermute | solution.py:254
  3.7 1.0 %collective-permute-start.2 = (f32[2,2,2,1024]{3,2,1,0:T(2,128)}, f32[2,2,2,1024]{3,2,1,0:T(2,128)S(1)}, u32[]{:S(2)}, u32[]{:S(2)}) collective-permute-start(f32[2,2,2,1024]{3,2,1,0:T(2,128)} %pa_ref.1), channel_id=1, source_target_pairs={{0,1},{1,0},{2,3},{3,2},{4,5},{5,4},{6,7},{7,6},{8,9},{9,8},{10,11... | collective-permute-start | bytes 98312 | tf_op jit(solution)/shard_map/ppermute | solution.py:251
  4.7 0.6 %collective-permute-done.a_ref.py_ref = f32[2,2,2,1024]{3,2,1,0:T(2,128)S(1)} collective-permute-done((f32[2,2,2,1024]{3,2,1,0:T(2,128)}, f32[2,2,2,1024]{3,2,1,0:T(2,128)S(1)}, u32[]{:S(2)}, u32[]{:S(2)}) %collective-permute-start) | collective-permute-done | bytes 32800 | tf_op jit(solution)/shard_map/ppermute | solution.py:254
  5.3 3.6 %collective-permute-start.1 = (f32[2,2,2,1024]{3,2,1,0:T(2,128)S(1)}, f32[2,2,2,1024]{3,2,1,0:T(2,128)S(1)}, u32[]{:S(2)}, u32[]{:S(2)}) collective-permute-start(f32[2,2,2,1024]{3,2,1,0:T(2,128)S(1)} %collective-permute-done.a_ref.py_ref), channel_id=1, source_target_pairs={{0,1},{1,0},{2,3},{3,2},{4,5},{5,4},{6,7},{7,6},{8,9},{9,8},{10,11... | collective-permute-start | bytes 98312 | tf_op jit(solution)/shard_map/ppermute | solution.py:251
  8.9 0.1 pad_add_fusion.where_ref
  9.0 0.0 collective-permute-done.2.b_ref.pc_ref
  9.0 0.0 copy-start.5
  9.0 0.8 %copy-done.5 = f32[2,2,2,1024]{3,2,1,0:T(2,128)S(1)} copy-done((f32[2,2,2,1024]{3,2,1,0:T(2,128)S(1)}, f32[2,2,2,1024]{3,2,1,0:T(2,128)}, u32[]{:S(2)}) %copy-start.5) | copy-done | bytes 32792
  9.7 1.6 %deposit_first.1.rest_0_ = f32[2,128,128]{2,1,0:T(8,128)S(1)} custom-call(s32[4]{0:T(128)S(1)} %pad_add_fusion.where_ref, f32[2,2,2,1024]{3,2,1,0:T(2,128)S(1)} %copy-done.5, f32[2,2,2,1024]{3,2,1,0:T(2,128)S(1)} %collective-permute-done.2.b_ref.pc_ref), custom_call_target="tpu_custom_call" | custom-call | tf_op jit(solution)/shard_map/deposit_first/pallas_call | solution.py:86
  11.4 0.0 copy-start.6
  11.4 0.0 copy-start.8
  11.4 0.0 copy-start.9
  11.4 0.0 copy-start.10
  11.4 0.0 collective-permute-done.1.b_ref.pyc_ref
  11.4 0.0 copy-start.7
  11.4 1.6 %deposit_second.1.own_ref = f32[2,128,128]{2,1,0:T(8,128)S(1)} custom-call(s32[4]{0:T(128)S(1)} %pad_add_fusion.where_ref, f32[2,2,2,1024]{3,2,1,0:T(2,128)S(1)} %collective-permute-done.a_ref.py_ref, f32[2,2,2,1024]{3,2,1,0:T(2,128)S(1)} %collective-permute-done.1.b_ref.pyc_ref, f32[2,128,128]{2,1,0:T(8,128)S(1)} %deposit_first.1.rest_0_), custom_call_target="tpu_custom_call" | custom-call | tf_op jit(solution)/shard_map/deposit_second/pallas_call | solution.py:86
  13.1 7.4 %collective-permute-start.4 = (f32[2,128,128]{2,1,0:T(8,128)S(1)}, f32[2,128,128]{2,1,0:T(8,128)S(1)}, u32[]{:S(2)}, u32[]{:S(2)}) collective-permute-start(f32[2,128,128]{2,1,0:T(8,128)S(1)} %deposit_second.1.own_ref), channel_id=1, source_target_pairs={{0,8},{1,249},{2,10},{3,251},{4,12},{5,253},{6,14},{7,255},{8,16},... | collective-permute-start | bytes 393224 | tf_op jit(solution)/shard_map/ppermute | solution.py:262
  20.5 0.9 %collective-permute-start.3 = (f32[2,128,128]{2,1,0:T(8,128)S(1)}, f32[2,128,128]{2,1,0:T(8,128)S(1)}, u32[]{:S(2)}, u32[]{:S(2)}) collective-permute-start(f32[2,128,128]{2,1,0:T(8,128)S(1)} %deposit_second.1.own_ref), channel_id=1, source_target_pairs={{0,4},{1,253},{2,6},{3,255},{4,8},{5,1},{6,10},{7,3},{8,12},{9,5},... | collective-permute-start | bytes 393224 | tf_op jit(solution)/shard_map/ppermute | solution.py:262
  21.3 1.1 %collective-permute-done.4.r2_ref = f32[2,128,128]{2,1,0:T(8,128)S(1)} collective-permute-done((f32[2,128,128]{2,1,0:T(8,128)S(1)}, f32[2,128,128]{2,1,0:T(8,128)S(1)}, u32[]{:S(2)}, u32[]{:S(2)}) %collective-permute-start.4) | collective-permute-done | bytes 131104 | tf_op jit(solution)/shard_map/ppermute | solution.py:262
  22.4 1.5 %collective-permute-start.6 = (f32[2,128,128]{2,1,0:T(8,128)S(1)}, f32[2,128,128]{2,1,0:T(8,128)S(1)}, u32[]{:S(2)}, u32[]{:S(2)}) collective-permute-start(f32[2,128,128]{2,1,0:T(8,128)S(1)} %collective-permute-done.4.r2_ref), channel_id=1, source_target_pairs={{0,1},{1,0},{2,3},{3,2},{4,5},{5,4},{6,7},{7,6},{8,9},{9,8},{10,11... | collective-permute-start | bytes 393224 | tf_op jit(solution)/shard_map/ppermute | solution.py:251
  24.0 0.5 %collective-permute-done.3.r1_ref = f32[2,128,128]{2,1,0:T(8,128)S(1)} collective-permute-done((f32[2,128,128]{2,1,0:T(8,128)S(1)}, f32[2,128,128]{2,1,0:T(8,128)S(1)}, u32[]{:S(2)}, u32[]{:S(2)}) %collective-permute-start.3) | collective-permute-done | bytes 131104 | tf_op jit(solution)/shard_map/ppermute | solution.py:262
  24.5 0.7 %collective-permute-start.5 = (f32[2,128,128]{2,1,0:T(8,128)S(1)}, f32[2,128,128]{2,1,0:T(8,128)S(1)}, u32[]{:S(2)}, u32[]{:S(2)}) collective-permute-start(f32[2,128,128]{2,1,0:T(8,128)S(1)} %collective-permute-done.3.r1_ref), channel_id=1, source_target_pairs={{0,1},{1,0},{2,3},{3,2},{4,5},{5,4},{6,7},{7,6},{8,9},{9,8},{10,11... | collective-permute-start | bytes 393224 | tf_op jit(solution)/shard_map/ppermute | solution.py:251
  25.1 0.0 collective-permute-done.6.s2_ref
  25.1 1.0 %collective-permute-done.5.s1_ref = f32[2,128,128]{2,1,0:T(8,128)S(1)} collective-permute-done((f32[2,128,128]{2,1,0:T(8,128)S(1)}, f32[2,128,128]{2,1,0:T(8,128)S(1)}, u32[]{:S(2)}, u32[]{:S(2)}) %collective-permute-start.5) | collective-permute-done | bytes 131104 | tf_op jit(solution)/shard_map/ppermute | solution.py:251
  26.1 0.0 copy-done.3
  26.1 0.0 copy-done.6
  26.1 0.0 copy-done.8
  26.1 0.0 copy-done.9
  26.1 0.0 copy-done.10
  26.1 0.0 copy-start
  26.1 1.2 %copy-done = f32[2,2,256,256]{3,2,1,0:T(8,128)S(1)} copy-done((f32[2,2,256,256]{3,2,1,0:T(8,128)S(1)}, f32[2,2,256,256]{3,2,1,0:T(8,128)}, u32[]{:S(2)}) %copy-start) | copy-done | bytes 1048600
  27.4 0.0 copy-start.1
  27.4 1.1 %copy-done.1 = bf16[768,512]{1,0:T(8,128)(2,1)S(1)} copy-done((bf16[768,512]{1,0:T(8,128)(2,1)S(1)}, bf16[768,512]{1,0:T(8,128)(2,1)}, u32[]{:S(2)}) %copy-start.1) | copy-done | bytes 786456
  28.5 0.0 copy-start.2
  28.5 1.1 %copy-done.2 = bf16[512,576]{1,0:T(8,128)(2,1)S(1)} copy-done((bf16[512,576]{1,0:T(8,128)(2,1)S(1)}, bf16[512,576]{1,0:T(8,128)(2,1)}, u32[]{:S(2)}) %copy-start.2) | copy-done | bytes 589848
  29.6 0.0 copy-start.4
  29.6 1.0 %copy-done.4 = bf16[768,256]{1,0:T(8,128)(2,1)S(1)} copy-done((bf16[768,256]{1,0:T(8,128)(2,1)S(1)}, bf16[768,256]{1,0:T(8,128)(2,1)}, u32[]{:S(2)}) %copy-start.4) | copy-done | bytes 393240
  30.6 7.3 %field_and_kick.1 = (f32[2,2,1024]{2,1,0:T(2,128)S(1)}, f32[2,2,1024]{2,1,0:T(2,128)S(1)}) custom-call(s32[4]{0:T(128)S(1)} %pad_add_fusion.where_ref, s32[2,2,16]{2,1,0:T(2,128)S(1)} %copy-done.9, s32[2,2,2,16]{3,2,1,0:T(2,128)S(1)} %copy-done.8, s32[2,2]{1,0:T(2,128)S(1)} %copy-done.10, f32[2,128,128]{2,1,0:T(8,128)S(1)} %deposit_second.1.own_ref, ...), custom_call_target="tpu_custom_call" | custom-call | tf_op jit(solution)/shard_map/field_and_kick/pallas_call | solution.py:193
  37.9 2.3 %collective-permute-start.7 = (f32[2,2,1024]{2,1,0:T(2,128)S(1)}, f32[2,2,1024]{2,1,0:T(2,128)S(1)}, u32[]{:S(2)}, u32[]{:S(2)}) collective-permute-start(f32[2,2,1024]{2,1,0:T(2,128)S(1)} %get-tuple-element.8), channel_id=1, source_target_pairs={{0,2},{1,3},{2,0},{3,1},{4,6},{5,7},{6,4},{7,5},{8,10},{9,11},{10,... | collective-permute-start | bytes 49160 | tf_op jit(solution)/shard_map/ppermute | solution.py:254
  40.2 2.0 %collective-permute-start.8 = (f32[2,2,1024]{2,1,0:T(2,128)S(1)}, f32[2,2,1024]{2,1,0:T(2,128)S(1)}, u32[]{:S(2)}, u32[]{:S(2)}) collective-permute-start(f32[2,2,1024]{2,1,0:T(2,128)S(1)} %get-tuple-element.7.near_ref), channel_id=1, source_target_pairs={{0,1},{1,0},{2,3},{3,2},{4,5},{5,4},{6,7},{7,6},{8,9},{9,8},{10,11... | collective-permute-start | bytes 49160 | tf_op jit(solution)/shard_map/ppermute | solution.py:251
  42.2 0.0 collective-permute-done.7.far_ref
  42.2 2.2 %collective-permute-start.9 = (f32[2,2,1024]{2,1,0:T(2,128)S(1)}, f32[2,2,1024]{2,1,0:T(2,128)S(1)}, u32[]{:S(2)}, u32[]{:S(2)}) collective-permute-start(f32[2,2,1024]{2,1,0:T(2,128)S(1)} %collective-permute-done.7.far_ref), channel_id=1, source_target_pairs={{0,1},{1,0},{2,3},{3,2},{4,5},{5,4},{6,7},{7,6},{8,9},{9,8},{10,11... | collective-permute-start | bytes 49160 | tf_op jit(solution)/shard_map/ppermute | solution.py:251
  44.4 0.0 collective-permute-done.8.nearc_ref
  44.4 0.8 %collective-permute-done.9.farc_ref = f32[2,2,1024]{2,1,0:T(2,128)S(1)} collective-permute-done((f32[2,2,1024]{2,1,0:T(2,128)S(1)}, f32[2,2,1024]{2,1,0:T(2,128)S(1)}, u32[]{:S(2)}, u32[]{:S(2)}) %collective-permute-start.9) | collective-permute-done | bytes 16416 | tf_op jit(solution)/shard_map/ppermute | solution.py:251
  45.3 0.0 copy-done.7
  45.3 1.2 %finish.1 = f32[2,2,2,1024]{3,2,1,0:T(2,128)} custom-call(s32[4]{0:T(128)S(1)} %pad_add_fusion.where_ref, f32[2,2,1024]{2,1,0:T(2,128)S(1)} %get-tuple-element.7.near_ref, f32[2,2,1024]{2,1,0:T(2,128)S(1)} %collective-permute-done.7.far_ref, f32[2,2,1024]{2,1,0:T(2,128)S(1)} %collective-permute-done.8.nearc_ref, ...), custom_call_target="tpu_custom_call" | custom-call | tf_op jit(solution)/shard_map/finish/pallas_call | solution.py:233
Async XLA Ops:
  0.0 26.1 %copy-start.3 = (bf16[128,1536]{1,0:T(8,128)(2,1)S(1)}, bf16[128,1536]{1,0:T(8,128)(2,1)}, u32[]{:S(2)}) copy-start(bf16[128,1536]{1,0:T(8,128)(2,1)} %constant.46.clone.brows_hbm) | copy-start | bytes 1179652
  0.0 5.3 %collective-permute-start = (f32[2,2,2,1024]{3,2,1,0:T(2,128)}, f32[2,2,2,1024]{3,2,1,0:T(2,128)S(1)}, u32[]{:S(2)}, u32[]{:S(2)}) collective-permute-start(f32[2,2,2,1024]{3,2,1,0:T(2,128)} %pa_ref.1), channel_id=1, source_target_pairs={{0,2},{1,3},{2,0},{3,1},{4,6},{5,7},{6,4},{7,5},{8,10},{9,11},{10,... | collective-permute-start | bytes 98312 | tf_op jit(solution)/shard_map/ppermute | solution.py:254
  3.7 5.2 %collective-permute-start.2 = (f32[2,2,2,1024]{3,2,1,0:T(2,128)}, f32[2,2,2,1024]{3,2,1,0:T(2,128)S(1)}, u32[]{:S(2)}, u32[]{:S(2)}) collective-permute-start(f32[2,2,2,1024]{3,2,1,0:T(2,128)} %pa_ref.1), channel_id=1, source_target_pairs={{0,1},{1,0},{2,3},{3,2},{4,5},{5,4},{6,7},{7,6},{8,9},{9,8},{10,11... | collective-permute-start | bytes 98312 | tf_op jit(solution)/shard_map/ppermute | solution.py:251
  5.3 6.2 %collective-permute-start.1 = (f32[2,2,2,1024]{3,2,1,0:T(2,128)S(1)}, f32[2,2,2,1024]{3,2,1,0:T(2,128)S(1)}, u32[]{:S(2)}, u32[]{:S(2)}) collective-permute-start(f32[2,2,2,1024]{3,2,1,0:T(2,128)S(1)} %collective-permute-done.a_ref.py_ref), channel_id=1, source_target_pairs={{0,1},{1,0},{2,3},{3,2},{4,5},{5,4},{6,7},{7,6},{8,9},{9,8},{10,11... | collective-permute-start | bytes 98312 | tf_op jit(solution)/shard_map/ppermute | solution.py:251
  9.0 0.8 %copy-start.5 = (f32[2,2,2,1024]{3,2,1,0:T(2,128)S(1)}, f32[2,2,2,1024]{3,2,1,0:T(2,128)}, u32[]{:S(2)}) copy-start(f32[2,2,2,1024]{3,2,1,0:T(2,128)} %pa_ref.1) | copy-start | bytes 98308
  11.4 14.7 %copy-start.6 = (f32[2,2,2,1024]{3,2,1,0:T(2,128)S(1)}, f32[2,2,2,1024]{3,2,1,0:T(2,128)}, u32[]{:S(2)}) copy-start(f32[2,2,2,1024]{3,2,1,0:T(2,128)} %pa_ref.1) | copy-start | bytes 98308
  11.4 14.7 %copy-start.8 = (s32[2,2,2,16]{3,2,1,0:T(2,128)S(1)}, s32[2,2,2,16]{3,2,1,0:T(2,128)}, u32[]{:S(2)}) copy-start(s32[2,2,2,16]{3,2,1,0:T(2,128)} %offsets_ref.1) | copy-start | bytes 1540
  11.4 14.7 %copy-start.9 = (s32[2,2,16]{2,1,0:T(2,128)S(1)}, s32[2,2,16]{2,1,0:T(2,128)}, u32[]{:S(2)}) copy-start(s32[2,2,16]{2,1,0:T(2,128)} %partners_ref.1) | copy-start | bytes 772
  11.4 14.7 %copy-start.10 = (s32[2,2]{1,0:T(2,128)S(1)}, s32[2,2]{1,0:T(2,128)}, u32[]{:S(2)}) copy-start(s32[2,2]{1,0:T(2,128)} %counts_ref.1) | copy-start | bytes 52
  11.4 33.9 %copy-start.7 = (f32[2,2,2,1024]{3,2,1,0:T(2,128)S(1)}, f32[2,2,2,1024]{3,2,1,0:T(2,128)}, u32[]{:S(2)}) copy-start(f32[2,2,2,1024]{3,2,1,0:T(2,128)} %momenta_ref.1) | copy-start | bytes 98308
  13.1 9.3 %collective-permute-start.4 = (f32[2,128,128]{2,1,0:T(8,128)S(1)}, f32[2,128,128]{2,1,0:T(8,128)S(1)}, u32[]{:S(2)}, u32[]{:S(2)}) collective-permute-start(f32[2,128,128]{2,1,0:T(8,128)S(1)} %deposit_second.1.own_ref), channel_id=1, source_target_pairs={{0,8},{1,249},{2,10},{3,251},{4,12},{5,253},{6,14},{7,255},{8,16},... | collective-permute-start | bytes 393224 | tf_op jit(solution)/shard_map/ppermute | solution.py:262
  20.5 4.0 %collective-permute-start.3 = (f32[2,128,128]{2,1,0:T(8,128)S(1)}, f32[2,128,128]{2,1,0:T(8,128)S(1)}, u32[]{:S(2)}, u32[]{:S(2)}) collective-permute-start(f32[2,128,128]{2,1,0:T(8,128)S(1)} %deposit_second.1.own_ref), channel_id=1, source_target_pairs={{0,4},{1,253},{2,6},{3,255},{4,8},{5,1},{6,10},{7,3},{8,12},{9,5},... | collective-permute-start | bytes 393224 | tf_op jit(solution)/shard_map/ppermute | solution.py:262
  22.4 2.7 %collective-permute-start.6 = (f32[2,128,128]{2,1,0:T(8,128)S(1)}, f32[2,128,128]{2,1,0:T(8,128)S(1)}, u32[]{:S(2)}, u32[]{:S(2)}) collective-permute-start(f32[2,128,128]{2,1,0:T(8,128)S(1)} %collective-permute-done.4.r2_ref), channel_id=1, source_target_pairs={{0,1},{1,0},{2,3},{3,2},{4,5},{5,4},{6,7},{7,6},{8,9},{9,8},{10,11... | collective-permute-start | bytes 393224 | tf_op jit(solution)/shard_map/ppermute | solution.py:251
  24.5 1.6 %collective-permute-start.5 = (f32[2,128,128]{2,1,0:T(8,128)S(1)}, f32[2,128,128]{2,1,0:T(8,128)S(1)}, u32[]{:S(2)}, u32[]{:S(2)}) collective-permute-start(f32[2,128,128]{2,1,0:T(8,128)S(1)} %collective-permute-done.3.r1_ref), channel_id=1, source_target_pairs={{0,1},{1,0},{2,3},{3,2},{4,5},{5,4},{6,7},{7,6},{8,9},{9,8},{10,11... | collective-permute-start | bytes 393224 | tf_op jit(solution)/shard_map/ppermute | solution.py:251
  26.1 1.2 %copy-start = (f32[2,2,256,256]{3,2,1,0:T(8,128)S(1)}, f32[2,2,256,256]{3,2,1,0:T(8,128)}, u32[]{:S(2)}) copy-start(f32[2,2,256,256]{3,2,1,0:T(8,128)} %kernel_hbm.1) | copy-start | bytes 3145732
  27.4 1.1 %copy-start.1 = (bf16[768,512]{1,0:T(8,128)(2,1)S(1)}, bf16[768,512]{1,0:T(8,128)(2,1)}, u32[]{:S(2)}) copy-start(bf16[768,512]{1,0:T(8,128)(2,1)} %constant.44.clone.cols_hbm) | copy-start | bytes 2359300
  28.5 1.1 %copy-start.2 = (bf16[512,576]{1,0:T(8,128)(2,1)S(1)}, bf16[512,576]{1,0:T(8,128)(2,1)}, u32[]{:S(2)}) copy-start(bf16[512,576]{1,0:T(8,128)(2,1)} %constant.43.clone.rows_hbm) | copy-start | bytes 1769476
  29.6 1.0 %copy-start.4 = (bf16[768,256]{1,0:T(8,128)(2,1)S(1)}, bf16[768,256]{1,0:T(8,128)(2,1)}, u32[]{:S(2)}) copy-start(bf16[768,256]{1,0:T(8,128)(2,1)} %constant.45.clone.bcols_hbm) | copy-start | bytes 1179652
  37.9 4.3 %collective-permute-start.7 = (f32[2,2,1024]{2,1,0:T(2,128)S(1)}, f32[2,2,1024]{2,1,0:T(2,128)S(1)}, u32[]{:S(2)}, u32[]{:S(2)}) collective-permute-start(f32[2,2,1024]{2,1,0:T(2,128)S(1)} %get-tuple-element.8), channel_id=1, source_target_pairs={{0,2},{1,3},{2,0},{3,1},{4,6},{5,7},{6,4},{7,5},{8,10},{9,11},{10,... | collective-permute-start | bytes 49160 | tf_op jit(solution)/shard_map/ppermute | solution.py:254
  40.2 4.2 %collective-permute-start.8 = (f32[2,2,1024]{2,1,0:T(2,128)S(1)}, f32[2,2,1024]{2,1,0:T(2,128)S(1)}, u32[]{:S(2)}, u32[]{:S(2)}) collective-permute-start(f32[2,2,1024]{2,1,0:T(2,128)S(1)} %get-tuple-element.7.near_ref), channel_id=1, source_target_pairs={{0,1},{1,0},{2,3},{3,2},{4,5},{5,4},{6,7},{7,6},{8,9},{9,8},{10,11... | collective-permute-start | bytes 49160 | tf_op jit(solution)/shard_map/ppermute | solution.py:251
  42.2 3.1 %collective-permute-start.9 = (f32[2,2,1024]{2,1,0:T(2,128)S(1)}, f32[2,2,1024]{2,1,0:T(2,128)S(1)}, u32[]{:S(2)}, u32[]{:S(2)}) collective-permute-start(f32[2,2,1024]{2,1,0:T(2,128)S(1)} %collective-permute-done.7.far_ref), channel_id=1, source_target_pairs={{0,1},{1,0},{2,3},{3,2},{4,5},{5,4},{6,7},{7,6},{8,9},{9,8},{10,11... | collective-permute-start | bytes 49160 | tf_op jit(solution)/shard_map/ppermute | solution.py:251

commit v2 on v1

v2 whole, which is shorter than its diff:
```python
import functools

import jax
import jax.numpy as jnp
import numpy as np
from jax import lax
from jax.experimental import pallas as pl
from jax.experimental.pallas import tpu as pltpu
from jax.sharding import PartitionSpec as P

GRID = 128
PAD = 256
OFFSET = 32
SPAN = GRID + 2 * OFFSET
HALF = 136
HOPS = 2
BF = jnp.bfloat16
F32 = jnp.float32
VM = pl.BlockSpec(memory_space=pltpu.VMEM)
SM = pl.BlockSpec(memory_space=pltpu.SMEM)
HBM = pl.BlockSpec(memory_space=pltpu.HBM)


def in_hbm(x):
    return pltpu.with_memory_space_constraint(x, pltpu.HBM)


def split_const(m):
    hi = m.astype(BF)
    lo = (m - hi.astype(np.float64)).astype(BF)
    return np.asarray(hi), np.asarray(lo)


def dft_tables():
    k = np.arange(PAD)
    w = 2.0 * np.pi / PAD
    half = np.arange(HALF)
    used = (half <= GRID)[:, None]
    r = np.arange(SPAN) - OFFSET
    ang = w * ((half[:, None] * r[None, :]) % PAD)
    hi, lo = split_const(np.concatenate([np.cos(ang) * used, -np.sin(ang) * used], 0))
    rows = np.concatenate([hi, hi, lo], 1)
    r = np.arange(PAD) - OFFSET
    ang = w * ((r[:, None] * k[None, :]) % PAD)
    hi, lo = split_const(np.concatenate([np.cos(ang), np.sin(ang)], 1))
    cols = np.concatenate([hi, hi, lo], 0)
    j = np.arange(GRID)
    ang = w * ((k[:, None] * j[None, :]) % PAD)
    hi, lo = split_const(np.concatenate([np.cos(ang), np.sin(ang)], 1))
    back_cols = np.concatenate([hi, hi, lo], 0)
    ang = w * ((j[:, None] * np.arange(GRID)[None, :]) % PAD)
    re = 2.0 * np.cos(ang)
    re[:, 0] = 1.0
    im = -2.0 * np.sin(ang)
    im[:, 0] = np.cos(np.pi * j)
    hi, lo = split_const(np.concatenate([re, im], 1) / (PAD * PAD))
    back_rows = np.concatenate([hi, hi, lo], 1)
    return rows, cols, back_cols, back_rows


def hilo(v):
    hi = v.astype(BF)
    lo = (v - hi.astype(F32)).astype(BF)
    return hi, lo


def dot(a, b):
    return jnp.dot(a, b, preferred_element_type=F32)


def hat(coord, lanes):
    cells = lax.broadcasted_iota(jnp.int32, (GRID, lanes), 0).astype(F32)
    return jnp.maximum(0.0, 1.0 - jnp.abs(coord - cells))


def chip_half():
    return lax.div(lax.axis_index("dom"), 2)


def core():
    return lax.rem(lax.axis_index("dom"), 2)


def params(mib):
    return pltpu.CompilerParams(vmem_limit_bytes=mib * 1024 * 1024)


def deposit_body(sources, *refs):
    *given, out_ref, tx, ty = refs
    prev_ref = given[sources] if len(given) > sources else None
    e = 1 - chip_half()
    n = given[0].shape[-1]
    for m in range(2):
        for i, ref in enumerate(given[:sources]):
            for coord, table in ((0, tx), (1, ty)):
                hi, lo = hilo(hat(ref[coord, e, pl.ds(m, 1), :], n))
                table[m, 0:GRID, i * n : (i + 1) * n] = hi
                table[m, GRID:, i * n : (i + 1) * n] = lo
        acc = lax.dot_general(
            tx[m], ty[m], (((1,), (1,)), ((), ())), preferred_element_type=F32
        )
        total = (acc[:GRID, :GRID] + acc[GRID:, GRID:]) + (acc[:GRID, GRID:] + acc[GRID:, :GRID])
        if prev_ref is not None:
            total = total + prev_ref[m]
        out_ref[m] = total


def deposit(sources, prev=None):
    n = sources[0].shape[-1]
    args = [*sources] + ([] if prev is None else [prev])
    return pl.pallas_call(
        functools.partial(deposit_body, len(sources)),
        out_shape=jax.ShapeDtypeStruct((2, GRID, GRID), F32),
        in_specs=[VM] * len(args),
        out_specs=VM,
        scratch_shapes=[pltpu.VMEM((2, 2 * GRID, len(sources) * n), BF)] * 2,
        compiler_params=params(16),
        name="deposit",
    )(*args)


def prepare_body(
    pc_ref, py_ref, pyc_ref, pa_hbm, kernel_hbm, half_ref, wx_ref, wy_ref, pa_ref, kernel_ref, sems
):
    own_copy = pltpu.make_async_copy(pa_hbm, pa_ref, sems.at[0])
    kernel_copy = pltpu.make_async_copy(kernel_hbm, kernel_ref, sems.at[1])
    own_copy.start()
    kernel_copy.start()
    h = chip_half()
    c = core()
    n = pa_ref.shape[-1]
    chunk = 512
    for i, ref in ((1, pc_ref), (2, py_ref), (3, pyc_ref), (0, pa_ref)):
        if i == 0:
            own_copy.wait()
        for start in range(0, n, chunk):
            at = slice(i * n + start, i * n + start + chunk)
            both = ref[0, h, :, start : start + chunk]
            wx_ref[:, at] = hat(jnp.where(c == 0, both[0:1], both[1:2]), chunk)
            both = ref[1, h, :, start : start + chunk]
            hi, lo = hilo(hat(jnp.where(c == 0, both[0:1], both[1:2]), chunk))
            wy_ref[0:GRID, at] = hi
            wy_ref[GRID : 2 * GRID, at] = hi
            wy_ref[2 * GRID :, at] = lo
    row = lax.broadcasted_iota(jnp.int32, (PAD, PAD), 0)
    col = lax.broadcasted_iota(jnp.int32, (PAD, PAD), 1)
    flip = jnp.where(((row + col) & (PAD - 1)) == 0, 1.0, 0.0).astype(BF)
    kernel_copy.wait()
    for comp in range(2):
        for part in range(2):
            whole = kernel_ref[comp, part]
            hi, lo = hilo(whole)
            both = jnp.concatenate([dot(flip[:HALF], hi), dot(flip[:HALF], lo)], 0)
            both = dot(both.astype(BF), flip)
            turned = both[:HALF] + both[HALF:]
            if part == 0:
                half_ref[comp, part] = 0.5 * (whole[:HALF] + turned)
            else:
                half_ref[comp, part] = 0.5 * (whole[:HALF] - turned)


def prepare(places, kernel_hat):
    n = 4 * places[0].shape[-1]
    return pl.pallas_call(
        prepare_body,
        out_shape=[
            jax.ShapeDtypeStruct((2, 2, HALF, PAD), F32),
            jax.ShapeDtypeStruct((GRID, n), F32),
            jax.ShapeDtypeStruct((3 * GRID, n), BF),
        ],
        in_specs=[VM] * 3 + [HBM] * 2,
        out_specs=[VM] * 3,
        scratch_shapes=[
            pltpu.VMEM(places[0].shape, F32),
            pltpu.VMEM(kernel_hat.shape, F32),
            pltpu.SemaphoreType.DMA((2,)),
        ],
        compiler_params=params(16),
        name="prepare",
    )(*places[1:], in_hbm(places[0]), in_hbm(kernel_hat))


def field_body(
    partners_hbm, offsets_hbm, counts_hbm,
    own_ref, r1_ref, r2_ref, s1_ref, s2_ref,
    rows_hbm, cols_hbm, bcols_hbm, brows_hbm,
    half_ref, wx_ref, wy_ref,
    out_ref,
    partners_ref, offsets_ref, counts_ref,
    grids, source, rows_ref, cols_ref, bcols_ref, brows_ref, sems,
):
    b = lax.axis_index("bunch")
    ndev = lax.axis_size("bunch")
    h = chip_half()
    c = core()
    fixed = [
        pltpu.make_async_copy(src, dst, sems.at[i])
        for i, (src, dst) in enumerate((
            (partners_hbm, partners_ref), (offsets_hbm, offsets_ref), (counts_hbm, counts_ref),
            (rows_hbm, rows_ref), (cols_hbm, cols_ref),
            (bcols_hbm, bcols_ref), (brows_hbm, brows_ref),
        ))
    ]
    for copy in fixed:
        copy.start()
    places = (2, 1 + 2 * c, 4 * c, 3 - 2 * c, 4 - 4 * c)
    for ref, place in zip((own_ref, r1_ref, r2_ref, s1_ref, s2_ref), places):
        grids[place] = ref[...]
    source[...] = jnp.zeros_like(source)
    lane = lax.broadcasted_iota(jnp.int32, (GRID, GRID), 1)
    for copy in fixed[:3]:
        copy.wait()
    live = counts_ref[h, c]
    for s in range(partners_ref.shape[-1]):
        p = partners_ref[h, c, s]
        rel = lax.rem(lax.div(p, 2) - b + HOPS + 2 * ndev, ndev)
        r0 = offsets_ref[0, h, c, s] + OFFSET
        c0 = offsets_ref[1, h, c, s] + OFFSET
        gain = jnp.where(s < live, 1.0, 0.0)
        turned = pltpu.roll(grids[rel, lax.rem(p, 2)], c0, 1) * gain
        low = jnp.where(lane >= c0, turned, 0.0)
        source[0, pl.ds(r0, GRID), :] += low
        source[1, pl.ds(r0, GRID), :] += turned - low
    hi, lo = hilo(jnp.concatenate([source[0, 0:SPAN, :], source[1, 0:SPAN, :]], 1))
    fixed[3].wait()
    half = dot(rows_ref[...], jnp.concatenate([hi, lo, hi], 0))
    hi, lo = hilo(half)
    fixed[4].wait()
    spec = dot(jnp.concatenate([hi, lo, hi], 1), cols_ref[...])
    spec_r = spec[:HALF, :PAD] + spec[HALF:, PAD:]
    spec_i = spec[HALF:, :PAD] - spec[:HALF, PAD:]
    fixed[5].wait()
    back = []
    for comp in range(2):
        kr = half_ref[comp, 0]
        ki = half_ref[comp, 1]
        prod = jnp.concatenate([kr * spec_r - ki * spec_i, kr * spec_i + ki * spec_r], 0)
        hi, lo = hilo(prod)
        t = dot(jnp.concatenate([hi, lo, hi], 1), bcols_ref[...])
        re = t[:HALF, :GRID] - t[HALF:, GRID:]
        im = t[:GRID, GRID:] + t[HALF : HALF + GRID, :GRID]
        first = lax.broadcasted_iota(jnp.int32, (GRID, GRID), 0) == 0
        im = jnp.where(first, re[GRID : GRID + 1], im)
        back.append(jnp.concatenate([re[:GRID], im], 0))
    hi, lo = hilo(jnp.concatenate(back, 1))
    fixed[6].wait()
    field = dot(brows_ref[...], jnp.concatenate([hi, lo, hi], 0))
    field = jnp.concatenate([field[:, :GRID], field[:, GRID:]], 0)
    hi, lo = hilo(field)
    maps = jnp.concatenate([hi, lo, hi], 1)
    n = out_ref.shape[-1]
    chunk = 512
    for start in range(0, 4 * n, chunk):
        t = dot(maps, wy_ref[:, start : start + chunk])
        wx = wx_ref[:, start : start + chunk]
        at = slice(start % n, start % n + chunk)
        out_ref[start // n, 0:1, at] = jnp.sum(t[:GRID] * wx, axis=0, keepdims=True)
        out_ref[start // n, 1:2, at] = jnp.sum(t[GRID:] * wx, axis=0, keepdims=True)


def field_and_kick(partners, offsets, counts, grids, prepared):
    n = prepared[1].shape[-1] // 4
    tables = [jnp.asarray(t) for t in dft_tables()]
    return pl.pallas_call(
        field_body,
        out_shape=jax.ShapeDtypeStruct((4, 2, n), F32),
        in_specs=[HBM] * 3 + [VM] * 5 + [HBM] * 4 + [VM] * 3,
        out_specs=VM,
        scratch_shapes=[
            *[pltpu.SMEM(t.shape, jnp.int32) for t in (partners, offsets, counts)],
            pltpu.VMEM((2 * HOPS + 1, 2, GRID, GRID), F32),
            pltpu.VMEM((2, SPAN + 8, GRID), F32),
            *[pltpu.VMEM(t.shape, BF) for t in tables],
            pltpu.SemaphoreType.DMA((7,)),
        ],
        compiler_params=params(24),
        name="field_and_kick",
    )(
        in_hbm(partners), in_hbm(offsets), in_hbm(counts), *grids,
        *[in_hbm(t) for t in tables], *prepared,
    )


def finish_body(mine_ref, core_ref, chip_ref, momenta_ref, out_ref):
    h = chip_half()
    c = core()
    for coord in range(2):
        at = slice(coord, coord + 1)
        near = mine_ref[0, at, :]
        nearc = core_ref[1, at, :]
        far = chip_ref[0, at, :]
        farc = chip_ref[1, at, :]
        for beam in range(2):
            same = jnp.where(h == beam, near, far)
            other = jnp.where(h == beam, nearc, farc)
            both = jnp.concatenate(
                [jnp.where(c == 0, same, other), jnp.where(c == 0, other, same)], 0
            )
            out_ref[coord, beam] = momenta_ref[coord, beam] + both


def finish(mine, from_core, from_chip, momenta):
    return pl.pallas_call(
        finish_body,
        out_shape=jax.ShapeDtypeStruct(momenta.shape, F32),
        in_specs=[VM] * 4,
        out_specs=VM,
        compiler_params=params(4),
        name="finish",
    )(mine, from_core, from_chip, momenta)


def per_device(positions, momenta, kernel_hat, partners, offsets, counts):
    blocks = lax.axis_size("bunch")
    doms = lax.axis_size("dom")

    def across_cores(x):
        return lax.ppermute(x, "dom", [(i, i ^ 1) for i in range(doms)])

    def across_chips(x):
        return lax.ppermute(x, "dom", [(i, i ^ 2) for i in range(doms)])

    def along_blocks(x, by):
        pairs = []
        for i in range(blocks):
            for j in range(doms):
                to = (i + (by if j % 2 == 0 else -by)) % blocks
                pairs.append((i * doms + j, to * doms + j))
        return lax.ppermute(x, ("bunch", "dom"), pairs)

    pos_y = across_chips(positions)
    pos_c = across_cores(positions)
    first = deposit([positions, pos_c])
    pos_y, first = lax.optimization_barrier((pos_y, first))
    pos_yc = across_cores(pos_y)
    second = deposit([pos_y], first)
    own = deposit([pos_yc], second)
    own, pos_yc = lax.optimization_barrier((own, pos_yc))
    r1 = along_blocks(own, 1)
    r2 = along_blocks(own, 2)
    prepared = prepare((positions, pos_c, pos_y, pos_yc), kernel_hat)
    r1, prepared = lax.optimization_barrier((r1, prepared))
    s1 = across_cores(r1)
    s2 = across_cores(r2)
    mine = field_and_kick(partners, offsets, counts, (own, r1, r2, s1, s2), prepared)
    from_core = across_cores(mine)
    from_chip = across_chips(jnp.stack([mine[2], from_core[3]]))
    return finish(mine, from_core, from_chip, momenta)


def solution(mesh):
    in_specs = (
        P(None, None, "bunch", "dom"),
        P(None, None, "bunch", "dom"),
        P(),
        P(None, "bunch", None),
        P(None, None, "bunch", None),
        P(None, "bunch"),
    )
    out_specs = P(None, None, "bunch", "dom")
    return jax.shard_map(
        per_device, mesh=mesh, in_specs=in_specs, out_specs=out_specs, check_vma=False
    )
```

time: 46.8 us -> 34.5 us (0.74)
  starting transfers between devices: 25.3 us -> 16.8 us
  local copies, waits for them, and re-layouts: 5.23 us -> 0.8 us
  waiting for transfers between devices: 3.96 us -> 7.94 us
  Pallas kernels: 11.8 us -> 8.67 us
    ppermute x6 -> x5, starting transfers between devices: 11 us -> 5.31 us  [across_cores(): return lax.ppermute(x, 'dom', [(i, i ^ 1) for i in range(doms)])]
    unnamed x22 -> x4, local copies, waits for them, and re-layouts: 5.23 us -> 0.79 us
    pallas_call x3 -> x5, Pallas kernels: 10.6 us -> 8.03 us  [the longest x1 3.83 us: field_and_kick(): pl.pallas_call(field_body, out_shape=jax.ShapeDtypeStruct((4, 2, n), F32)...]
    ppermute x2, waiting for transfers between devices: 0.56 us -> 2.85 us  [across_chips(): return lax.ppermute(x, 'dom', [(i, i ^ 2) for i in range(doms)])]
    ppermute x2, starting transfers between devices: 6.05 us -> 3.9 us  [across_chips(): return lax.ppermute(x, 'dom', [(i, i ^ 2) for i in range(doms)])]
    ppermute x2, waiting for transfers between devices: 1.57 us -> 2.95 us  [along_blocks(): return lax.ppermute(x, ('bunch', 'dom'), pairs)]
    ppermute x2, starting transfers between devices: 8.25 us -> 7.64 us  [along_blocks(): return lax.ppermute(x, ('bunch', 'dom'), pairs)]
    pallas_call x1, Pallas kernels: 1.19 us -> 0.65 us  [finish(): pl.pallas_call(finish_body, out_shape=jax.ShapeDtypeStruct(momenta.shape,...]
  transfers between devices with their start and end apart: 10 -> 9, of which waited for: 5 -> 7; matrix products, arithmetic and copies ran while one was open for 0% -> 0% of each run, Pallas kernels for 4% -> 10%
where the time goes in v2:
time: 34.5 us; the launch traced here: 34.3 us
  starting transfers between devices  16.8 us (49%)
  Pallas kernels  8.67 us (25%)
  waiting for transfers between devices  7.94 us (23%)
  local copies, waits for them, and re-layouts  0.8 us (2%)
    ppermute x2, starting transfers between devices, along_blocks(): return lax.ppermute(x, ('bunch', 'dom'), pairs)  7.64 us
    ppermute x5, starting transfers between devices, across_cores(): return lax.ppermute(x, 'dom', [(i, i ^ 1) for i in range(doms)])  5.31 us
    ppermute x2, starting transfers between devices, across_chips(): return lax.ppermute(x, 'dom', [(i, i ^ 2) for i in range(doms)])  3.9 us
    pallas_call x1, Pallas kernels, field_and_kick(): pl.pallas_call(field_body, out_shape=jax.ShapeDtypeStruct((4, 2, n), F32)...  3.83 us
    ppermute x2, waiting for transfers between devices, along_blocks(): return lax.ppermute(x, ('bunch', 'dom'), pairs)  2.95 us
    ppermute x2, waiting for transfers between devices, across_chips(): return lax.ppermute(x, 'dom', [(i, i ^ 2) for i in range(doms)])  2.85 us
    pallas_call x3, Pallas kernels, deposit(): pl.pallas_call(functools.partial(deposit_body, len(sources)), out_shape=j...  2.37 us
    ppermute x5, waiting for transfers between devices, across_cores(): return lax.ppermute(x, 'dom', [(i, i ^ 1) for i in range(doms)])  2.13 us
  transfers between devices with their start and end apart: 9, of which 7 were waited for; matrix products, arithmetic and copies ran while one was open for 0% of the time, Pallas kernels for 10%

profile of v2, /device:TPU:1, one launch (start us, length us, event | category | flops | bytes accessed | tf_op | source)
XLA Modules:
  0.0 34.3 jit_solution(4517521940896119098)
XLA Ops:
  0.0 3.2 %collective-permute-start.1 = (f32[2,2,2,1024]{3,2,1,0:T(2,128)}, f32[2,2,2,1024]{3,2,1,0:T(2,128)S(1)}, u32[]{:S(2)}, u32[]{:S(2)}) collective-permute-start(f32[2,2,2,1024]{3,2,1,0:T(2,128)} %pa_hbm.1), channel_id=1, source_target_pairs={{0,1},{1,0},{2,3},{3,2},{4,5},{5,4},{6,7},{7,6},{8,9},{9,8},{10,11... | collective-permute-start | bytes 98312 | tf_op jit(solution)/shard_map/ppermute | solution.py:318
  3.2 1.2 %collective-permute-start = (f32[2,2,2,1024]{3,2,1,0:T(2,128)}, f32[2,2,2,1024]{3,2,1,0:T(2,128)S(1)}, u32[]{:S(2)}, u32[]{:S(2)}) collective-permute-start(f32[2,2,2,1024]{3,2,1,0:T(2,128)} %pa_hbm.1), channel_id=1, source_target_pairs={{0,2},{1,3},{2,0},{3,1},{4,6},{5,7},{6,4},{7,5},{8,10},{9,11},{10,... | collective-permute-start | bytes 98312 | tf_op jit(solution)/shard_map/ppermute | solution.py:321
  4.4 0.0 collective-permute-done.1.refs_1_.pc_ref
  4.4 0.0 copy-start
  4.4 0.8 %copy-done = f32[2,2,2,1024]{3,2,1,0:T(2,128)S(1)} copy-done((f32[2,2,2,1024]{3,2,1,0:T(2,128)S(1)}, f32[2,2,2,1024]{3,2,1,0:T(2,128)}, u32[]{:S(2)}) %copy-start) | copy-done | bytes 32792
  5.2 1.1 %deposit.3.refs_1_ = f32[2,128,128]{2,1,0:T(8,128)S(1)} custom-call(f32[2,2,2,1024]{3,2,1,0:T(2,128)S(1)} %copy-done, f32[2,2,2,1024]{3,2,1,0:T(2,128)S(1)} %collective-permute-done.1.refs_1_.pc_ref), custom_call_target="tpu_custom_call" | custom-call | tf_op jit(solution)/shard_map/deposit/pallas_call | solution.py:111
  6.3 1.4 %collective-permute-done.refs_0_.py_ref = f32[2,2,2,1024]{3,2,1,0:T(2,128)S(1)} collective-permute-done((f32[2,2,2,1024]{3,2,1,0:T(2,128)}, f32[2,2,2,1024]{3,2,1,0:T(2,128)S(1)}, u32[]{:S(2)}, u32[]{:S(2)}) %collective-permute-start) | collective-permute-done | bytes 32800 | tf_op jit(solution)/shard_map/ppermute | solution.py:321
  7.7 1.2 %collective-permute-start.2 = (f32[2,2,2,1024]{3,2,1,0:T(2,128)S(1)}, f32[2,2,2,1024]{3,2,1,0:T(2,128)S(1)}, u32[]{:S(2)}, u32[]{:S(2)}) collective-permute-start(f32[2,2,2,1024]{3,2,1,0:T(2,128)S(1)} %collective-permute-done.refs_0_.py_ref), channel_id=1, source_target_pairs={{0,1},{1,0},{2,3},{3,2},{4,5},{5,4},{6,7},{7,6},{8,9},{9,8},{10,11... | collective-permute-start | bytes 98312 | tf_op jit(solution)/shard_map/ppermute | solution.py:318
  8.9 0.6 %deposit.4.refs_1_ = f32[2,128,128]{2,1,0:T(8,128)S(1)} custom-call(f32[2,2,2,1024]{3,2,1,0:T(2,128)S(1)} %collective-permute-done.refs_0_.py_ref, f32[2,128,128]{2,1,0:T(8,128)S(1)} %deposit.3.refs_1_), custom_call_target="tpu_custom_call" | custom-call | tf_op jit(solution)/shard_map/deposit/pallas_call | solution.py:111
  9.5 0.2 collective-permute-done.2.refs_0_.pyc_ref
  9.7 0.6 %deposit.5.own_ref = f32[2,128,128]{2,1,0:T(8,128)S(1)} custom-call(f32[2,2,2,1024]{3,2,1,0:T(2,128)S(1)} %collective-permute-done.2.refs_0_.pyc_ref, f32[2,128,128]{2,1,0:T(8,128)S(1)} %deposit.4.refs_1_), custom_call_target="tpu_custom_call" | custom-call | tf_op jit(solution)/shard_map/deposit/pallas_call | solution.py:111
  10.4 7.1 %collective-permute-start.3 = (f32[2,128,128]{2,1,0:T(8,128)S(1)}, f32[2,128,128]{2,1,0:T(8,128)S(1)}, u32[]{:S(2)}, u32[]{:S(2)}) collective-permute-start(f32[2,128,128]{2,1,0:T(8,128)S(1)} %deposit.5.own_ref), channel_id=1, source_target_pairs={{0,4},{1,253},{2,6},{3,255},{4,8},{5,1},{6,10},{7,3},{8,12},{9,5},... | collective-permute-start | bytes 393224 | tf_op jit(solution)/shard_map/ppermute | solution.py:329
  17.5 0.5 %collective-permute-start.4 = (f32[2,128,128]{2,1,0:T(8,128)S(1)}, f32[2,128,128]{2,1,0:T(8,128)S(1)}, u32[]{:S(2)}, u32[]{:S(2)}) collective-permute-start(f32[2,128,128]{2,1,0:T(8,128)S(1)} %deposit.5.own_ref), channel_id=1, source_target_pairs={{0,8},{1,249},{2,10},{3,251},{4,12},{5,253},{6,14},{7,255},{8,16},... | collective-permute-start | bytes 393224 | tf_op jit(solution)/shard_map/ppermute | solution.py:329
  18.0 1.8 %prepare.1 = (f32[2,2,136,256]{3,2,1,0:T(8,128)S(1)}, f32[128,4096]{1,0:T(8,128)S(1)}, bf16[384,4096]{1,0:T(8,128)(2,1)S(1)}) custom-call(f32[2,2,2,1024]{3,2,1,0:T(2,128)S(1)} %collective-permute-done.1.refs_1_.pc_ref, f32[2,2,2,1024]{3,2,1,0:T(2,128)S(1)} %collective-permute-done.refs_0_.py_ref, ...), custom_call_target="tpu_custom_call" | custom-call | tf_op jit(solution)/shard_map/prepare/pallas_call | solution.py:164
  19.9 0.0 collective-permute-done.3.r1_ref
  19.9 0.0 copy-start.1
  19.9 2.9 %collective-permute-done.4.r2_ref = f32[2,128,128]{2,1,0:T(8,128)S(1)} collective-permute-done((f32[2,128,128]{2,1,0:T(8,128)S(1)}, f32[2,128,128]{2,1,0:T(8,128)S(1)}, u32[]{:S(2)}, u32[]{:S(2)}) %collective-permute-start.4) | collective-permute-done | bytes 131104 | tf_op jit(solution)/shard_map/ppermute | solution.py:329
  22.8 0.0 collective-permute-start.6
  22.8 0.5 %collective-permute-start.5 = (f32[2,128,128]{2,1,0:T(8,128)S(1)}, f32[2,128,128]{2,1,0:T(8,128)S(1)}, u32[]{:S(2)}, u32[]{:S(2)}) collective-permute-start(f32[2,128,128]{2,1,0:T(8,128)S(1)} %collective-permute-done.3.r1_ref), channel_id=1, source_target_pairs={{0,1},{1,0},{2,3},{3,2},{4,5},{5,4},{6,7},{7,6},{8,9},{9,8},{10,11... | collective-permute-start | bytes 393224 | tf_op jit(solution)/shard_map/ppermute | solution.py:318
  23.3 0.8 %collective-permute-done.6.s2_ref = f32[2,128,128]{2,1,0:T(8,128)S(1)} collective-permute-done((f32[2,128,128]{2,1,0:T(8,128)S(1)}, f32[2,128,128]{2,1,0:T(8,128)S(1)}, u32[]{:S(2)}, u32[]{:S(2)}) %collective-permute-start.6) | collective-permute-done | bytes 131104 | tf_op jit(solution)/shard_map/ppermute | solution.py:318
  24.2 0.2 collective-permute-done.5.s1_ref
  24.4 3.8 %field_and_kick.1.mine_ref = f32[4,2,1024]{2,1,0:T(2,128)S(1)} custom-call(s32[2,2,16]{2,1,0:T(2,128)} %partners_hbm.1, s32[2,2,2,16]{3,2,1,0:T(2,128)} %offsets_hbm.1, s32[2,2]{1,0:T(2,128)} %counts_hbm.1, f32[2,128,128]{2,1,0:T(8,128)S(1)} %deposit.5.own_ref, f32[2,128,128]{2,1,0:T(8,128)S(1)} %collective-permute-done.3.r1_ref, ...), custom_call_target="tpu_custom_call" | custom-call | tf_op jit(solution)/shard_map/field_and_kick/pallas_call | solution.py:264
  28.2 0.4 %collective-permute-start.7 = (f32[4,2,1024]{2,1,0:T(2,128)S(1)}, f32[4,2,1024]{2,1,0:T(2,128)S(1)}, u32[]{:S(2)}, u32[]{:S(2)}) collective-permute-start(f32[4,2,1024]{2,1,0:T(2,128)S(1)} %field_and_kick.1.mine_ref), channel_id=1, source_target_pairs={{0,1},{1,0},{2,3},{3,2},{4,5},{5,4},{6,7},{7,6},{8,9},{9,8},{10,11... | collective-permute-start | bytes 98312 | tf_op jit(solution)/shard_map/ppermute | solution.py:318
  28.6 0.9 %collective-permute-done.7.core_ref = f32[4,2,1024]{2,1,0:T(2,128)S(1)} collective-permute-done((f32[4,2,1024]{2,1,0:T(2,128)S(1)}, f32[4,2,1024]{2,1,0:T(2,128)S(1)}, u32[]{:S(2)}, u32[]{:S(2)}) %collective-permute-start.7) | collective-permute-done | bytes 32800 | tf_op jit(solution)/shard_map/ppermute | solution.py:318
  29.5 2.7 %collective-permute-start.8 = (f32[2,2,1024]{2,1,0:T(2,128)S(1)}, f32[2,2,1024]{2,1,0:T(2,128)S(1)}, u32[]{:S(2)}, u32[]{:S(2)}) collective-permute-start(f32[2,2,1024]{2,1,0:T(2,128)S(1)} %pad_maximum_fusion), channel_id=1, source_target_pairs={{0,2},{1,3},{2,0},{3,1},{4,6},{5,7},{6,4},{7,5},{8,10},{9,11},{10,... | collective-permute-start | bytes 49160 | tf_op jit(solution)/shard_map/ppermute | solution.py:321
  32.2 1.5 %collective-permute-done.8.chip_ref = f32[2,2,1024]{2,1,0:T(2,128)S(1)} collective-permute-done((f32[2,2,1024]{2,1,0:T(2,128)S(1)}, f32[2,2,1024]{2,1,0:T(2,128)S(1)}, u32[]{:S(2)}, u32[]{:S(2)}) %collective-permute-start.8) | collective-permute-done | bytes 16416 | tf_op jit(solution)/shard_map/ppermute | solution.py:321
  33.7 0.0 copy-done.1
  33.7 0.6 %finish.1 = f32[2,2,2,1024]{3,2,1,0:T(2,128)} custom-call(f32[4,2,1024]{2,1,0:T(2,128)S(1)} %field_and_kick.1.mine_ref, f32[4,2,1024]{2,1,0:T(2,128)S(1)} %collective-permute-done.7.core_ref, f32[2,2,1024]{2,1,0:T(2,128)S(1)} %collective-permute-done.8.chip_ref, f32[2,2,2,1024]{3,2,1,0:T(2,128)S(1)} %copy-done.1), custom_call_target="tpu_custom_call" | custom-call | tf_op jit(solution)/shard_map/finish/pallas_call | solution.py:303
  (3 shorter events, 0.0 us)
Async XLA Ops:
  0.0 4.4 %collective-permute-start.1 = (f32[2,2,2,1024]{3,2,1,0:T(2,128)}, f32[2,2,2,1024]{3,2,1,0:T(2,128)S(1)}, u32[]{:S(2)}, u32[]{:S(2)}) collective-permute-start(f32[2,2,2,1024]{3,2,1,0:T(2,128)} %pa_hbm.1), channel_id=1, source_target_pairs={{0,1},{1,0},{2,3},{3,2},{4,5},{5,4},{6,7},{7,6},{8,9},{9,8},{10,11... | collective-permute-start | bytes 98312 | tf_op jit(solution)/shard_map/ppermute | solution.py:318
  3.2 4.5 %collective-permute-start = (f32[2,2,2,1024]{3,2,1,0:T(2,128)}, f32[2,2,2,1024]{3,2,1,0:T(2,128)S(1)}, u32[]{:S(2)}, u32[]{:S(2)}) collective-permute-start(f32[2,2,2,1024]{3,2,1,0:T(2,128)} %pa_hbm.1), channel_id=1, source_target_pairs={{0,2},{1,3},{2,0},{3,1},{4,6},{5,7},{6,4},{7,5},{8,10},{9,11},{10,... | collective-permute-start | bytes 98312 | tf_op jit(solution)/shard_map/ppermute | solution.py:321
  4.4 0.8 %copy-start = (f32[2,2,2,1024]{3,2,1,0:T(2,128)S(1)}, f32[2,2,2,1024]{3,2,1,0:T(2,128)}, u32[]{:S(2)}) copy-start(f32[2,2,2,1024]{3,2,1,0:T(2,128)} %pa_hbm.1) | copy-start | bytes 98308
  7.7 2.0 %collective-permute-start.2 = (f32[2,2,2,1024]{3,2,1,0:T(2,128)S(1)}, f32[2,2,2,1024]{3,2,1,0:T(2,128)S(1)}, u32[]{:S(2)}, u32[]{:S(2)}) collective-permute-start(f32[2,2,2,1024]{3,2,1,0:T(2,128)S(1)} %collective-permute-done.refs_0_.py_ref), channel_id=1, source_target_pairs={{0,1},{1,0},{2,3},{3,2},{4,5},{5,4},{6,7},{7,6},{8,9},{9,8},{10,11... | collective-permute-start | bytes 98312 | tf_op jit(solution)/shard_map/ppermute | solution.py:318
  10.4 9.5 %collective-permute-start.3 = (f32[2,128,128]{2,1,0:T(8,128)S(1)}, f32[2,128,128]{2,1,0:T(8,128)S(1)}, u32[]{:S(2)}, u32[]{:S(2)}) collective-permute-start(f32[2,128,128]{2,1,0:T(8,128)S(1)} %deposit.5.own_ref), channel_id=1, source_target_pairs={{0,4},{1,253},{2,6},{3,255},{4,8},{5,1},{6,10},{7,3},{8,12},{9,5},... | collective-permute-start | bytes 393224 | tf_op jit(solution)/shard_map/ppermute | solution.py:329
  17.5 5.3 %collective-permute-start.4 = (f32[2,128,128]{2,1,0:T(8,128)S(1)}, f32[2,128,128]{2,1,0:T(8,128)S(1)}, u32[]{:S(2)}, u32[]{:S(2)}) collective-permute-start(f32[2,128,128]{2,1,0:T(8,128)S(1)} %deposit.5.own_ref), channel_id=1, source_target_pairs={{0,8},{1,249},{2,10},{3,251},{4,12},{5,253},{6,14},{7,255},{8,16},... | collective-permute-start | bytes 393224 | tf_op jit(solution)/shard_map/ppermute | solution.py:329
  19.9 13.8 %copy-start.1 = (f32[2,2,2,1024]{3,2,1,0:T(2,128)S(1)}, f32[2,2,2,1024]{3,2,1,0:T(2,128)}, u32[]{:S(2)}) copy-start(f32[2,2,2,1024]{3,2,1,0:T(2,128)} %momenta_ref.1) | copy-start | bytes 98308
  22.8 1.3 %collective-permute-start.6 = (f32[2,128,128]{2,1,0:T(8,128)S(1)}, f32[2,128,128]{2,1,0:T(8,128)S(1)}, u32[]{:S(2)}, u32[]{:S(2)}) collective-permute-start(f32[2,128,128]{2,1,0:T(8,128)S(1)} %collective-permute-done.4.r2_ref), channel_id=1, source_target_pairs={{0,1},{1,0},{2,3},{3,2},{4,5},{5,4},{6,7},{7,6},{8,9},{9,8},{10,11... | collective-permute-start | bytes 393224 | tf_op jit(solution)/shard_map/ppermute | solution.py:318
  22.8 1.5 %collective-permute-start.5 = (f32[2,128,128]{2,1,0:T(8,128)S(1)}, f32[2,128,128]{2,1,0:T(8,128)S(1)}, u32[]{:S(2)}, u32[]{:S(2)}) collective-permute-start(f32[2,128,128]{2,1,0:T(8,128)S(1)} %collective-permute-done.3.r1_ref), channel_id=1, source_target_pairs={{0,1},{1,0},{2,3},{3,2},{4,5},{5,4},{6,7},{7,6},{8,9},{9,8},{10,11... | collective-permute-start | bytes 393224 | tf_op jit(solution)/shard_map/ppermute | solution.py:318
  28.2 1.3 %collective-permute-start.7 = (f32[4,2,1024]{2,1,0:T(2,128)S(1)}, f32[4,2,1024]{2,1,0:T(2,128)S(1)}, u32[]{:S(2)}, u32[]{:S(2)}) collective-permute-start(f32[4,2,1024]{2,1,0:T(2,128)S(1)} %field_and_kick.1.mine_ref), channel_id=1, source_target_pairs={{0,1},{1,0},{2,3},{3,2},{4,5},{5,4},{6,7},{7,6},{8,9},{9,8},{10,11... | collective-permute-start | bytes 98312 | tf_op jit(solution)/shard_map/ppermute | solution.py:318
  29.5 4.2 %collective-permute-start.8 = (f32[2,2,1024]{2,1,0:T(2,128)S(1)}, f32[2,2,1024]{2,1,0:T(2,128)S(1)}, u32[]{:S(2)}, u32[]{:S(2)}) collective-permute-start(f32[2,2,1024]{2,1,0:T(2,128)S(1)} %pad_maximum_fusion), channel_id=1, source_target_pairs={{0,2},{1,3},{2,0},{3,1},{4,6},{5,7},{6,4},{7,5},{8,10},{9,11},{10,... | collective-permute-start | bytes 49160 | tf_op jit(solution)/shard_map/ppermute | solution.py:321

commit v3 on v2

--- a/solution.py
+++ b/solution.py
@@ -14,6 +14,7 @@
 SPAN = GRID + 2 * OFFSET
 HALF = 136
 HOPS = 2
+CHUNK = 512
 BF = jnp.bfloat16
 F32 = jnp.float32
 VM = pl.BlockSpec(memory_space=pltpu.VMEM)
@@ -120,8 +121,18 @@
 
 
 def prepare_body(
-    pc_ref, py_ref, pyc_ref, pa_hbm, kernel_hbm, half_ref, wx_ref, wy_ref, pa_ref, kernel_ref, sems
+    pc_ref, py_ref, pyc_ref, pa_hbm, kernel_hbm, partners_hbm, offsets_hbm, counts_hbm,
+    half_ref, wx_ref, wy_ref, slots_ref,
+    pa_ref, kernel_ref, partners_ref, offsets_ref, counts_ref, sems,
 ):
+    small = [
+        pltpu.make_async_copy(src, dst, sems.at[i + 2])
+        for i, (src, dst) in enumerate((
+            (partners_hbm, partners_ref), (offsets_hbm, offsets_ref), (counts_hbm, counts_ref)
+        ))
+    ]
+    for copy in small:
+        copy.start()
     own_copy = pltpu.make_async_copy(pa_hbm, pa_ref, sems.at[0])
     kernel_copy = pltpu.make_async_copy(kernel_hbm, kernel_ref, sems.at[1])
     own_copy.start()
@@ -157,79 +168,95 @@
                 half_ref[comp, part] = 0.5 * (whole[:HALF] + turned)
             else:
                 half_ref[comp, part] = 0.5 * (whole[:HALF] - turned)
-
-
-def prepare(places, kernel_hat):
+    for copy in small:
+        copy.wait()
+    b = lax.axis_index("bunch")
+    ndev = lax.axis_size("bunch")
+    live = counts_ref[h, c]
+    for s in range(partners_ref.shape[-1]):
+        p = partners_ref[h, c, s]
+        rel = lax.rem(lax.div(p, 2) - b + HOPS + 2 * ndev, ndev)
+        r0 = offsets_ref[0, h, c, s] + OFFSET
+        c0 = offsets_ref[1, h, c, s] + OFFSET
+        used = jnp.where(s < live, 1, 0)
+        code = ((used * 16 + rel * 2 + lax.rem(p, 2)) * 128 + r0) * 128 + c0
+        slots_ref[s : s + 1, :] = jnp.full((1, 128), code, jnp.int32)
+
+
+def prepare(places, kernel_hat, partners, offsets, counts):
     n = 4 * places[0].shape[-1]
+    small = (partners, offsets, counts)
     return pl.pallas_call(
         prepare_body,
         out_shape=[
             jax.ShapeDtypeStruct((2, 2, HALF, PAD), F32),
             jax.ShapeDtypeStruct((GRID, n), F32),
             jax.ShapeDtypeStruct((3 * GRID, n), BF),
+            jax.ShapeDtypeStruct((partners.shape[-1], 128), jnp.int32),
         ],
-        in_specs=[VM] * 3 + [HBM] * 2,
-        out_specs=[VM] * 3,
+        in_specs=[VM] * 3 + [HBM] * 5,
+        out_specs=[VM] * 4,
         scratch_shapes=[
             pltpu.VMEM(places[0].shape, F32),
             pltpu.VMEM(kernel_hat.shape, F32),
-            pltpu.SemaphoreType.DMA((2,)),
+            *[pltpu.SMEM(t.shape, jnp.int32) for t in small],
+            pltpu.SemaphoreType.DMA((5,)),
         ],
         compiler_params=params(16),
         name="prepare",
-    )(*places[1:], in_hbm(places[0]), in_hbm(kernel_hat))
+    )(*places[1:], *[in_hbm(t) for t in (places[0], kernel_hat, *small)])
+
+
+def kick_of(maps, wx, wy):
+    t = dot(maps, wy)
+    kx = jnp.sum(t[:GRID] * wx, axis=0, keepdims=True)
+    ky = jnp.sum(t[GRID:] * wx, axis=0, keepdims=True)
+    return kx, ky
 
 
 def field_body(
-    partners_hbm, offsets_hbm, counts_hbm,
     own_ref, r1_ref, r2_ref, s1_ref, s2_ref,
     rows_hbm, cols_hbm, bcols_hbm, brows_hbm,
-    half_ref, wx_ref, wy_ref,
-    out_ref,
-    partners_ref, offsets_ref, counts_ref,
+    half_ref, wx_ref, wy_ref, slots_ref,
+    maps_ref, out_ref,
     grids, source, rows_ref, cols_ref, bcols_ref, brows_ref, sems,
 ):
-    b = lax.axis_index("bunch")
-    ndev = lax.axis_size("bunch")
-    h = chip_half()
     c = core()
     fixed = [
         pltpu.make_async_copy(src, dst, sems.at[i])
         for i, (src, dst) in enumerate((
-            (partners_hbm, partners_ref), (offsets_hbm, offsets_ref), (counts_hbm, counts_ref),
             (rows_hbm, rows_ref), (cols_hbm, cols_ref),
             (bcols_hbm, bcols_ref), (brows_hbm, brows_ref),
         ))
     ]
     for copy in fixed:
         copy.start()
+    slots = slots_ref[...]
     places = (2, 1 + 2 * c, 4 * c, 3 - 2 * c, 4 - 4 * c)
     for ref, place in zip((own_ref, r1_ref, r2_ref, s1_ref, s2_ref), places):
-        grids[place] = ref[...]
+        grids[2 * place] = ref[0]
+        grids[2 * place + 1] = ref[1]
     source[...] = jnp.zeros_like(source)
     lane = lax.broadcasted_iota(jnp.int32, (GRID, GRID), 1)
-    for copy in fixed[:3]:
-        copy.wait()
-    live = counts_ref[h, c]
-    for s in range(partners_ref.shape[-1]):
-        p = partners_ref[h, c, s]
-        rel = lax.rem(lax.div(p, 2) - b + HOPS + 2 * ndev, ndev)
-        r0 = offsets_ref[0, h, c, s] + OFFSET
-        c0 = offsets_ref[1, h, c, s] + OFFSET
-        gain = jnp.where(s < live, 1.0, 0.0)
-        turned = pltpu.roll(grids[rel, lax.rem(p, 2)], c0, 1) * gain
+    for s in range(slots_ref.shape[0]):
+        code = slots[s, 0]
+        c0 = code & 127
+        r0 = lax.shift_right_logical(code, 7) & 127
+        which = lax.shift_right_logical(code, 14) & 15
+        gain = lax.shift_right_logical(code, 18).astype(F32)
+        turned = pltpu.roll(grids[which], c0, 1) * gain
         low = jnp.where(lane >= c0, turned, 0.0)
         source[0, pl.ds(r0, GRID), :] += low
         source[1, pl.ds(r0, GRID), :] += turned - low
     hi, lo = hilo(jnp.concatenate([source[0, 0:SPAN, :], source[1, 0:SPAN, :]], 1))
-    fixed[3].wait()
+    fixed[0].wait()
     half = dot(rows_ref[...], jnp.concatenate([hi, lo, hi], 0))
     hi, lo = hilo(half)
-    fixed[4].wait()
+    fixed[1].wait()
     spec = dot(jnp.concatenate([hi, lo, hi], 1), cols_ref[...])
     spec_r = spec[:HALF, :PAD] + spec[HALF:, PAD:]
     spec_i = spec[HALF:, :PAD] - spec[:HALF, PAD:]
-    fixed[5].wait()
+    fixed[2].wait()
     back = []
     for comp in range(2):
         kr = half_ref[comp, 0]
@@ -243,42 +270,67 @@
         im = jnp.where(first, re[GRID : GRID + 1], im)
         back.append(jnp.concatenate([re[:GRID], im], 0))
     hi, lo = hilo(jnp.concatenate(back, 1))
-    fixed[6].wait()
+    fixed[3].wait()
     field = dot(brows_ref[...], jnp.concatenate([hi, lo, hi], 0))
     field = jnp.concatenate([field[:, :GRID], field[:, GRID:]], 0)
     hi, lo = hilo(field)
     maps = jnp.concatenate([hi, lo, hi], 1)
+    maps_ref[...] = maps
     n = out_ref.shape[-1]
-    chunk = 512
-    for start in range(0, 4 * n, chunk):
-        t = dot(maps, wy_ref[:, start : start + chunk])
-        wx = wx_ref[:, start : start + chunk]
-        at = slice(start % n, start % n + chunk)
-        out_ref[start // n, 0:1, at] = jnp.sum(t[:GRID] * wx, axis=0, keepdims=True)
-        out_ref[start // n, 1:2, at] = jnp.sum(t[GRID:] * wx, axis=0, keepdims=True)
-
-
-def field_and_kick(partners, offsets, counts, grids, prepared):
+    for start in range(0, n, CHUNK):
+        at = slice(3 * n + start, 3 * n + start + CHUNK)
+        kx, ky = kick_of(maps, wx_ref[:, at], wy_ref[:, at])
+        out_ref[0:1, start : start + CHUNK] = kx
+        out_ref[1:2, start : start + CHUNK] = ky
+
+
+def field(grids, prepared):
     n = prepared[1].shape[-1] // 4
     tables = [jnp.asarray(t) for t in dft_tables()]
     return pl.pallas_call(
         field_body,
-        out_shape=jax.ShapeDtypeStruct((4, 2, n), F32),
-        in_specs=[HBM] * 3 + [VM] * 5 + [HBM] * 4 + [VM] * 3,
-        out_specs=VM,
+        out_shape=[
+            jax.ShapeDtypeStruct((2 * GRID, 3 * GRID), BF),
+            jax.ShapeDtypeStruct((2, n), F32),
+        ],
+        in_specs=[VM] * 5 + [HBM] * 4 + [VM] * 4,
+        out_specs=[VM] * 2,
         scratch_shapes=[
-            *[pltpu.SMEM(t.shape, jnp.int32) for t in (partners, offsets, counts)],
-            pltpu.VMEM((2 * HOPS + 1, 2, GRID, GRID), F32),
+            pltpu.VMEM((4 * HOPS + 2, GRID, GRID), F32),
             pltpu.VMEM((2, SPAN + 8, GRID), F32),
             *[pltpu.VMEM(t.shape, BF) for t in tables],
-            pltpu.SemaphoreType.DMA((7,)),
+            pltpu.SemaphoreType.DMA((4,)),
         ],
         compiler_params=params(24),
-        name="field_and_kick",
-    )(
-        in_hbm(partners), in_hbm(offsets), in_hbm(counts), *grids,
-        *[in_hbm(t) for t in tables], *prepared,
-    )
+        name="field",
+    )(*grids, *[in_hbm(t) for t in tables], *prepared)
+
+
+def kick_body(maps_ref, wx_ref, wy_ref, near_ref, far_ref):
+    maps = maps_ref[...]
+    n = far_ref.shape[-1]
+    for start in range(0, 3 * n, CHUNK):
+        at = slice(start, start + CHUNK)
+        kx, ky = kick_of(maps, wx_ref[:, at], wy_ref[:, at])
+        to = slice(start % n, start % n + CHUNK)
+        if start < 2 * n:
+            near_ref[start // n, 0:1, to] = kx
+            near_ref[start // n, 1:2, to] = ky
+        else:
+            far_ref[0:1, to] = kx
+            far_ref[1:2, to] = ky
+
+
+def kick(maps, wx, wy):
+    n = wx.shape[-1] // 4
+    return pl.pallas_call(
+        kick_body,
+        out_shape=[jax.ShapeDtypeStruct((2, 2, n), F32), jax.ShapeDtypeStruct((2, n), F32)],
+        in_specs=[VM] * 3,
+        out_specs=[VM] * 2,
+        compiler_params=params(8),
+        name="kick",
+    )(maps, wx, wy)
 
 
 def finish_body(mine_ref, core_ref, chip_ref, momenta_ref, out_ref):
@@ -338,13 +390,17 @@
     own, pos_yc = lax.optimization_barrier((own, pos_yc))
     r1 = along_blocks(own, 1)
     r2 = along_blocks(own, 2)
-    prepared = prepare((positions, pos_c, pos_y, pos_yc), kernel_hat)
+    prepared = prepare((positions, pos_c, pos_y, pos_yc), kernel_hat, partners, offsets, counts)
     r1, prepared = lax.optimization_barrier((r1, prepared))
     s1 = across_cores(r1)
+    r2, s1 = lax.optimization_barrier((r2, s1))
     s2 = across_cores(r2)
-    mine = field_and_kick(partners, offsets, counts, (own, r1, r2, s1, s2), prepared)
+    maps, diagonal = field((own, r1, r2, s1, s2), prepared)
+    from_core_far = across_cores(diagonal)
+    near, far = kick(maps, prepared[1], prepared[2])
+    message, mine = lax.optimization_barrier((jnp.stack([far, from_core_far]), near))
+    from_chip = across_chips(message)
     from_core = across_cores(mine)
-    from_chip = across_chips(jnp.stack([mine[2], from_core[3]]))
     return finish(mine, from_core, from_chip, momenta)
 
 

time: 34.5 us -> 33.7 us (0.977)
  waiting for transfers between devices: 7.94 us -> 5.56 us
  starting transfers between devices: 16.8 us -> 17.8 us
  Pallas kernels: 8.67 us -> 9.24 us
    ppermute x2, waiting for transfers between devices: 2.95 us -> 1.75 us  [along_blocks(): return lax.ppermute(x, ('bunch', 'dom'), pairs)]
    ppermute x5 -> x6, starting transfers between devices: 5.31 us -> 6.28 us  [across_cores(): return lax.ppermute(x, 'dom', [(i, i ^ 1) for i in range(doms)])]
    ppermute x2, waiting for transfers between devices: 2.85 us -> 2.23 us  [across_chips(): return lax.ppermute(x, 'dom', [(i, i ^ 2) for i in range(doms)])]
    ppermute x5 -> x6, waiting for transfers between devices: 2.13 us -> 1.58 us  [across_cores(): return lax.ppermute(x, 'dom', [(i, i ^ 1) for i in range(doms)])]
    pallas_call x1 -> x2, Pallas kernels: 3.83 us -> 4.18 us  [the longest x1 3.16 us: field(): pl.pallas_call(field_body, out_shape=[jax.ShapeDtypeStruct((2 * GRID, 3 *...]
  transfers between devices with their start and end apart: 9 -> 10, of which waited for: 7 -> 5; matrix products, arithmetic and copies ran while one was open for 0% -> 0% of each run, Pallas kernels for 10% -> 14%
where the time goes in v3:
time: 33.7 us; the launch traced here: 33.5 us
  starting transfers between devices  17.8 us (53%)
  Pallas kernels  9.24 us (27%)
  waiting for transfers between devices  5.56 us (16%)
  local copies, waits for them, and re-layouts  0.79 us (2%)
    ppermute x2, starting transfers between devices, along_blocks(): return lax.ppermute(x, ('bunch', 'dom'), pairs)  7.64 us
    ppermute x6, starting transfers between devices, across_cores(): return lax.ppermute(x, 'dom', [(i, i ^ 1) for i in range(doms)])  6.28 us
    ppermute x2, starting transfers between devices, across_chips(): return lax.ppermute(x, 'dom', [(i, i ^ 2) for i in range(doms)])  3.88 us
    pallas_call x1, Pallas kernels, field(): pl.pallas_call(field_body, out_shape=[jax.ShapeDtypeStruct((2 * GRID, 3 *...  3.16 us
    pallas_call x3, Pallas kernels, deposit(): pl.pallas_call(functools.partial(deposit_body, len(sources)), out_shape=j...  2.37 us
    ppermute x2, waiting for transfers between devices, across_chips(): return lax.ppermute(x, 'dom', [(i, i ^ 2) for i in range(doms)])  2.23 us
    pallas_call x1, Pallas kernels, prepare(): pl.pallas_call(prepare_body, out_shape=[jax.ShapeDtypeStruct((2, 2, HALF,...  2.03 us
    ppermute x2, waiting for transfers between devices, along_blocks(): return lax.ppermute(x, ('bunch', 'dom'), pairs)  1.75 us
  transfers between devices with their start and end apart: 10, of which 5 were waited for; matrix products, arithmetic and copies ran while one was open for 0% of the time, Pallas kernels for 14%

profile of v3, /device:TPU:1, one launch (start us, length us, event | category | flops | bytes accessed | tf_op | source)
XLA Modules:
  0.0 33.5 jit_solution(12891888363054880074)
XLA Ops:
  0.0 3.2 %collective-permute-start.1 = (f32[2,2,2,1024]{3,2,1,0:T(2,128)}, f32[2,2,2,1024]{3,2,1,0:T(2,128)S(1)}, u32[]{:S(2)}, u32[]{:S(2)}) collective-permute-start(f32[2,2,2,1024]{3,2,1,0:T(2,128)} %pa_hbm.1), channel_id=1, source_target_pairs={{0,1},{1,0},{2,3},{3,2},{4,5},{5,4},{6,7},{7,6},{8,9},{9,8},{10,11... | collective-permute-start | bytes 98312 | tf_op jit(solution)/shard_map/ppermute | solution.py:370
  3.2 1.2 %collective-permute-start = (f32[2,2,2,1024]{3,2,1,0:T(2,128)}, f32[2,2,2,1024]{3,2,1,0:T(2,128)S(1)}, u32[]{:S(2)}, u32[]{:S(2)}) collective-permute-start(f32[2,2,2,1024]{3,2,1,0:T(2,128)} %pa_hbm.1), channel_id=1, source_target_pairs={{0,2},{1,3},{2,0},{3,1},{4,6},{5,7},{6,4},{7,5},{8,10},{9,11},{10,... | collective-permute-start | bytes 98312 | tf_op jit(solution)/shard_map/ppermute | solution.py:373
  4.4 0.0 collective-permute-done.1.refs_1_.pc_ref
  4.4 0.0 copy-start
  4.4 0.8 %copy-done = f32[2,2,2,1024]{3,2,1,0:T(2,128)S(1)} copy-done((f32[2,2,2,1024]{3,2,1,0:T(2,128)S(1)}, f32[2,2,2,1024]{3,2,1,0:T(2,128)}, u32[]{:S(2)}) %copy-start) | copy-done | bytes 32792
  5.2 1.1 %deposit.3.refs_1_ = f32[2,128,128]{2,1,0:T(8,128)S(1)} custom-call(f32[2,2,2,1024]{3,2,1,0:T(2,128)S(1)} %copy-done, f32[2,2,2,1024]{3,2,1,0:T(2,128)S(1)} %collective-permute-done.1.refs_1_.pc_ref), custom_call_target="tpu_custom_call" | custom-call | tf_op jit(solution)/shard_map/deposit/pallas_call | solution.py:112
  6.3 1.4 %collective-permute-done.refs_0_.py_ref = f32[2,2,2,1024]{3,2,1,0:T(2,128)S(1)} collective-permute-done((f32[2,2,2,1024]{3,2,1,0:T(2,128)}, f32[2,2,2,1024]{3,2,1,0:T(2,128)S(1)}, u32[]{:S(2)}, u32[]{:S(2)}) %collective-permute-start) | collective-permute-done | bytes 32800 | tf_op jit(solution)/shard_map/ppermute | solution.py:373
  7.7 1.2 %collective-permute-start.2 = (f32[2,2,2,1024]{3,2,1,0:T(2,128)S(1)}, f32[2,2,2,1024]{3,2,1,0:T(2,128)S(1)}, u32[]{:S(2)}, u32[]{:S(2)}) collective-permute-start(f32[2,2,2,1024]{3,2,1,0:T(2,128)S(1)} %collective-permute-done.refs_0_.py_ref), channel_id=1, source_target_pairs={{0,1},{1,0},{2,3},{3,2},{4,5},{5,4},{6,7},{7,6},{8,9},{9,8},{10,11... | collective-permute-start | bytes 98312 | tf_op jit(solution)/shard_map/ppermute | solution.py:370
  8.9 0.6 %deposit.4.refs_1_ = f32[2,128,128]{2,1,0:T(8,128)S(1)} custom-call(f32[2,2,2,1024]{3,2,1,0:T(2,128)S(1)} %collective-permute-done.refs_0_.py_ref, f32[2,128,128]{2,1,0:T(8,128)S(1)} %deposit.3.refs_1_), custom_call_target="tpu_custom_call" | custom-call | tf_op jit(solution)/shard_map/deposit/pallas_call | solution.py:112
  9.5 0.2 collective-permute-done.2.refs_0_.pyc_ref
  9.7 0.6 %deposit.5.own_ref = f32[2,128,128]{2,1,0:T(8,128)S(1)} custom-call(f32[2,2,2,1024]{3,2,1,0:T(2,128)S(1)} %collective-permute-done.2.refs_0_.pyc_ref, f32[2,128,128]{2,1,0:T(8,128)S(1)} %deposit.4.refs_1_), custom_call_target="tpu_custom_call" | custom-call | tf_op jit(solution)/shard_map/deposit/pallas_call | solution.py:112
  10.4 7.1 %collective-permute-start.3 = (f32[2,128,128]{2,1,0:T(8,128)S(1)}, f32[2,128,128]{2,1,0:T(8,128)S(1)}, u32[]{:S(2)}, u32[]{:S(2)}) collective-permute-start(f32[2,128,128]{2,1,0:T(8,128)S(1)} %deposit.5.own_ref), channel_id=1, source_target_pairs={{0,4},{1,253},{2,6},{3,255},{4,8},{5,1},{6,10},{7,3},{8,12},{9,5},... | collective-permute-start | bytes 393224 | tf_op jit(solution)/shard_map/ppermute | solution.py:381
  17.5 0.5 %collective-permute-start.4 = (f32[2,128,128]{2,1,0:T(8,128)S(1)}, f32[2,128,128]{2,1,0:T(8,128)S(1)}, u32[]{:S(2)}, u32[]{:S(2)}) collective-permute-start(f32[2,128,128]{2,1,0:T(8,128)S(1)} %deposit.5.own_ref), channel_id=1, source_target_pairs={{0,8},{1,249},{2,10},{3,251},{4,12},{5,253},{6,14},{7,255},{8,16},... | collective-permute-start | bytes 393224 | tf_op jit(solution)/shard_map/ppermute | solution.py:381
  18.0 2.0 %prepare.1 = (f32[2,2,136,256]{3,2,1,0:T(8,128)S(1)}, f32[128,4096]{1,0:T(8,128)S(1)}, bf16[384,4096]{1,0:T(8,128)(2,1)S(1)}, s32[16,128]{1,0:T(8,128)S(1)}) custom-call(f32[2,2,2,1024]{3,2,1,0:T(2,128)S(1)} %collective-permute-done.1.refs_1_.pc_ref, f32[2,2,2,1024]{3,2,1,0:T(2,128)S(1)} %collective-permute-done.refs_0_.py_ref, ...), custom_call_target="tpu_custom_call" | custom-call | tf_op jit(solution)/shard_map/prepare/pallas_call | solution.py:189
  20.1 0.0 collective-permute-done.3.r1_ref
  20.1 1.0 %collective-permute-start.5 = (f32[2,128,128]{2,1,0:T(8,128)S(1)}, f32[2,128,128]{2,1,0:T(8,128)S(1)}, u32[]{:S(2)}, u32[]{:S(2)}) collective-permute-start(f32[2,128,128]{2,1,0:T(8,128)S(1)} %collective-permute-done.3.r1_ref), channel_id=1, source_target_pairs={{0,1},{1,0},{2,3},{3,2},{4,5},{5,4},{6,7},{7,6},{8,9},{9,8},{10,11... | collective-permute-start | bytes 393224 | tf_op jit(solution)/shard_map/ppermute | solution.py:370
  21.1 1.7 %collective-permute-done.4.r2_ref = f32[2,128,128]{2,1,0:T(8,128)S(1)} collective-permute-done((f32[2,128,128]{2,1,0:T(8,128)S(1)}, f32[2,128,128]{2,1,0:T(8,128)S(1)}, u32[]{:S(2)}, u32[]{:S(2)}) %collective-permute-start.4) | collective-permute-done | bytes 131104 | tf_op jit(solution)/shard_map/ppermute | solution.py:381
  22.8 0.0 collective-permute-done.5.s1_ref
  22.8 0.0 collective-permute-start.6
  22.8 1.3 %collective-permute-done.6.s2_ref = f32[2,128,128]{2,1,0:T(8,128)S(1)} collective-permute-done((f32[2,128,128]{2,1,0:T(8,128)S(1)}, f32[2,128,128]{2,1,0:T(8,128)S(1)}, u32[]{:S(2)}, u32[]{:S(2)}) %collective-permute-start.6) | collective-permute-done | bytes 131104 | tf_op jit(solution)/shard_map/ppermute | solution.py:370
  24.2 3.2 %field.1 = (bf16[256,384]{1,0:T(8,128)(2,1)S(1)}, f32[2,1024]{1,0:T(2,128)S(1)}) custom-call(f32[2,128,128]{2,1,0:T(8,128)S(1)} %deposit.5.own_ref, f32[2,128,128]{2,1,0:T(8,128)S(1)} %collective-permute-done.3.r1_ref, f32[2,128,128]{2,1,0:T(8,128)S(1)} %collective-permute-done.4.r2_ref, f32[2,128,128]{2,1,0:T(8,128)S(1)} %collective-permute-done.5.s1_ref, ...), custom_call_target="tpu_custom_call" | custom-call | tf_op jit(solution)/shard_map/field/pallas_call | solution.py:290
  27.3 0.0 copy-start.1
  27.4 0.2 collective-permute-start.7
  27.6 1.0 %kick.1 = (f32[2,2,1024]{2,1,0:T(2,128)S(1)}, f32[2,1024]{1,0:T(2,128)S(1)}) custom-call(bf16[256,384]{1,0:T(8,128)(2,1)S(1)} %get-tuple-element.41.maps_ref, f32[128,4096]{1,0:T(8,128)S(1)} %get-tuple-element.38.wx_ref, bf16[384,4096]{1,0:T(8,128)(2,1)S(1)} %get-tuple-element.39.wy_ref), custom_call_target="tpu_custom_call" | custom-call | tf_op jit(solution)/shard_map/kick/pallas_call | solution.py:326
  28.6 0.0 collective-permute-done.7
  28.7 2.7 %collective-permute-start.9 = (f32[2,2,1024]{2,1,0:T(2,128)S(1)}, f32[2,2,1024]{2,1,0:T(2,128)S(1)}, u32[]{:S(2)}, u32[]{:S(2)}) collective-permute-start(f32[2,2,1024]{2,1,0:T(2,128)S(1)} %pad_maximum_fusion), channel_id=1, source_target_pairs={{0,2},{1,3},{2,0},{3,1},{4,6},{5,7},{6,4},{7,5},{8,10},{9,11},{10,... | collective-permute-start | bytes 49160 | tf_op jit(solution)/shard_map/ppermute | solution.py:373
  31.4 0.6 %collective-permute-start.8 = (f32[2,2,1024]{2,1,0:T(2,128)S(1)}, f32[2,2,1024]{2,1,0:T(2,128)S(1)}, u32[]{:S(2)}, u32[]{:S(2)}) collective-permute-start(f32[2,2,1024]{2,1,0:T(2,128)S(1)} %get-tuple-element.45.mine_ref), channel_id=1, source_target_pairs={{0,1},{1,0},{2,3},{3,2},{4,5},{5,4},{6,7},{7,6},{8,9},{9,8},{10,11... | collective-permute-start | bytes 49160 | tf_op jit(solution)/shard_map/ppermute | solution.py:370
  32.0 0.8 %collective-permute-done.9.chip_ref = f32[2,2,1024]{2,1,0:T(2,128)S(1)} collective-permute-done((f32[2,2,1024]{2,1,0:T(2,128)S(1)}, f32[2,2,1024]{2,1,0:T(2,128)S(1)}, u32[]{:S(2)}, u32[]{:S(2)}) %collective-permute-start.9) | collective-permute-done | bytes 16416 | tf_op jit(solution)/shard_map/ppermute | solution.py:373
  32.8 0.0 collective-permute-done.8.core_ref
  32.8 0.0 copy-done.1
  32.8 0.6 %finish.1 = f32[2,2,2,1024]{3,2,1,0:T(2,128)} custom-call(f32[2,2,1024]{2,1,0:T(2,128)S(1)} %get-tuple-element.45.mine_ref, f32[2,2,1024]{2,1,0:T(2,128)S(1)} %collective-permute-done.8.core_ref, f32[2,2,1024]{2,1,0:T(2,128)S(1)} %collective-permute-done.9.chip_ref, f32[2,2,2,1024]{3,2,1,0:T(2,128)S(1)} %copy-done.1), custom_call_target="tpu_custom_call" | custom-call | tf_op jit(solution)/shard_map/finish/pallas_call | solution.py:355
  (1 shorter events, 0.0 us)
Async XLA Ops:
  0.0 4.4 %collective-permute-start.1 = (f32[2,2,2,1024]{3,2,1,0:T(2,128)}, f32[2,2,2,1024]{3,2,1,0:T(2,128)S(1)}, u32[]{:S(2)}, u32[]{:S(2)}) collective-permute-start(f32[2,2,2,1024]{3,2,1,0:T(2,128)} %pa_hbm.1), channel_id=1, source_target_pairs={{0,1},{1,0},{2,3},{3,2},{4,5},{5,4},{6,7},{7,6},{8,9},{9,8},{10,11... | collective-permute-start | bytes 98312 | tf_op jit(solution)/shard_map/ppermute | solution.py:370
  3.2 4.5 %collective-permute-start = (f32[2,2,2,1024]{3,2,1,0:T(2,128)}, f32[2,2,2,1024]{3,2,1,0:T(2,128)S(1)}, u32[]{:S(2)}, u32[]{:S(2)}) collective-permute-start(f32[2,2,2,1024]{3,2,1,0:T(2,128)} %pa_hbm.1), channel_id=1, source_target_pairs={{0,2},{1,3},{2,0},{3,1},{4,6},{5,7},{6,4},{7,5},{8,10},{9,11},{10,... | collective-permute-start | bytes 98312 | tf_op jit(solution)/shard_map/ppermute | solution.py:373
  4.4 0.8 %copy-start = (f32[2,2,2,1024]{3,2,1,0:T(2,128)S(1)}, f32[2,2,2,1024]{3,2,1,0:T(2,128)}, u32[]{:S(2)}) copy-start(f32[2,2,2,1024]{3,2,1,0:T(2,128)} %pa_hbm.1) | copy-start | bytes 98308
  7.7 2.0 %collective-permute-start.2 = (f32[2,2,2,1024]{3,2,1,0:T(2,128)S(1)}, f32[2,2,2,1024]{3,2,1,0:T(2,128)S(1)}, u32[]{:S(2)}, u32[]{:S(2)}) collective-permute-start(f32[2,2,2,1024]{3,2,1,0:T(2,128)S(1)} %collective-permute-done.refs_0_.py_ref), channel_id=1, source_target_pairs={{0,1},{1,0},{2,3},{3,2},{4,5},{5,4},{6,7},{7,6},{8,9},{9,8},{10,11... | collective-permute-start | bytes 98312 | tf_op jit(solution)/shard_map/ppermute | solution.py:370
  10.4 9.7 %collective-permute-start.3 = (f32[2,128,128]{2,1,0:T(8,128)S(1)}, f32[2,128,128]{2,1,0:T(8,128)S(1)}, u32[]{:S(2)}, u32[]{:S(2)}) collective-permute-start(f32[2,128,128]{2,1,0:T(8,128)S(1)} %deposit.5.own_ref), channel_id=1, source_target_pairs={{0,4},{1,253},{2,6},{3,255},{4,8},{5,1},{6,10},{7,3},{8,12},{9,5},... | collective-permute-start | bytes 393224 | tf_op jit(solution)/shard_map/ppermute | solution.py:381
  17.5 5.3 %collective-permute-start.4 = (f32[2,128,128]{2,1,0:T(8,128)S(1)}, f32[2,128,128]{2,1,0:T(8,128)S(1)}, u32[]{:S(2)}, u32[]{:S(2)}) collective-permute-start(f32[2,128,128]{2,1,0:T(8,128)S(1)} %deposit.5.own_ref), channel_id=1, source_target_pairs={{0,8},{1,249},{2,10},{3,251},{4,12},{5,253},{6,14},{7,255},{8,16},... | collective-permute-start | bytes 393224 | tf_op jit(solution)/shard_map/ppermute | solution.py:381
  20.1 2.8 %collective-permute-start.5 = (f32[2,128,128]{2,1,0:T(8,128)S(1)}, f32[2,128,128]{2,1,0:T(8,128)S(1)}, u32[]{:S(2)}, u32[]{:S(2)}) collective-permute-start(f32[2,128,128]{2,1,0:T(8,128)S(1)} %collective-permute-done.3.r1_ref), channel_id=1, source_target_pairs={{0,1},{1,0},{2,3},{3,2},{4,5},{5,4},{6,7},{7,6},{8,9},{9,8},{10,11... | collective-permute-start | bytes 393224 | tf_op jit(solution)/shard_map/ppermute | solution.py:370
  22.8 1.3 %collective-permute-start.6 = (f32[2,128,128]{2,1,0:T(8,128)S(1)}, f32[2,128,128]{2,1,0:T(8,128)S(1)}, u32[]{:S(2)}, u32[]{:S(2)}) collective-permute-start(f32[2,128,128]{2,1,0:T(8,128)S(1)} %collective-permute-done.4.r2_ref), channel_id=1, source_target_pairs={{0,1},{1,0},{2,3},{3,2},{4,5},{5,4},{6,7},{7,6},{8,9},{9,8},{10,11... | collective-permute-start | bytes 393224 | tf_op jit(solution)/shard_map/ppermute | solution.py:370
  27.3 5.5 %copy-start.1 = (f32[2,2,2,1024]{3,2,1,0:T(2,128)S(1)}, f32[2,2,2,1024]{3,2,1,0:T(2,128)}, u32[]{:S(2)}) copy-start(f32[2,2,2,1024]{3,2,1,0:T(2,128)} %momenta_ref.1) | copy-start | bytes 98308
  27.4 1.3 %collective-permute-start.7 = (f32[2,1024]{1,0:T(2,128)S(1)}, f32[2,1024]{1,0:T(2,128)S(1)}, u32[]{:S(2)}, u32[]{:S(2)}) collective-permute-start(f32[2,1024]{1,0:T(2,128)S(1)} %get-tuple-element.43), channel_id=1, source_target_pairs={{0,1},{1,0},{2,3},{3,2},{4,5},{5,4},{6,7},{7,6},{8,9},{9,8},{10,11... | collective-permute-start | bytes 24584 | tf_op jit(solution)/shard_map/ppermute | solution.py:370
  28.7 4.2 %collective-permute-start.9 = (f32[2,2,1024]{2,1,0:T(2,128)S(1)}, f32[2,2,1024]{2,1,0:T(2,128)S(1)}, u32[]{:S(2)}, u32[]{:S(2)}) collective-permute-start(f32[2,2,1024]{2,1,0:T(2,128)S(1)} %pad_maximum_fusion), channel_id=1, source_target_pairs={{0,2},{1,3},{2,0},{3,1},{4,6},{5,7},{6,4},{7,5},{8,10},{9,11},{10,... | collective-permute-start | bytes 49160 | tf_op jit(solution)/shard_map/ppermute | solution.py:373
  31.4 1.5 %collective-permute-start.8 = (f32[2,2,1024]{2,1,0:T(2,128)S(1)}, f32[2,2,1024]{2,1,0:T(2,128)S(1)}, u32[]{:S(2)}, u32[]{:S(2)}) collective-permute-start(f32[2,2,1024]{2,1,0:T(2,128)S(1)} %get-tuple-element.45.mine_ref), channel_id=1, source_target_pairs={{0,1},{1,0},{2,3},{3,2},{4,5},{5,4},{6,7},{7,6},{8,9},{9,8},{10,11... | collective-permute-start | bytes 49160 | tf_op jit(solution)/shard_map/ppermute | solution.py:370

commit v4 on v3

--- a/solution.py
+++ b/solution.py
@@ -15,6 +15,9 @@
 HALF = 136
 HOPS = 2
 CHUNK = 512
+TILE = 16
+DEP_US = 0.01
+PACKED_US = 100.0
 BF = jnp.bfloat16
 F32 = jnp.float32
 VM = pl.BlockSpec(memory_space=pltpu.VMEM)
@@ -74,6 +77,36 @@
     return jnp.maximum(0.0, 1.0 - jnp.abs(coord - cells))
 
 
+def hat_split(coord):
+    lanes = coord.shape[-1]
+    cell = jnp.floor(coord)
+    frac = coord - cell
+    coarse = jnp.floor(frac * 256.0) * (1.0 / 256.0)
+    fine = frac - coarse
+
+    def rows(v):
+        return jnp.broadcast_to(v, (TILE, lanes)).astype(BF)
+
+    here, there = rows(cell), rows(cell + 1.0)
+    hi = (rows(1.0 - coarse), rows(coarse))
+    lo = (rows(-fine), rows(fine))
+    zero = jnp.zeros((TILE, lanes), BF)
+    base = lax.broadcasted_iota(jnp.int32, (TILE, lanes), 0).astype(F32)
+    for start in range(0, GRID, TILE):
+        cells = (base + float(start)).astype(BF)
+        at_here = cells == here
+        at_there = cells == there
+        yield (
+            slice(start, start + TILE),
+            jnp.where(at_here, hi[0], jnp.where(at_there, hi[1], zero)),
+            jnp.where(at_here, lo[0], jnp.where(at_there, lo[1], zero)),
+        )
+
+
+def shifted(rows, by):
+    return slice(rows.start + by, rows.stop + by)
+
+
 def chip_half():
     return lax.div(lax.axis_index("dom"), 2)
 
@@ -82,81 +115,157 @@
     return lax.rem(lax.axis_index("dom"), 2)
 
 
+def cost(us):
+    return pl.CostEstimate(flops=int(us * 1e9), transcendentals=0, bytes_accessed=0)
+
+
 def params(mib):
     return pltpu.CompilerParams(vmem_limit_bytes=mib * 1024 * 1024)
 
 
-def deposit_body(sources, *refs):
-    *given, out_ref, tx, ty = refs
+def deposit_rows(rows, tx, ty):
+    for start, coords in rows:
+        for coord, table in zip(coords, (tx, ty)):
+            n = coord.shape[-1]
+            at = slice(start, start + n)
+            for cells, hi, lo in hat_split(coord):
+                table[cells, at] = hi
+                table[shifted(cells, GRID), at] = lo
+    return table_product(tx, ty)
+
+
+def table_product(tx, ty):
+    acc = lax.dot_general(
+        tx[...], ty[...], (((1,), (1,)), ((), ())), preferred_element_type=F32
+    )
+    return (acc[:GRID, :GRID] + acc[GRID:, GRID:]) + (acc[:GRID, GRID:] + acc[GRID:, :GRID])
+
+
+def deposit_body(sources, keep, *refs):
+    given = refs[: len(refs) - (4 if keep else 3)]
+    out_ref, *kept, tx, ty = refs[len(given) :]
     prev_ref = given[sources] if len(given) > sources else None
     e = 1 - chip_half()
     n = given[0].shape[-1]
     for m in range(2):
+        rows = []
         for i, ref in enumerate(given[:sources]):
-            for coord, table in ((0, tx), (1, ty)):
-                hi, lo = hilo(hat(ref[coord, e, pl.ds(m, 1), :], n))
-                table[m, 0:GRID, i * n : (i + 1) * n] = hi
-                table[m, GRID:, i * n : (i + 1) * n] = lo
-        acc = lax.dot_general(
-            tx[m], ty[m], (((1,), (1,)), ((), ())), preferred_element_type=F32
-        )
-        total = (acc[:GRID, :GRID] + acc[GRID:, GRID:]) + (acc[:GRID, GRID:] + acc[GRID:, :GRID])
+            for start in range(0, n, CHUNK):
+                at = slice(start, start + CHUNK)
+                rows.append(
+                    (i * n + start, [ref[coord, e, pl.ds(m, 1), at] for coord in range(2)])
+                )
+        total = deposit_rows(rows, tx.at[m], ty.at[m])
         if prev_ref is not None:
             total = total + prev_ref[m]
         out_ref[m] = total
-
-
-def deposit(sources, prev=None):
+    for kept_ref in kept:
+        for i, ref in enumerate(given[:sources]):
+            for coord in range(2):
+                kept_ref[i, coord] = ref[coord, e]
+
+
+def deposit(sources, prev=None, keep=True):
     n = sources[0].shape[-1]
     args = [*sources] + ([] if prev is None else [prev])
     return pl.pallas_call(
-        functools.partial(deposit_body, len(sources)),
-        out_shape=jax.ShapeDtypeStruct((2, GRID, GRID), F32),
+        functools.partial(deposit_body, len(sources), keep),
+        out_shape=[
+            jax.ShapeDtypeStruct((2, GRID, GRID), F32),
+            jax.ShapeDtypeStruct((len(sources), 2, 2, n), F32),
+        ][: 1 + keep],
         in_specs=[VM] * len(args),
-        out_specs=VM,
+        out_specs=[VM] * (1 + keep),
         scratch_shapes=[pltpu.VMEM((2, 2 * GRID, len(sources) * n), BF)] * 2,
         compiler_params=params(16),
+        cost_estimate=cost(DEP_US),
         name="deposit",
     )(*args)
 
 
-def prepare_body(
-    pc_ref, py_ref, pyc_ref, pa_hbm, kernel_hbm, partners_hbm, offsets_hbm, counts_hbm,
-    half_ref, wx_ref, wy_ref, slots_ref,
-    pa_ref, kernel_ref, partners_ref, offsets_ref, counts_ref, sems,
+def pack_body(near_ref, y_ref, yc_ref, out_ref):
+    e = 1 - chip_half()
+    out_ref[0] = near_ref[0]
+    out_ref[1] = near_ref[1]
+    out_ref[2] = y_ref[0]
+    for coord in range(2):
+        out_ref[3, coord] = yc_ref[coord, e]
+
+
+def pack(near, y, yc):
+    return pl.pallas_call(
+        pack_body,
+        out_shape=jax.ShapeDtypeStruct((4, *near.shape[1:]), F32),
+        in_specs=[VM] * 3,
+        out_specs=VM,
+        compiler_params=params(4),
+        name="pack",
+    )(near, y, yc)
+
+
+def deposit_packed_body(pos_ref, out_ref, tx, ty):
+    sources, _, members, n = pos_ref.shape
+    for m in range(members):
+        rows = []
+        for i in range(sources):
+            for start in range(0, n, CHUNK):
+                at = slice(start, start + CHUNK)
+                rows.append(
+                    (i * n + start, [pos_ref[i, coord, m : m + 1, at] for coord in range(2)])
+                )
+        out_ref[m] = deposit_rows(rows, tx.at[m], ty.at[m])
+
+
+def deposit_packed(pos):
+    return pl.pallas_call(
+        deposit_packed_body,
+        out_shape=jax.ShapeDtypeStruct((2, GRID, GRID), F32),
+        in_specs=[VM],
+        out_specs=VM,
+        scratch_shapes=[pltpu.VMEM((2, 2 * GRID, pos.shape[0] * pos.shape[-1]), BF)] * 2,
+        compiler_params=params(20),
+        cost_estimate=cost(PACKED_US),
+        name="deposit_packed",
+    )(pos)
+
+
+def first_body(
+    pc_ref, pa_hbm, kernel_hbm, partners_hbm, offsets_hbm, counts_hbm,
+    out_ref, kept_ref, pa_ref, half_ref, slots_ref,
+    tx, ty, kernel_ref, partners_ref, offsets_ref, counts_ref, sems,
 ):
-    small = [
-        pltpu.make_async_copy(src, dst, sems.at[i + 2])
+    copies = [
+        pltpu.make_async_copy(src, dst, sems.at[i])
         for i, (src, dst) in enumerate((
-            (partners_hbm, partners_ref), (offsets_hbm, offsets_ref), (counts_hbm, counts_ref)
+            (pa_hbm, pa_ref), (kernel_hbm, kernel_ref), (partners_hbm, partners_ref),
+            (offsets_hbm, offsets_ref), (counts_hbm, counts_ref),
         ))
     ]
-    for copy in small:
+    for copy in copies:
         copy.start()
-    own_copy = pltpu.make_async_copy(pa_hbm, pa_ref, sems.at[0])
-    kernel_copy = pltpu.make_async_copy(kernel_hbm, kernel_ref, sems.at[1])
-    own_copy.start()
-    kernel_copy.start()
     h = chip_half()
     c = core()
-    n = pa_ref.shape[-1]
-    chunk = 512
-    for i, ref in ((1, pc_ref), (2, py_ref), (3, pyc_ref), (0, pa_ref)):
+    e = 1 - h
+    n = pc_ref.shape[-1]
+    for i, ref in ((1, pc_ref), (0, pa_ref)):
         if i == 0:
-            own_copy.wait()
-        for start in range(0, n, chunk):
-            at = slice(i * n + start, i * n + start + chunk)
-            both = ref[0, h, :, start : start + chunk]
-            wx_ref[:, at] = hat(jnp.where(c == 0, both[0:1], both[1:2]), chunk)
-            both = ref[1, h, :, start : start + chunk]
-            hi, lo = hilo(hat(jnp.where(c == 0, both[0:1], both[1:2]), chunk))
-            wy_ref[0:GRID, at] = hi
-            wy_ref[GRID : 2 * GRID, at] = hi
-            wy_ref[2 * GRID :, at] = lo
+            copies[0].wait()
+        for m in range(2):
+            for start in range(0, n, CHUNK):
+                at = slice(i * n + start, i * n + start + CHUNK)
+                for coord, table in ((0, tx), (1, ty)):
+                    row = ref[coord, e, pl.ds(m, 1), start : start + CHUNK]
+                    for cells, hi, lo in hat_split(row):
+                        table[m, cells, at] = hi
+                        table[m, shifted(cells, GRID), at] = lo
+        for coord in range(2):
+            kept_ref[i, coord] = ref[coord, e]
+    for m in range(2):
+        out_ref[m] = table_product(tx.at[m], ty.at[m])
     row = lax.broadcasted_iota(jnp.int32, (PAD, PAD), 0)
     col = lax.broadcasted_iota(jnp.int32, (PAD, PAD), 1)
     flip = jnp.where(((row + col) & (PAD - 1)) == 0, 1.0, 0.0).astype(BF)
-    kernel_copy.wait()
+    copies[1].wait()
     for comp in range(2):
         for part in range(2):
             whole = kernel_ref[comp, part]
@@ -168,7 +277,7 @@
                 half_ref[comp, part] = 0.5 * (whole[:HALF] + turned)
             else:
                 half_ref[comp, part] = 0.5 * (whole[:HALF] - turned)
-    for copy in small:
+    for copy in copies[2:]:
         copy.wait()
     b = lax.axis_index("bunch")
     ndev = lax.axis_size("bunch")
@@ -183,28 +292,44 @@
         slots_ref[s : s + 1, :] = jnp.full((1, 128), code, jnp.int32)
 
 
-def prepare(places, kernel_hat, partners, offsets, counts):
-    n = 4 * places[0].shape[-1]
+def first_deposit(positions, pos_c, kernel_hat, partners, offsets, counts):
+    n = positions.shape[-1]
     small = (partners, offsets, counts)
     return pl.pallas_call(
-        prepare_body,
+        first_body,
         out_shape=[
+            jax.ShapeDtypeStruct((2, GRID, GRID), F32),
+            jax.ShapeDtypeStruct((2, 2, 2, n), F32),
+            jax.ShapeDtypeStruct(positions.shape, F32),
             jax.ShapeDtypeStruct((2, 2, HALF, PAD), F32),
-            jax.ShapeDtypeStruct((GRID, n), F32),
-            jax.ShapeDtypeStruct((3 * GRID, n), BF),
             jax.ShapeDtypeStruct((partners.shape[-1], 128), jnp.int32),
         ],
-        in_specs=[VM] * 3 + [HBM] * 5,
-        out_specs=[VM] * 4,
+        in_specs=[VM] + [HBM] * 5,
+        out_specs=[VM] * 5,
         scratch_shapes=[
-            pltpu.VMEM(places[0].shape, F32),
+            *[pltpu.VMEM((2, 2 * GRID, 2 * n), BF)] * 2,
             pltpu.VMEM(kernel_hat.shape, F32),
             *[pltpu.SMEM(t.shape, jnp.int32) for t in small],
             pltpu.SemaphoreType.DMA((5,)),
         ],
         compiler_params=params(16),
-        name="prepare",
-    )(*places[1:], *[in_hbm(t) for t in (places[0], kernel_hat, *small)])
+        name="first_deposit",
+    )(pos_c, *[in_hbm(t) for t in (positions, kernel_hat, *small)])
+
+
+def kick_tables(ref, start, lanes, wx_ref, wy_ref, to):
+    h = chip_half()
+    c = core()
+    rows = []
+    for coord in range(2):
+        both = ref[coord, h, :, start : start + lanes]
+        rows.append(jnp.where(c == 0, both[0:1], both[1:2]))
+    at = slice(to, to + lanes)
+    wx_ref[:, at] = hat(rows[0], lanes)
+    for cells, hi, lo in hat_split(rows[1]):
+        wy_ref[cells, at] = hi
+        wy_ref[shifted(cells, GRID), at] = hi
+        wy_ref[shifted(cells, 2 * GRID), at] = lo
 
 
 def kick_of(maps, wx, wy):
@@ -217,9 +342,9 @@
 def field_body(
     own_ref, r1_ref, r2_ref, s1_ref, s2_ref,
     rows_hbm, cols_hbm, bcols_hbm, brows_hbm,
-    half_ref, wx_ref, wy_ref, slots_ref,
+    half_ref, slots_ref, pyc_ref,
     maps_ref, out_ref,
-    grids, source, rows_ref, cols_ref, bcols_ref, brows_ref, sems,
+    wx_ref, wy_ref, grids, source, rows_ref, cols_ref, bcols_ref, brows_ref, sems,
 ):
     c = core()
     fixed = [
@@ -232,6 +357,9 @@
     for copy in fixed:
         copy.start()
     slots = slots_ref[...]
+    n = out_ref.shape[-1]
+    for start in range(0, n, CHUNK):
+        kick_tables(pyc_ref, start, CHUNK, wx_ref, wy_ref, start)
     places = (2, 1 + 2 * c, 4 * c, 3 - 2 * c, 4 - 4 * c)
     for ref, place in zip((own_ref, r1_ref, r2_ref, s1_ref, s2_ref), places):
         grids[2 * place] = ref[0]
@@ -276,16 +404,15 @@
     hi, lo = hilo(field)
     maps = jnp.concatenate([hi, lo, hi], 1)
     maps_ref[...] = maps
-    n = out_ref.shape[-1]
     for start in range(0, n, CHUNK):
-        at = slice(3 * n + start, 3 * n + start + CHUNK)
+        at = slice(start, start + CHUNK)
         kx, ky = kick_of(maps, wx_ref[:, at], wy_ref[:, at])
         out_ref[0:1, start : start + CHUNK] = kx
         out_ref[1:2, start : start + CHUNK] = ky
 
 
-def field(grids, prepared):
-    n = prepared[1].shape[-1] // 4
+def field(grids, half, slots, pos_yc):
+    n = pos_yc.shape[-1]
     tables = [jnp.asarray(t) for t in dft_tables()]
     return pl.pallas_call(
         field_body,
@@ -293,9 +420,11 @@
             jax.ShapeDtypeStruct((2 * GRID, 3 * GRID), BF),
             jax.ShapeDtypeStruct((2, n), F32),
         ],
-        in_specs=[VM] * 5 + [HBM] * 4 + [VM] * 4,
+        in_specs=[VM] * 5 + [HBM] * 4 + [VM] * 3,
         out_specs=[VM] * 2,
         scratch_shapes=[
+            pltpu.VMEM((GRID, n), F32),
+            pltpu.VMEM((3 * GRID, n), BF),
             pltpu.VMEM((4 * HOPS + 2, GRID, GRID), F32),
             pltpu.VMEM((2, SPAN + 8, GRID), F32),
             *[pltpu.VMEM(t.shape, BF) for t in tables],
@@ -303,34 +432,37 @@
         ],
         compiler_params=params(24),
         name="field",
-    )(*grids, *[in_hbm(t) for t in tables], *prepared)
-
-
-def kick_body(maps_ref, wx_ref, wy_ref, near_ref, far_ref):
+    )(*grids, *[in_hbm(t) for t in tables], half, slots, pos_yc)
+
+
+def kick_body(maps_ref, pa_ref, pc_ref, py_ref, near_ref, far_ref, wx_ref, wy_ref):
     maps = maps_ref[...]
     n = far_ref.shape[-1]
-    for start in range(0, 3 * n, CHUNK):
-        at = slice(start, start + CHUNK)
-        kx, ky = kick_of(maps, wx_ref[:, at], wy_ref[:, at])
-        to = slice(start % n, start % n + CHUNK)
-        if start < 2 * n:
-            near_ref[start // n, 0:1, to] = kx
-            near_ref[start // n, 1:2, to] = ky
-        else:
-            far_ref[0:1, to] = kx
-            far_ref[1:2, to] = ky
-
-
-def kick(maps, wx, wy):
-    n = wx.shape[-1] // 4
+    for i, ref in enumerate((pa_ref, pc_ref, py_ref)):
+        for start in range(0, n, CHUNK):
+            at = slice(i * n + start, i * n + start + CHUNK)
+            kick_tables(ref, start, CHUNK, wx_ref, wy_ref, i * n + start)
+            kx, ky = kick_of(maps, wx_ref[:, at], wy_ref[:, at])
+            to = slice(start, start + CHUNK)
+            if i < 2:
+                near_ref[i, 0:1, to] = kx
+                near_ref[i, 1:2, to] = ky
+            else:
+                far_ref[0:1, to] = kx
+                far_ref[1:2, to] = ky
+
+
+def kick(maps, places):
+    n = places[0].shape[-1]
     return pl.pallas_call(
         kick_body,
         out_shape=[jax.ShapeDtypeStruct((2, 2, n), F32), jax.ShapeDtypeStruct((2, n), F32)],
-        in_specs=[VM] * 3,
+        in_specs=[VM] * 4,
         out_specs=[VM] * 2,
+        scratch_shapes=[pltpu.VMEM((GRID, 3 * n), F32), pltpu.VMEM((3 * GRID, 3 * n), BF)],
         compiler_params=params(8),
         name="kick",
-    )(maps, wx, wy)
+    )(maps, *places)
 
 
 def finish_body(mine_ref, core_ref, chip_ref, momenta_ref, out_ref):
@@ -382,22 +514,23 @@
 
     pos_y = across_chips(positions)
     pos_c = across_cores(positions)
-    first = deposit([positions, pos_c])
+    first, near, pos_own, half, slots = first_deposit(
+        positions, pos_c, kernel_hat, partners, offsets, counts
+    )
     pos_y, first = lax.optimization_barrier((pos_y, first))
     pos_yc = across_cores(pos_y)
-    second = deposit([pos_y], first)
-    own = deposit([pos_yc], second)
-    own, pos_yc = lax.optimization_barrier((own, pos_yc))
+    second, kept_y = deposit([pos_y], first)
+    message = pack(near, kept_y, pos_yc)
+    p2 = along_blocks(message, 2)
+    (own,) = deposit([pos_yc], second, False)
     r1 = along_blocks(own, 1)
-    r2 = along_blocks(own, 2)
-    prepared = prepare((positions, pos_c, pos_y, pos_yc), kernel_hat, partners, offsets, counts)
-    r1, prepared = lax.optimization_barrier((r1, prepared))
+    r2 = deposit_packed(p2)
+    r1, r2 = lax.optimization_barrier((r1, r2))
+    s2 = across_cores(r2)
     s1 = across_cores(r1)
-    r2, s1 = lax.optimization_barrier((r2, s1))
-    s2 = across_cores(r2)
-    maps, diagonal = field((own, r1, r2, s1, s2), prepared)
+    maps, diagonal = field((own, r1, r2, s1, s2), half, slots, pos_yc)
     from_core_far = across_cores(diagonal)
-    near, far = kick(maps, prepared[1], prepared[2])
+    near, far = kick(maps, (pos_own, pos_c, pos_y))
     message, mine = lax.optimization_barrier((jnp.stack([far, from_core_far]), near))
     from_chip = across_chips(message)
     from_core = across_cores(mine)

time: 33.7 us -> 32.7 us (0.970)
  waiting for transfers between devices: 5.56 us -> 4.72 us
  local copies, waits for them, and re-layouts: 0.79 us -> 0.01 us
  Pallas kernels: 9.24 us -> 9.96 us
    unnamed x4 -> x2, local copies, waits for them, and re-layouts: 0.79 us -> 0.01 us
    pallas_call x4 -> x5, Pallas kernels: 4.41 us -> 5.08 us  [the longest x1 2.38 us: first_deposit(): pl.pallas_call(first_body, out_shape=[jax.ShapeDtypeStruct((2, GRID, GRID...]
    ppermute x2, starting transfers between devices: 7.64 us -> 8.25 us  [along_blocks(): return lax.ppermute(x, ('bunch', 'dom'), pairs)]
    ppermute x6, starting transfers between devices: 6.28 us -> 5.68 us  [across_cores(): return lax.ppermute(x, 'dom', [(i, i ^ 1) for i in range(doms)])]
    ppermute x2, waiting for transfers between devices: 1.75 us -> 1.36 us  [along_blocks(): return lax.ppermute(x, ('bunch', 'dom'), pairs)]
    ppermute x2, waiting for transfers between devices: 2.23 us -> 1.88 us  [across_chips(): return lax.ppermute(x, 'dom', [(i, i ^ 2) for i in range(doms)])]
  transfers between devices with their start and end apart: 10 -> 10, of which waited for: 5 -> 6; matrix products, arithmetic and copies ran while one was open for 0% -> 0% of each run, Pallas kernels for 14% -> 19%
where the time goes in v4:
time: 32.7 us; the launch traced here: 32.6 us
  starting transfers between devices  17.8 us (54%)
  Pallas kernels  9.96 us (30%)
  waiting for transfers between devices  4.72 us (14%)
    ppermute x2, starting transfers between devices, along_blocks(): return lax.ppermute(x, ('bunch', 'dom'), pairs)  8.25 us
    ppermute x6, starting transfers between devices, across_cores(): return lax.ppermute(x, 'dom', [(i, i ^ 1) for i in range(doms)])  5.68 us
    ppermute x2, starting transfers between devices, across_chips(): return lax.ppermute(x, 'dom', [(i, i ^ 2) for i in range(doms)])  3.88 us
    pallas_call x1, Pallas kernels, field(): pl.pallas_call(field_body, out_shape=[jax.ShapeDtypeStruct((2 * GRID, 3 *...  3.2 us
    pallas_call x1, Pallas kernels, first_deposit(): pl.pallas_call(first_body, out_shape=[jax.ShapeDtypeStruct((2, GRID, GRID...  2.38 us
    ppermute x2, waiting for transfers between devices, across_chips(): return lax.ppermute(x, 'dom', [(i, i ^ 2) for i in range(doms)])  1.88 us
    pallas_call x1, Pallas kernels, deposit_packed(): pl.pallas_call(deposit_packed_body, out_shape=jax.ShapeDtypeStruct((2, GR...  1.59 us
    ppermute x6, waiting for transfers between devices, across_cores(): return lax.ppermute(x, 'dom', [(i, i ^ 1) for i in range(doms)])  1.48 us
  transfers between devices with their start and end apart: 10, of which 6 were waited for; matrix products, arithmetic and copies ran while one was open for 0% of the time, Pallas kernels for 19%

profile of v4, /device:TPU:1, one launch (start us, length us, event | category | flops | bytes accessed | tf_op | source)
XLA Modules:
  0.0 32.6 jit_solution(13590938737608250861)
XLA Ops:
  0.0 3.2 %collective-permute-start.1 = (f32[2,2,2,1024]{3,2,1,0:T(2,128)}, f32[2,2,2,1024]{3,2,1,0:T(2,128)S(1)}, u32[]{:S(2)}, u32[]{:S(2)}) collective-permute-start(f32[2,2,2,1024]{3,2,1,0:T(2,128)} %pa_hbm.1), channel_id=1, source_target_pairs={{0,1},{1,0},{2,3},{3,2},{4,5},{5,4},{6,7},{7,6},{8,9},{9,8},{10,11... | collective-permute-start | bytes 98312 | tf_op jit(solution)/shard_map/ppermute | solution.py:502
  3.2 1.2 %collective-permute-start = (f32[2,2,2,1024]{3,2,1,0:T(2,128)}, f32[2,2,2,1024]{3,2,1,0:T(2,128)S(1)}, u32[]{:S(2)}, u32[]{:S(2)}) collective-permute-start(f32[2,2,2,1024]{3,2,1,0:T(2,128)} %pa_hbm.1), channel_id=1, source_target_pairs={{0,2},{1,3},{2,0},{3,1},{4,6},{5,7},{6,4},{7,5},{8,10},{9,11},{10,... | collective-permute-start | bytes 98312 | tf_op jit(solution)/shard_map/ppermute | solution.py:505
  4.4 0.0 collective-permute-done.1.pc_ref
  4.4 2.4 %first_deposit.1 = (f32[2,128,128]{2,1,0:T(8,128)S(1)}, f32[2,2,2,1024]{3,2,1,0:T(2,128)S(1)}, f32[2,2,2,1024]{3,2,1,0:T(2,128)S(1)}, f32[2,2,136,256]{3,2,1,0:T(8,128)S(1)}, s32[16,128]{1,0:T(8,128)S(1)}) custom-call(f32[2,2,2,1024]{3,2,1,0:T(2,128)S(1)} %collective-permute-done.1.pc_ref, f32[2,2,2,1024]{3,2,1,0:T(2,128)} %pa_hbm.1, ...), custom_call_target="tpu_custom_call" | custom-call | tf_op jit(solution)/shard_map/first_deposit/pallas_call | solution.py:298
  6.8 0.9 %collective-permute-done.refs_0_.py_ref = f32[2,2,2,1024]{3,2,1,0:T(2,128)S(1)} collective-permute-done((f32[2,2,2,1024]{3,2,1,0:T(2,128)}, f32[2,2,2,1024]{3,2,1,0:T(2,128)S(1)}, u32[]{:S(2)}, u32[]{:S(2)}) %collective-permute-start) | collective-permute-done | bytes 32800 | tf_op jit(solution)/shard_map/ppermute | solution.py:505
  7.7 1.2 %collective-permute-start.2 = (f32[2,2,2,1024]{3,2,1,0:T(2,128)S(1)}, f32[2,2,2,1024]{3,2,1,0:T(2,128)S(1)}, u32[]{:S(2)}, u32[]{:S(2)}) collective-permute-start(f32[2,2,2,1024]{3,2,1,0:T(2,128)S(1)} %collective-permute-done.refs_0_.py_ref), channel_id=1, source_target_pairs={{0,1},{1,0},{2,3},{3,2},{4,5},{5,4},{6,7},{7,6},{8,9},{9,8},{10,11... | collective-permute-start | bytes 98312 | tf_op jit(solution)/shard_map/ppermute | solution.py:502
  8.9 0.5 %deposit.2 = (f32[2,128,128]{2,1,0:T(8,128)S(1)}, f32[1,2,2,1024]{3,2,1,0:T(2,128)S(1)}) custom-call(f32[2,2,2,1024]{3,2,1,0:T(2,128)S(1)} %collective-permute-done.refs_0_.py_ref, f32[2,128,128]{2,1,0:T(8,128)S(1)} %get-tuple-element.24.refs_1_), custom_call_target="tpu_custom_call" | custom-call | flops 10000000 | tf_op jit(solution)/shard_map/deposit/pallas_call | solution.py:171
  9.4 0.3 collective-permute-done.2.refs_0_.yc_ref.pyc_ref
  9.7 7.3 %collective-permute-start.4 = (f32[4,2,2,1024]{3,2,1,0:T(2,128)S(1)}, f32[4,2,2,1024]{3,2,1,0:T(2,128)S(1)}, u32[]{:S(2)}, u32[]{:S(2)}) collective-permute-start(f32[4,2,2,1024]{3,2,1,0:T(2,128)S(1)} %pack.1), channel_id=1, source_target_pairs={{0,8},{1,249},{2,10},{3,251},{4,12},{5,253},{6,14},{7,255},{8,16},... | collective-permute-start | bytes 196616 | tf_op jit(solution)/shard_map/ppermute | solution.py:513
  17.1 0.6 %deposit.3.own_ref = f32[2,128,128]{2,1,0:T(8,128)S(1)} custom-call(f32[2,2,2,1024]{3,2,1,0:T(2,128)S(1)} %collective-permute-done.2.refs_0_.yc_ref.pyc_ref, f32[2,128,128]{2,1,0:T(8,128)S(1)} %get-tuple-element.25.refs_1_), custom_call_target="tpu_custom_call" | custom-call | flops 10000000 | tf_op jit(solution)/shard_map/deposit/pallas_call | solution.py:171
  17.6 0.9 %collective-permute-start.3 = (f32[2,128,128]{2,1,0:T(8,128)S(1)}, f32[2,128,128]{2,1,0:T(8,128)S(1)}, u32[]{:S(2)}, u32[]{:S(2)}) collective-permute-start(f32[2,128,128]{2,1,0:T(8,128)S(1)} %deposit.3.own_ref), channel_id=1, source_target_pairs={{0,4},{1,253},{2,6},{3,255},{4,8},{5,1},{6,10},{7,3},{8,12},{9,5},... | collective-permute-start | bytes 393224 | tf_op jit(solution)/shard_map/ppermute | solution.py:513
  18.6 0.0 collective-permute-done.4.pos_ref
  18.6 1.6 %deposit_packed.1.r2_ref = f32[2,128,128]{2,1,0:T(8,128)S(1)} custom-call(f32[4,2,2,1024]{3,2,1,0:T(2,128)S(1)} %collective-permute-done.4.pos_ref), custom_call_target="tpu_custom_call" | custom-call | flops 99999997952 | tf_op jit(solution)/shard_map/deposit_packed/pallas_call | solution.py:220
  20.2 1.4 %collective-permute-done.3.r1_ref = f32[2,128,128]{2,1,0:T(8,128)S(1)} collective-permute-done((f32[2,128,128]{2,1,0:T(8,128)S(1)}, f32[2,128,128]{2,1,0:T(8,128)S(1)}, u32[]{:S(2)}, u32[]{:S(2)}) %collective-permute-start.3) | collective-permute-done | bytes 131104 | tf_op jit(solution)/shard_map/ppermute | solution.py:513
  21.5 0.3 collective-permute-start.5
  21.8 0.2 collective-permute-start.6
  22.0 0.8 %collective-permute-done.5.s1_ref = f32[2,128,128]{2,1,0:T(8,128)S(1)} collective-permute-done((f32[2,128,128]{2,1,0:T(8,128)S(1)}, f32[2,128,128]{2,1,0:T(8,128)S(1)}, u32[]{:S(2)}, u32[]{:S(2)}) %collective-permute-start.5) | collective-permute-done | bytes 131104 | tf_op jit(solution)/shard_map/ppermute | solution.py:502
  22.9 0.3 collective-permute-done.6.s2_ref
  23.2 3.2 %field.1 = (bf16[256,384]{1,0:T(8,128)(2,1)S(1)}, f32[2,1024]{1,0:T(2,128)S(1)}) custom-call(f32[2,128,128]{2,1,0:T(8,128)S(1)} %deposit.3.own_ref, f32[2,128,128]{2,1,0:T(8,128)S(1)} %collective-permute-done.3.r1_ref, f32[2,128,128]{2,1,0:T(8,128)S(1)} %deposit_packed.1.r2_ref, f32[2,128,128]{2,1,0:T(8,128)S(1)} %collective-permute-done.5.s1_ref, ...), custom_call_target="tpu_custom_call" | custom-call | tf_op jit(solution)/shard_map/field/pallas_call | solution.py:417
  26.4 0.3 collective-permute-start.7
  26.7 1.0 %kick.1 = (f32[2,2,1024]{2,1,0:T(2,128)S(1)}, f32[2,1024]{1,0:T(2,128)S(1)}) custom-call(bf16[256,384]{1,0:T(8,128)(2,1)S(1)} %get-tuple-element.32.maps_ref, f32[2,2,2,1024]{3,2,1,0:T(2,128)S(1)} %get-tuple-element.33.pa_ref, f32[2,2,2,1024]{3,2,1,0:T(2,128)S(1)} %collective-permute-done.1.pc_ref, f32[2,2,2,1024]{3,2,1,0:T(2,128)S(1)} %collective-permute-done.refs_0_.py_ref), custom_call_target="tpu_custom_call" | custom-call | tf_op jit(solution)/shard_map/kick/pallas_call | solution.py:457
  27.7 0.0 copy-start
  27.7 0.0 collective-permute-done.7
  27.7 2.7 %collective-permute-start.9 = (f32[2,2,1024]{2,1,0:T(2,128)S(1)}, f32[2,2,1024]{2,1,0:T(2,128)S(1)}, u32[]{:S(2)}, u32[]{:S(2)}) collective-permute-start(f32[2,2,1024]{2,1,0:T(2,128)S(1)} %pad_maximum_fusion), channel_id=1, source_target_pairs={{0,2},{1,3},{2,0},{3,1},{4,6},{5,7},{6,4},{7,5},{8,10},{9,11},{10,... | collective-permute-start | bytes 49160 | tf_op jit(solution)/shard_map/ppermute | solution.py:505
  30.5 0.5 %collective-permute-start.8 = (f32[2,2,1024]{2,1,0:T(2,128)S(1)}, f32[2,2,1024]{2,1,0:T(2,128)S(1)}, u32[]{:S(2)}, u32[]{:S(2)}) collective-permute-start(f32[2,2,1024]{2,1,0:T(2,128)S(1)} %get-tuple-element.37.mine_ref), channel_id=1, source_target_pairs={{0,1},{1,0},{2,3},{3,2},{4,5},{5,4},{6,7},{7,6},{8,9},{9,8},{10,11... | collective-permute-start | bytes 49160 | tf_op jit(solution)/shard_map/ppermute | solution.py:502
  31.0 1.0 %collective-permute-done.9.chip_ref = f32[2,2,1024]{2,1,0:T(2,128)S(1)} collective-permute-done((f32[2,2,1024]{2,1,0:T(2,128)S(1)}, f32[2,2,1024]{2,1,0:T(2,128)S(1)}, u32[]{:S(2)}, u32[]{:S(2)}) %collective-permute-start.9) | collective-permute-done | bytes 16416 | tf_op jit(solution)/shard_map/ppermute | solution.py:505
  31.9 0.0 collective-permute-done.8.core_ref
  31.9 0.0 copy-done
  31.9 0.6 %finish.1 = f32[2,2,2,1024]{3,2,1,0:T(2,128)} custom-call(f32[2,2,1024]{2,1,0:T(2,128)S(1)} %get-tuple-element.37.mine_ref, f32[2,2,1024]{2,1,0:T(2,128)S(1)} %collective-permute-done.8.core_ref, f32[2,2,1024]{2,1,0:T(2,128)S(1)} %collective-permute-done.9.chip_ref, f32[2,2,2,1024]{3,2,1,0:T(2,128)S(1)} %copy-done), custom_call_target="tpu_custom_call" | custom-call | tf_op jit(solution)/shard_map/finish/pallas_call | solution.py:487
  (2 shorter events, 0.0 us)
Async XLA Ops:
  0.0 4.4 %collective-permute-start.1 = (f32[2,2,2,1024]{3,2,1,0:T(2,128)}, f32[2,2,2,1024]{3,2,1,0:T(2,128)S(1)}, u32[]{:S(2)}, u32[]{:S(2)}) collective-permute-start(f32[2,2,2,1024]{3,2,1,0:T(2,128)} %pa_hbm.1), channel_id=1, source_target_pairs={{0,1},{1,0},{2,3},{3,2},{4,5},{5,4},{6,7},{7,6},{8,9},{9,8},{10,11... | collective-permute-start | bytes 98312 | tf_op jit(solution)/shard_map/ppermute | solution.py:502
  3.2 4.5 %collective-permute-start = (f32[2,2,2,1024]{3,2,1,0:T(2,128)}, f32[2,2,2,1024]{3,2,1,0:T(2,128)S(1)}, u32[]{:S(2)}, u32[]{:S(2)}) collective-permute-start(f32[2,2,2,1024]{3,2,1,0:T(2,128)} %pa_hbm.1), channel_id=1, source_target_pairs={{0,2},{1,3},{2,0},{3,1},{4,6},{5,7},{6,4},{7,5},{8,10},{9,11},{10,... | collective-permute-start | bytes 98312 | tf_op jit(solution)/shard_map/ppermute | solution.py:505
  7.7 2.0 %collective-permute-start.2 = (f32[2,2,2,1024]{3,2,1,0:T(2,128)S(1)}, f32[2,2,2,1024]{3,2,1,0:T(2,128)S(1)}, u32[]{:S(2)}, u32[]{:S(2)}) collective-permute-start(f32[2,2,2,1024]{3,2,1,0:T(2,128)S(1)} %collective-permute-done.refs_0_.py_ref), channel_id=1, source_target_pairs={{0,1},{1,0},{2,3},{3,2},{4,5},{5,4},{6,7},{7,6},{8,9},{9,8},{10,11... | collective-permute-start | bytes 98312 | tf_op jit(solution)/shard_map/ppermute | solution.py:502
  9.7 8.8 %collective-permute-start.4 = (f32[4,2,2,1024]{3,2,1,0:T(2,128)S(1)}, f32[4,2,2,1024]{3,2,1,0:T(2,128)S(1)}, u32[]{:S(2)}, u32[]{:S(2)}) collective-permute-start(f32[4,2,2,1024]{3,2,1,0:T(2,128)S(1)} %pack.1), channel_id=1, source_target_pairs={{0,8},{1,249},{2,10},{3,251},{4,12},{5,253},{6,14},{7,255},{8,16},... | collective-permute-start | bytes 196616 | tf_op jit(solution)/shard_map/ppermute | solution.py:513
  17.6 3.9 %collective-permute-start.3 = (f32[2,128,128]{2,1,0:T(8,128)S(1)}, f32[2,128,128]{2,1,0:T(8,128)S(1)}, u32[]{:S(2)}, u32[]{:S(2)}) collective-permute-start(f32[2,128,128]{2,1,0:T(8,128)S(1)} %deposit.3.own_ref), channel_id=1, source_target_pairs={{0,4},{1,253},{2,6},{3,255},{4,8},{5,1},{6,10},{7,3},{8,12},{9,5},... | collective-permute-start | bytes 393224 | tf_op jit(solution)/shard_map/ppermute | solution.py:513
  21.5 1.3 %collective-permute-start.5 = (f32[2,128,128]{2,1,0:T(8,128)S(1)}, f32[2,128,128]{2,1,0:T(8,128)S(1)}, u32[]{:S(2)}, u32[]{:S(2)}) collective-permute-start(f32[2,128,128]{2,1,0:T(8,128)S(1)} %collective-permute-done.3.r1_ref), channel_id=1, source_target_pairs={{0,1},{1,0},{2,3},{3,2},{4,5},{5,4},{6,7},{7,6},{8,9},{9,8},{10,11... | collective-permute-start | bytes 393224 | tf_op jit(solution)/shard_map/ppermute | solution.py:502
  21.8 1.3 %collective-permute-start.6 = (f32[2,128,128]{2,1,0:T(8,128)S(1)}, f32[2,128,128]{2,1,0:T(8,128)S(1)}, u32[]{:S(2)}, u32[]{:S(2)}) collective-permute-start(f32[2,128,128]{2,1,0:T(8,128)S(1)} %deposit_packed.1.r2_ref), channel_id=1, source_target_pairs={{0,1},{1,0},{2,3},{3,2},{4,5},{5,4},{6,7},{7,6},{8,9},{9,8},{10,11... | collective-permute-start | bytes 393224 | tf_op jit(solution)/shard_map/ppermute | solution.py:502
  26.4 1.3 %collective-permute-start.7 = (f32[2,1024]{1,0:T(2,128)S(1)}, f32[2,1024]{1,0:T(2,128)S(1)}, u32[]{:S(2)}, u32[]{:S(2)}) collective-permute-start(f32[2,1024]{1,0:T(2,128)S(1)} %get-tuple-element.35), channel_id=1, source_target_pairs={{0,1},{1,0},{2,3},{3,2},{4,5},{5,4},{6,7},{7,6},{8,9},{9,8},{10,11... | collective-permute-start | bytes 24584 | tf_op jit(solution)/shard_map/ppermute | solution.py:502
  27.7 4.2 %copy-start = (f32[2,2,2,1024]{3,2,1,0:T(2,128)S(1)}, f32[2,2,2,1024]{3,2,1,0:T(2,128)}, u32[]{:S(2)}) copy-start(f32[2,2,2,1024]{3,2,1,0:T(2,128)} %momenta_ref.1) | copy-start | bytes 98308
  27.7 4.2 %collective-permute-start.9 = (f32[2,2,1024]{2,1,0:T(2,128)S(1)}, f32[2,2,1024]{2,1,0:T(2,128)S(1)}, u32[]{:S(2)}, u32[]{:S(2)}) collective-permute-start(f32[2,2,1024]{2,1,0:T(2,128)S(1)} %pad_maximum_fusion), channel_id=1, source_target_pairs={{0,2},{1,3},{2,0},{3,1},{4,6},{5,7},{6,4},{7,5},{8,10},{9,11},{10,... | collective-permute-start | bytes 49160 | tf_op jit(solution)/shard_map/ppermute | solution.py:505
  30.5 1.5 %collective-permute-start.8 = (f32[2,2,1024]{2,1,0:T(2,128)S(1)}, f32[2,2,1024]{2,1,0:T(2,128)S(1)}, u32[]{:S(2)}, u32[]{:S(2)}) collective-permute-start(f32[2,2,1024]{2,1,0:T(2,128)S(1)} %get-tuple-element.37.mine_ref), channel_id=1, source_target_pairs={{0,1},{1,0},{2,3},{3,2},{4,5},{5,4},{6,7},{7,6},{8,9},{9,8},{10,11... | collective-permute-start | bytes 49160 | tf_op jit(solution)/shard_map/ppermute | solution.py:502

commit v5 on v4

--- a/solution.py
+++ b/solution.py
@@ -231,14 +231,16 @@
 
 def first_body(
     pc_ref, pa_hbm, kernel_hbm, partners_hbm, offsets_hbm, counts_hbm,
-    out_ref, kept_ref, pa_ref, half_ref, slots_ref,
+    rows_hbm, cols_hbm, bcols_hbm, brows_hbm,
+    out_ref, kept_ref, pa_ref, half_ref, slots_ref, rows_ref, cols_ref, bcols_ref, brows_ref,
     tx, ty, kernel_ref, partners_ref, offsets_ref, counts_ref, sems,
 ):
     copies = [
         pltpu.make_async_copy(src, dst, sems.at[i])
         for i, (src, dst) in enumerate((
             (pa_hbm, pa_ref), (kernel_hbm, kernel_ref), (partners_hbm, partners_ref),
-            (offsets_hbm, offsets_ref), (counts_hbm, counts_ref),
+            (offsets_hbm, offsets_ref), (counts_hbm, counts_ref), (rows_hbm, rows_ref),
+            (cols_hbm, cols_ref), (bcols_hbm, bcols_ref), (brows_hbm, brows_ref),
         ))
     ]
     for copy in copies:
@@ -295,6 +297,7 @@
 def first_deposit(positions, pos_c, kernel_hat, partners, offsets, counts):
     n = positions.shape[-1]
     small = (partners, offsets, counts)
+    tables = [jnp.asarray(t) for t in dft_tables()]
     return pl.pallas_call(
         first_body,
         out_shape=[
@@ -303,18 +306,19 @@
             jax.ShapeDtypeStruct(positions.shape, F32),
             jax.ShapeDtypeStruct((2, 2, HALF, PAD), F32),
             jax.ShapeDtypeStruct((partners.shape[-1], 128), jnp.int32),
+            *[jax.ShapeDtypeStruct(t.shape, BF) for t in tables],
         ],
-        in_specs=[VM] + [HBM] * 5,
-        out_specs=[VM] * 5,
+        in_specs=[VM] + [HBM] * 9,
+        out_specs=[VM] * 9,
         scratch_shapes=[
             *[pltpu.VMEM((2, 2 * GRID, 2 * n), BF)] * 2,
             pltpu.VMEM(kernel_hat.shape, F32),
             *[pltpu.SMEM(t.shape, jnp.int32) for t in small],
-            pltpu.SemaphoreType.DMA((5,)),
+            pltpu.SemaphoreType.DMA((9,)),
         ],
         compiler_params=params(16),
         name="first_deposit",
-    )(pos_c, *[in_hbm(t) for t in (positions, kernel_hat, *small)])
+    )(pos_c, *[in_hbm(t) for t in (positions, kernel_hat, *small, *tables)])
 
 
 def kick_tables(ref, start, lanes, wx_ref, wy_ref, to):
@@ -341,21 +345,11 @@
 
 def field_body(
     own_ref, r1_ref, r2_ref, s1_ref, s2_ref,
-    rows_hbm, cols_hbm, bcols_hbm, brows_hbm,
-    half_ref, slots_ref, pyc_ref,
+    half_ref, slots_ref, rows_ref, cols_ref, bcols_ref, brows_ref, pyc_ref,
     maps_ref, out_ref,
-    wx_ref, wy_ref, grids, source, rows_ref, cols_ref, bcols_ref, brows_ref, sems,
+    wx_ref, wy_ref, grids, source,
 ):
     c = core()
-    fixed = [
-        pltpu.make_async_copy(src, dst, sems.at[i])
-        for i, (src, dst) in enumerate((
-            (rows_hbm, rows_ref), (cols_hbm, cols_ref),
-            (bcols_hbm, bcols_ref), (brows_hbm, brows_ref),
-        ))
-    ]
-    for copy in fixed:
-        copy.start()
     slots = slots_ref[...]
     n = out_ref.shape[-1]
     for start in range(0, n, CHUNK):
@@ -377,14 +371,11 @@
         source[0, pl.ds(r0, GRID), :] += low
         source[1, pl.ds(r0, GRID), :] += turned - low
     hi, lo = hilo(jnp.concatenate([source[0, 0:SPAN, :], source[1, 0:SPAN, :]], 1))
-    fixed[0].wait()
     half = dot(rows_ref[...], jnp.concatenate([hi, lo, hi], 0))
     hi, lo = hilo(half)
-    fixed[1].wait()
     spec = dot(jnp.concatenate([hi, lo, hi], 1), cols_ref[...])
     spec_r = spec[:HALF, :PAD] + spec[HALF:, PAD:]
     spec_i = spec[HALF:, :PAD] - spec[:HALF, PAD:]
-    fixed[2].wait()
     back = []
     for comp in range(2):
         kr = half_ref[comp, 0]
@@ -398,7 +389,6 @@
         im = jnp.where(first, re[GRID : GRID + 1], im)
         back.append(jnp.concatenate([re[:GRID], im], 0))
     hi, lo = hilo(jnp.concatenate(back, 1))
-    fixed[3].wait()
     field = dot(brows_ref[...], jnp.concatenate([hi, lo, hi], 0))
     field = jnp.concatenate([field[:, :GRID], field[:, GRID:]], 0)
     hi, lo = hilo(field)
@@ -411,28 +401,25 @@
         out_ref[1:2, start : start + CHUNK] = ky
 
 
-def field(grids, half, slots, pos_yc):
+def field(grids, half, slots, tables, pos_yc):
     n = pos_yc.shape[-1]
-    tables = [jnp.asarray(t) for t in dft_tables()]
     return pl.pallas_call(
         field_body,
         out_shape=[
             jax.ShapeDtypeStruct((2 * GRID, 3 * GRID), BF),
             jax.ShapeDtypeStruct((2, n), F32),
         ],
-        in_specs=[VM] * 5 + [HBM] * 4 + [VM] * 3,
+        in_specs=[VM] * 12,
         out_specs=[VM] * 2,
         scratch_shapes=[
             pltpu.VMEM((GRID, n), F32),
             pltpu.VMEM((3 * GRID, n), BF),
             pltpu.VMEM((4 * HOPS + 2, GRID, GRID), F32),
             pltpu.VMEM((2, SPAN + 8, GRID), F32),
-            *[pltpu.VMEM(t.shape, BF) for t in tables],
-            pltpu.SemaphoreType.DMA((4,)),
         ],
         compiler_params=params(24),
         name="field",
-    )(*grids, *[in_hbm(t) for t in tables], half, slots, pos_yc)
+    )(*grids, half, slots, *tables, pos_yc)
 
 
 def kick_body(maps_ref, pa_ref, pc_ref, py_ref, near_ref, far_ref, wx_ref, wy_ref):
@@ -514,7 +501,7 @@
 
     pos_y = across_chips(positions)
     pos_c = across_cores(positions)
-    first, near, pos_own, half, slots = first_deposit(
+    first, near, pos_own, half, slots, *tables = first_deposit(
         positions, pos_c, kernel_hat, partners, offsets, counts
     )
     pos_y, first = lax.optimization_barrier((pos_y, first))
@@ -528,7 +515,7 @@
     r1, r2 = lax.optimization_barrier((r1, r2))
     s2 = across_cores(r2)
     s1 = across_cores(r1)
-    maps, diagonal = field((own, r1, r2, s1, s2), half, slots, pos_yc)
+    maps, diagonal = field((own, r1, r2, s1, s2), half, slots, tables, pos_yc)
     from_core_far = across_cores(diagonal)
     near, far = kick(maps, (pos_own, pos_c, pos_y))
     message, mine = lax.optimization_barrier((jnp.stack([far, from_core_far]), near))

time: 32.7 us -> 31.5 us (0.963)
  Pallas kernels: 9.96 us -> 8.86 us
    pallas_call x1, Pallas kernels: 3.2 us -> 2.07 us  [field(): pl.pallas_call(field_body, out_shape=[jax.ShapeDtypeStruct((2 * GRID, 3 *...]
  transfers between devices with their start and end apart: 10 -> 10, of which waited for: 6 -> 6; matrix products, arithmetic and copies ran while one was open for 0% -> 0% of each run, Pallas kernels for 19% -> 20%
where the time goes in v5:
time: 31.5 us; the launch traced here: 31.4 us
  starting transfers between devices  17.9 us (57%)
  Pallas kernels  8.86 us (28%)
  waiting for transfers between devices  4.63 us (15%)
    ppermute x2, starting transfers between devices, along_blocks(): return lax.ppermute(x, ('bunch', 'dom'), pairs)  8.25 us
    ppermute x6, starting transfers between devices, across_cores(): return lax.ppermute(x, 'dom', [(i, i ^ 1) for i in range(doms)])  5.73 us
    ppermute x2, starting transfers between devices, across_chips(): return lax.ppermute(x, 'dom', [(i, i ^ 2) for i in range(doms)])  3.88 us
    pallas_call x1, Pallas kernels, first_deposit(): pl.pallas_call(first_body, out_shape=[jax.ShapeDtypeStruct((2, GRID, GRID...  2.42 us
    pallas_call x1, Pallas kernels, field(): pl.pallas_call(field_body, out_shape=[jax.ShapeDtypeStruct((2 * GRID, 3 *...  2.07 us
    ppermute x2, waiting for transfers between devices, across_chips(): return lax.ppermute(x, 'dom', [(i, i ^ 2) for i in range(doms)])  1.84 us
    pallas_call x1, Pallas kernels, deposit_packed(): pl.pallas_call(deposit_packed_body, out_shape=jax.ShapeDtypeStruct((2, GR...  1.59 us
    ppermute x6, waiting for transfers between devices, across_cores(): return lax.ppermute(x, 'dom', [(i, i ^ 1) for i in range(doms)])  1.43 us
  transfers between devices with their start and end apart: 10, of which 6 were waited for; matrix products, arithmetic and copies ran while one was open for 0% of the time, Pallas kernels for 20%

profile of v5, /device:TPU:1, one launch (start us, length us, event | category | flops | bytes accessed | tf_op | source)
XLA Modules:
  0.0 31.4 jit_solution(1504146823139802287)
XLA Ops:
  0.0 3.2 %collective-permute-start.1 = (f32[2,2,2,1024]{3,2,1,0:T(2,128)}, f32[2,2,2,1024]{3,2,1,0:T(2,128)S(1)}, u32[]{:S(2)}, u32[]{:S(2)}) collective-permute-start(f32[2,2,2,1024]{3,2,1,0:T(2,128)} %pa_hbm.1), channel_id=1, source_target_pairs={{0,1},{1,0},{2,3},{3,2},{4,5},{5,4},{6,7},{7,6},{8,9},{9,8},{10,11... | collective-permute-start | bytes 98312 | tf_op jit(solution)/shard_map/ppermute | solution.py:489
  3.2 1.2 %collective-permute-start = (f32[2,2,2,1024]{3,2,1,0:T(2,128)}, f32[2,2,2,1024]{3,2,1,0:T(2,128)S(1)}, u32[]{:S(2)}, u32[]{:S(2)}) collective-permute-start(f32[2,2,2,1024]{3,2,1,0:T(2,128)} %pa_hbm.1), channel_id=1, source_target_pairs={{0,2},{1,3},{2,0},{3,1},{4,6},{5,7},{6,4},{7,5},{8,10},{9,11},{10,... | collective-permute-start | bytes 98312 | tf_op jit(solution)/shard_map/ppermute | solution.py:492
  4.4 0.0 collective-permute-done.1.pc_ref
  4.4 2.4 %first_deposit.1 = (f32[2,128,128]{2,1,0:T(8,128)S(1)}, f32[2,2,2,1024]{3,2,1,0:T(2,128)S(1)}, f32[2,2,2,1024]{3,2,1,0:T(2,128)S(1)}, f32[2,2,136,256]{3,2,1,0:T...) custom-call(f32[2,2,2,1024]{3,2,1,0:T(2,128)S(1)} %collective-permut, ...), custom_call_target="tpu_custom_call" | custom-call | tf_op jit(solution)/shard_map/first_deposit/pallas_call | solution.py:301
  6.9 0.9 %collective-permute-done.refs_0_.py_ref = f32[2,2,2,1024]{3,2,1,0:T(2,128)S(1)} collective-permute-done((f32[2,2,2,1024]{3,2,1,0:T(2,128)}, f32[2,2,2,1024]{3,2,1,0:T(2,128)S(1)}, u32[]{:S(2)}, u32[]{:S(2)}) %collective-permute-start) | collective-permute-done | bytes 32800 | tf_op jit(solution)/shard_map/ppermute | solution.py:492
  7.7 1.2 %collective-permute-start.2 = (f32[2,2,2,1024]{3,2,1,0:T(2,128)S(1)}, f32[2,2,2,1024]{3,2,1,0:T(2,128)S(1)}, u32[]{:S(2)}, u32[]{:S(2)}) collective-permute-start(f32[2,2,2,1024]{3,2,1,0:T(2,128)S(1)} %collective-permute-done.refs_0_.py_ref), channel_id=1, source_target_pairs={{0,1},{1,0},{2,3},{3,2},{4,5},{5,4},{6,7},{7,6},{8,9},{9,8},{10,11... | collective-permute-start | bytes 98312 | tf_op jit(solution)/shard_map/ppermute | solution.py:489
  8.9 0.5 %deposit.2 = (f32[2,128,128]{2,1,0:T(8,128)S(1)}, f32[1,2,2,1024]{3,2,1,0:T(2,128)S(1)}) custom-call(f32[2,2,2,1024]{3,2,1,0:T(2,128)S(1)} %collective-permute-done.refs_0_.py_ref, f32[2,128,128]{2,1,0:T(8,128)S(1)} %get-tuple-element.28.refs_1_), custom_call_target="tpu_custom_call" | custom-call | flops 10000000 | tf_op jit(solution)/shard_map/deposit/pallas_call | solution.py:171
  9.4 0.3 collective-permute-done.2.refs_0_.yc_ref.pyc_ref
  9.7 7.3 %collective-permute-start.4 = (f32[4,2,2,1024]{3,2,1,0:T(2,128)S(1)}, f32[4,2,2,1024]{3,2,1,0:T(2,128)S(1)}, u32[]{:S(2)}, u32[]{:S(2)}) collective-permute-start(f32[4,2,2,1024]{3,2,1,0:T(2,128)S(1)} %pack.1), channel_id=1, source_target_pairs={{0,8},{1,249},{2,10},{3,251},{4,12},{5,253},{6,14},{7,255},{8,16},... | collective-permute-start | bytes 196616 | tf_op jit(solution)/shard_map/ppermute | solution.py:500
  17.1 0.6 %deposit.3.own_ref = f32[2,128,128]{2,1,0:T(8,128)S(1)} custom-call(f32[2,2,2,1024]{3,2,1,0:T(2,128)S(1)} %collective-permute-done.2.refs_0_.yc_ref.pyc_ref, f32[2,128,128]{2,1,0:T(8,128)S(1)} %get-tuple-element.29.refs_1_), custom_call_target="tpu_custom_call" | custom-call | flops 10000000 | tf_op jit(solution)/shard_map/deposit/pallas_call | solution.py:171
  17.6 0.9 %collective-permute-start.3 = (f32[2,128,128]{2,1,0:T(8,128)S(1)}, f32[2,128,128]{2,1,0:T(8,128)S(1)}, u32[]{:S(2)}, u32[]{:S(2)}) collective-permute-start(f32[2,128,128]{2,1,0:T(8,128)S(1)} %deposit.3.own_ref), channel_id=1, source_target_pairs={{0,4},{1,253},{2,6},{3,255},{4,8},{5,1},{6,10},{7,3},{8,12},{9,5},... | collective-permute-start | bytes 393224 | tf_op jit(solution)/shard_map/ppermute | solution.py:500
  18.6 0.0 collective-permute-done.4.pos_ref
  18.6 1.6 %deposit_packed.1.r2_ref = f32[2,128,128]{2,1,0:T(8,128)S(1)} custom-call(f32[4,2,2,1024]{3,2,1,0:T(2,128)S(1)} %collective-permute-done.4.pos_ref), custom_call_target="tpu_custom_call" | custom-call | flops 99999997952 | tf_op jit(solution)/shard_map/deposit_packed/pallas_call | solution.py:220
  20.2 1.4 %collective-permute-done.3.r1_ref = f32[2,128,128]{2,1,0:T(8,128)S(1)} collective-permute-done((f32[2,128,128]{2,1,0:T(8,128)S(1)}, f32[2,128,128]{2,1,0:T(8,128)S(1)}, u32[]{:S(2)}, u32[]{:S(2)}) %collective-permute-start.3) | collective-permute-done | bytes 131104 | tf_op jit(solution)/shard_map/ppermute | solution.py:500
  21.5 0.3 collective-permute-start.5
  21.8 0.2 collective-permute-start.6
  22.0 0.8 %collective-permute-done.5.s1_ref = f32[2,128,128]{2,1,0:T(8,128)S(1)} collective-permute-done((f32[2,128,128]{2,1,0:T(8,128)S(1)}, f32[2,128,128]{2,1,0:T(8,128)S(1)}, u32[]{:S(2)}, u32[]{:S(2)}) %collective-permute-start.5) | collective-permute-done | bytes 131104 | tf_op jit(solution)/shard_map/ppermute | solution.py:489
  22.9 0.3 collective-permute-done.6.s2_ref
  23.1 2.1 %field.1 = (bf16[256,384]{1,0:T(8,128)(2,1)S(1)}, f32[2,1024]{1,0:T(2,128)S(1)}) custom-call(f32[2,128,128]{2,1,0:T(8,128)S(1)} %deposit.3.own_ref, f32[2,128,128]{2,1,0:T(8,128)S(1)} %collective-permute-done.3.r1_ref, f32[2,128,128]{2,1,0:T(8,128)S(1)} %deposit_packed.1.r2_ref, f32[2,128,128]{2,1,0:T(8,128)S(1)} %collective-permute-done.5.s1_ref, ...), custom_call_target="tpu_custom_call" | custom-call | tf_op jit(solution)/shard_map/field/pallas_call | solution.py:406
  25.2 0.3 %collective-permute-start.7 = (f32[2,1024]{1,0:T(2,128)S(1)}, f32[2,1024]{1,0:T(2,128)S(1)}, u32[]{:S(2)}, u32[]{:S(2)}) collective-permute-start(f32[2,1024]{1,0:T(2,128)S(1)} %get-tuple-element.43), channel_id=1, source_target_pairs={{0,1},{1,0},{2,3},{3,2},{4,5},{5,4},{6,7},{7,6},{8,9},{9,8},{10,11... | collective-permute-start | bytes 24584 | tf_op jit(solution)/shard_map/ppermute | solution.py:489
  25.5 1.0 %kick.1 = (f32[2,2,1024]{2,1,0:T(2,128)S(1)}, f32[2,1024]{1,0:T(2,128)S(1)}) custom-call(bf16[256,384]{1,0:T(8,128)(2,1)S(1)} %get-tuple-element.40.maps_ref, f32[2,2,2,1024]{3,2,1,0:T(2,128)S(1)} %get-tuple-element.41.pa_ref, f32[2,2,2,1024]{3,2,1,0:T(2,128)S(1)} %collective-permute-done.1.pc_ref, f32[2,2,2,1024]{3,2,1,0:T(2,128)S(1)} %collective-permute-done.refs_0_.py_ref), custom_call_target="tpu_custom_call" | custom-call | tf_op jit(solution)/shard_map/kick/pallas_call | solution.py:444
  26.6 0.0 copy-start
  26.6 0.0 collective-permute-done.7
  26.6 2.7 %collective-permute-start.9 = (f32[2,2,1024]{2,1,0:T(2,128)S(1)}, f32[2,2,1024]{2,1,0:T(2,128)S(1)}, u32[]{:S(2)}, u32[]{:S(2)}) collective-permute-start(f32[2,2,1024]{2,1,0:T(2,128)S(1)} %pad_maximum_fusion), channel_id=1, source_target_pairs={{0,2},{1,3},{2,0},{3,1},{4,6},{5,7},{6,4},{7,5},{8,10},{9,11},{10,... | collective-permute-start | bytes 49160 | tf_op jit(solution)/shard_map/ppermute | solution.py:492
  29.3 0.5 %collective-permute-start.8 = (f32[2,2,1024]{2,1,0:T(2,128)S(1)}, f32[2,2,1024]{2,1,0:T(2,128)S(1)}, u32[]{:S(2)}, u32[]{:S(2)}) collective-permute-start(f32[2,2,1024]{2,1,0:T(2,128)S(1)} %get-tuple-element.45.mine_ref), channel_id=1, source_target_pairs={{0,1},{1,0},{2,3},{3,2},{4,5},{5,4},{6,7},{7,6},{8,9},{9,8},{10,11... | collective-permute-start | bytes 49160 | tf_op jit(solution)/shard_map/ppermute | solution.py:489
  29.8 1.0 %collective-permute-done.9.chip_ref = f32[2,2,1024]{2,1,0:T(2,128)S(1)} collective-permute-done((f32[2,2,1024]{2,1,0:T(2,128)S(1)}, f32[2,2,1024]{2,1,0:T(2,128)S(1)}, u32[]{:S(2)}, u32[]{:S(2)}) %collective-permute-start.9) | collective-permute-done | bytes 16416 | tf_op jit(solution)/shard_map/ppermute | solution.py:492
  30.8 0.0 collective-permute-done.8.core_ref
  30.8 0.0 copy-done
  30.8 0.6 %finish.1 = f32[2,2,2,1024]{3,2,1,0:T(2,128)} custom-call(f32[2,2,1024]{2,1,0:T(2,128)S(1)} %get-tuple-element.45.mine_ref, f32[2,2,1024]{2,1,0:T(2,128)S(1)} %collective-permute-done.8.core_ref, f32[2,2,1024]{2,1,0:T(2,128)S(1)} %collective-permute-done.9.chip_ref, f32[2,2,2,1024]{3,2,1,0:T(2,128)S(1)} %copy-done), custom_call_target="tpu_custom_call" | custom-call | tf_op jit(solution)/shard_map/finish/pallas_call | solution.py:474
  (2 shorter events, 0.0 us)
Async XLA Ops:
  0.0 4.4 %collective-permute-start.1 = (f32[2,2,2,1024]{3,2,1,0:T(2,128)}, f32[2,2,2,1024]{3,2,1,0:T(2,128)S(1)}, u32[]{:S(2)}, u32[]{:S(2)}) collective-permute-start(f32[2,2,2,1024]{3,2,1,0:T(2,128)} %pa_hbm.1), channel_id=1, source_target_pairs={{0,1},{1,0},{2,3},{3,2},{4,5},{5,4},{6,7},{7,6},{8,9},{9,8},{10,11... | collective-permute-start | bytes 98312 | tf_op jit(solution)/shard_map/ppermute | solution.py:489
  3.2 4.5 %collective-permute-start = (f32[2,2,2,1024]{3,2,1,0:T(2,128)}, f32[2,2,2,1024]{3,2,1,0:T(2,128)S(1)}, u32[]{:S(2)}, u32[]{:S(2)}) collective-permute-start(f32[2,2,2,1024]{3,2,1,0:T(2,128)} %pa_hbm.1), channel_id=1, source_target_pairs={{0,2},{1,3},{2,0},{3,1},{4,6},{5,7},{6,4},{7,5},{8,10},{9,11},{10,... | collective-permute-start | bytes 98312 | tf_op jit(solution)/shard_map/ppermute | solution.py:492
  7.7 2.0 %collective-permute-start.2 = (f32[2,2,2,1024]{3,2,1,0:T(2,128)S(1)}, f32[2,2,2,1024]{3,2,1,0:T(2,128)S(1)}, u32[]{:S(2)}, u32[]{:S(2)}) collective-permute-start(f32[2,2,2,1024]{3,2,1,0:T(2,128)S(1)} %collective-permute-done.refs_0_.py_ref), channel_id=1, source_target_pairs={{0,1},{1,0},{2,3},{3,2},{4,5},{5,4},{6,7},{7,6},{8,9},{9,8},{10,11... | collective-permute-start | bytes 98312 | tf_op jit(solution)/shard_map/ppermute | solution.py:489
  9.7 8.8 %collective-permute-start.4 = (f32[4,2,2,1024]{3,2,1,0:T(2,128)S(1)}, f32[4,2,2,1024]{3,2,1,0:T(2,128)S(1)}, u32[]{:S(2)}, u32[]{:S(2)}) collective-permute-start(f32[4,2,2,1024]{3,2,1,0:T(2,128)S(1)} %pack.1), channel_id=1, source_target_pairs={{0,8},{1,249},{2,10},{3,251},{4,12},{5,253},{6,14},{7,255},{8,16},... | collective-permute-start | bytes 196616 | tf_op jit(solution)/shard_map/ppermute | solution.py:500
  17.6 3.9 %collective-permute-start.3 = (f32[2,128,128]{2,1,0:T(8,128)S(1)}, f32[2,128,128]{2,1,0:T(8,128)S(1)}, u32[]{:S(2)}, u32[]{:S(2)}) collective-permute-start(f32[2,128,128]{2,1,0:T(8,128)S(1)} %deposit.3.own_ref), channel_id=1, source_target_pairs={{0,4},{1,253},{2,6},{3,255},{4,8},{5,1},{6,10},{7,3},{8,12},{9,5},... | collective-permute-start | bytes 393224 | tf_op jit(solution)/shard_map/ppermute | solution.py:500
  21.5 1.3 %collective-permute-start.5 = (f32[2,128,128]{2,1,0:T(8,128)S(1)}, f32[2,128,128]{2,1,0:T(8,128)S(1)}, u32[]{:S(2)}, u32[]{:S(2)}) collective-permute-start(f32[2,128,128]{2,1,0:T(8,128)S(1)} %collective-permute-done.3.r1_ref), channel_id=1, source_target_pairs={{0,1},{1,0},{2,3},{3,2},{4,5},{5,4},{6,7},{7,6},{8,9},{9,8},{10,11... | collective-permute-start | bytes 393224 | tf_op jit(solution)/shard_map/ppermute | solution.py:489
  21.8 1.3 %collective-permute-start.6 = (f32[2,128,128]{2,1,0:T(8,128)S(1)}, f32[2,128,128]{2,1,0:T(8,128)S(1)}, u32[]{:S(2)}, u32[]{:S(2)}) collective-permute-start(f32[2,128,128]{2,1,0:T(8,128)S(1)} %deposit_packed.1.r2_ref), channel_id=1, source_target_pairs={{0,1},{1,0},{2,3},{3,2},{4,5},{5,4},{6,7},{7,6},{8,9},{9,8},{10,11... | collective-permute-start | bytes 393224 | tf_op jit(solution)/shard_map/ppermute | solution.py:489
  25.2 1.4 %collective-permute-start.7 = (f32[2,1024]{1,0:T(2,128)S(1)}, f32[2,1024]{1,0:T(2,128)S(1)}, u32[]{:S(2)}, u32[]{:S(2)}) collective-permute-start(f32[2,1024]{1,0:T(2,128)S(1)} %get-tuple-element.43), channel_id=1, source_target_pairs={{0,1},{1,0},{2,3},{3,2},{4,5},{5,4},{6,7},{7,6},{8,9},{9,8},{10,11... | collective-permute-start | bytes 24584 | tf_op jit(solution)/shard_map/ppermute | solution.py:489
  26.6 4.2 %copy-start = (f32[2,2,2,1024]{3,2,1,0:T(2,128)S(1)}, f32[2,2,2,1024]{3,2,1,0:T(2,128)}, u32[]{:S(2)}) copy-start(f32[2,2,2,1024]{3,2,1,0:T(2,128)} %momenta_ref.1) | copy-start | bytes 98308
  26.6 4.2 %collective-permute-start.9 = (f32[2,2,1024]{2,1,0:T(2,128)S(1)}, f32[2,2,1024]{2,1,0:T(2,128)S(1)}, u32[]{:S(2)}, u32[]{:S(2)}) collective-permute-start(f32[2,2,1024]{2,1,0:T(2,128)S(1)} %pad_maximum_fusion), channel_id=1, source_target_pairs={{0,2},{1,3},{2,0},{3,1},{4,6},{5,7},{6,4},{7,5},{8,10},{9,11},{10,... | collective-permute-start | bytes 49160 | tf_op jit(solution)/shard_map/ppermute | solution.py:492
  29.3 1.5 %collective-permute-start.8 = (f32[2,2,1024]{2,1,0:T(2,128)S(1)}, f32[2,2,1024]{2,1,0:T(2,128)S(1)}, u32[]{:S(2)}, u32[]{:S(2)}) collective-permute-start(f32[2,2,1024]{2,1,0:T(2,128)S(1)} %get-tuple-element.45.mine_ref), channel_id=1, source_target_pairs={{0,1},{1,0},{2,3},{3,2},{4,5},{5,4},{6,7},{7,6},{8,9},{9,8},{10,11... | collective-permute-start | bytes 49160 | tf_op jit(solution)/shard_map/ppermute | solution.py:489

commit v6 on v5

--- a/solution.py
+++ b/solution.py
@@ -345,15 +345,13 @@
 
 def field_body(
     own_ref, r1_ref, r2_ref, s1_ref, s2_ref,
-    half_ref, slots_ref, rows_ref, cols_ref, bcols_ref, brows_ref, pyc_ref,
+    half_ref, slots_ref, rows_ref, cols_ref, bcols_ref, brows_ref, wx_ref, wy_ref,
     maps_ref, out_ref,
-    wx_ref, wy_ref, grids, source,
+    grids, source,
 ):
     c = core()
     slots = slots_ref[...]
     n = out_ref.shape[-1]
-    for start in range(0, n, CHUNK):
-        kick_tables(pyc_ref, start, CHUNK, wx_ref, wy_ref, start)
     places = (2, 1 + 2 * c, 4 * c, 3 - 2 * c, 4 - 4 * c)
     for ref, place in zip((own_ref, r1_ref, r2_ref, s1_ref, s2_ref), places):
         grids[2 * place] = ref[0]
@@ -401,25 +399,40 @@
         out_ref[1:2, start : start + CHUNK] = ky
 
 
-def field(grids, half, slots, tables, pos_yc):
-    n = pos_yc.shape[-1]
+def tables_body(pos_ref, wx_ref, wy_ref):
+    for start in range(0, pos_ref.shape[-1], CHUNK):
+        kick_tables(pos_ref, start, CHUNK, wx_ref, wy_ref, start)
+
+
+def weight_tables(pos):
+    n = pos.shape[-1]
+    return pl.pallas_call(
+        tables_body,
+        out_shape=[jax.ShapeDtypeStruct((GRID, n), F32), jax.ShapeDtypeStruct((3 * GRID, n), BF)],
+        in_specs=[VM],
+        out_specs=[VM] * 2,
+        compiler_params=params(8),
+        name="weight_tables",
+    )(pos)
+
+
+def field(grids, half, slots, tables, weights):
+    n = weights[0].shape[-1]
     return pl.pallas_call(
         field_body,
         out_shape=[
             jax.ShapeDtypeStruct((2 * GRID, 3 * GRID), BF),
             jax.ShapeDtypeStruct((2, n), F32),
         ],
-        in_specs=[VM] * 12,
+        in_specs=[VM] * 13,
         out_specs=[VM] * 2,
         scratch_shapes=[
-            pltpu.VMEM((GRID, n), F32),
-            pltpu.VMEM((3 * GRID, n), BF),
             pltpu.VMEM((4 * HOPS + 2, GRID, GRID), F32),
             pltpu.VMEM((2, SPAN + 8, GRID), F32),
         ],
         compiler_params=params(24),
         name="field",
-    )(*grids, half, slots, *tables, pos_yc)
+    )(*grids, half, slots, *tables, *weights)
 
 
 def kick_body(maps_ref, pa_ref, pc_ref, py_ref, near_ref, far_ref, wx_ref, wy_ref):
@@ -515,7 +528,9 @@
     r1, r2 = lax.optimization_barrier((r1, r2))
     s2 = across_cores(r2)
     s1 = across_cores(r1)
-    maps, diagonal = field((own, r1, r2, s1, s2), half, slots, tables, pos_yc)
+    late_yc, r2 = lax.optimization_barrier((pos_yc, r2))
+    weights = weight_tables(late_yc)
+    maps, diagonal = field((own, r1, r2, s1, s2), half, slots, tables, weights)
     from_core_far = across_cores(diagonal)
     near, far = kick(maps, (pos_own, pos_c, pos_y))
     message, mine = lax.optimization_barrier((jnp.stack([far, from_core_far]), near))

time: 31.5 us -> 31.5 us (level)
  no operation moved by 1% of the time
where the time goes in v6:
time: 31.5 us; the launch traced here: 31.4 us
  starting transfers between devices  17.9 us (57%)
  Pallas kernels  9.04 us (29%)
  waiting for transfers between devices  4.45 us (14%)
    ppermute x2, starting transfers between devices, along_blocks(): return lax.ppermute(x, ('bunch', 'dom'), pairs)  8.25 us
    ppermute x6, starting transfers between devices, across_cores(): return lax.ppermute(x, 'dom', [(i, i ^ 1) for i in range(doms)])  5.73 us
    ppermute x2, starting transfers between devices, across_chips(): return lax.ppermute(x, 'dom', [(i, i ^ 2) for i in range(doms)])  3.88 us
    pallas_call x1, Pallas kernels, first_deposit(): pl.pallas_call(first_body, out_shape=[jax.ShapeDtypeStruct((2, GRID, GRID...  2.42 us
    pallas_call x1, Pallas kernels, field(): pl.pallas_call(field_body, out_shape=[jax.ShapeDtypeStruct((2 * GRID, 3 *...  2.06 us
    ppermute x2, waiting for transfers between devices, across_chips(): return lax.ppermute(x, 'dom', [(i, i ^ 2) for i in range(doms)])  1.85 us
    pallas_call x1, Pallas kernels, deposit_packed(): pl.pallas_call(deposit_packed_body, out_shape=jax.ShapeDtypeStruct((2, GR...  1.59 us
    ppermute x2, waiting for transfers between devices, along_blocks(): return lax.ppermute(x, ('bunch', 'dom'), pairs)  1.36 us
  transfers between devices with their start and end apart: 10, of which 6 were waited for; matrix products, arithmetic and copies ran while one was open for 0% of the time, Pallas kernels for 20%

profile of v6, /device:TPU:1, one launch (start us, length us, event | category | flops | bytes accessed | tf_op | source)
XLA Modules:
  0.0 31.4 jit_solution(48226507941813675)
XLA Ops:
  0.0 3.2 %collective-permute-start.1 = (f32[2,2,2,1024]{3,2,1,0:T(2,128)}, f32[2,2,2,1024]{3,2,1,0:T(2,128)S(1)}, u32[]{:S(2)}, u32[]{:S(2)}) collective-permute-start(f32[2,2,2,1024]{3,2,1,0:T(2,128)} %pa_hbm.1), channel_id=1, source_target_pairs={{0,1},{1,0},{2,3},{3,2},{4,5},{5,4},{6,7},{7,6},{8,9},{9,8},{10,11... | collective-permute-start | bytes 98312 | tf_op jit(solution)/shard_map/ppermute | solution.py:502
  3.2 1.2 %collective-permute-start = (f32[2,2,2,1024]{3,2,1,0:T(2,128)}, f32[2,2,2,1024]{3,2,1,0:T(2,128)S(1)}, u32[]{:S(2)}, u32[]{:S(2)}) collective-permute-start(f32[2,2,2,1024]{3,2,1,0:T(2,128)} %pa_hbm.1), channel_id=1, source_target_pairs={{0,2},{1,3},{2,0},{3,1},{4,6},{5,7},{6,4},{7,5},{8,10},{9,11},{10,... | collective-permute-start | bytes 98312 | tf_op jit(solution)/shard_map/ppermute | solution.py:505
  4.4 0.0 collective-permute-done.1.pc_ref
  4.4 2.4 %first_deposit.1 = (f32[2,128,128]{2,1,0:T(8,128)S(1)}, f32[2,2,2,1024]{3,2,1,0:T(2,128)S(1)}, f32[2,2,2,1024]{3,2,1,0:T(2,128)S(1)}, f32[2,2,136,256]{3,2,1,0:T...) custom-call(f32[2,2,2,1024]{3,2,1,0:T(2,128)S(1)} %collective-permut, ...), custom_call_target="tpu_custom_call" | custom-call | tf_op jit(solution)/shard_map/first_deposit/pallas_call | solution.py:301
  6.9 0.9 %collective-permute-done.refs_0_.py_ref = f32[2,2,2,1024]{3,2,1,0:T(2,128)S(1)} collective-permute-done((f32[2,2,2,1024]{3,2,1,0:T(2,128)}, f32[2,2,2,1024]{3,2,1,0:T(2,128)S(1)}, u32[]{:S(2)}, u32[]{:S(2)}) %collective-permute-start) | collective-permute-done | bytes 32800 | tf_op jit(solution)/shard_map/ppermute | solution.py:505
  7.7 1.2 %collective-permute-start.2 = (f32[2,2,2,1024]{3,2,1,0:T(2,128)S(1)}, f32[2,2,2,1024]{3,2,1,0:T(2,128)S(1)}, u32[]{:S(2)}, u32[]{:S(2)}) collective-permute-start(f32[2,2,2,1024]{3,2,1,0:T(2,128)S(1)} %collective-permute-done.refs_0_.py_ref), channel_id=1, source_target_pairs={{0,1},{1,0},{2,3},{3,2},{4,5},{5,4},{6,7},{7,6},{8,9},{9,8},{10,11... | collective-permute-start | bytes 98312 | tf_op jit(solution)/shard_map/ppermute | solution.py:502
  8.9 0.5 %deposit.2 = (f32[2,128,128]{2,1,0:T(8,128)S(1)}, f32[1,2,2,1024]{3,2,1,0:T(2,128)S(1)}) custom-call(f32[2,2,2,1024]{3,2,1,0:T(2,128)S(1)} %collective-permute-done.refs_0_.py_ref, f32[2,128,128]{2,1,0:T(8,128)S(1)} %get-tuple-element.32.refs_1_), custom_call_target="tpu_custom_call" | custom-call | flops 10000000 | tf_op jit(solution)/shard_map/deposit/pallas_call | solution.py:171
  9.4 0.3 collective-permute-done.2.refs_0_.yc_ref.pos_ref
  9.7 7.3 %collective-permute-start.4 = (f32[4,2,2,1024]{3,2,1,0:T(2,128)S(1)}, f32[4,2,2,1024]{3,2,1,0:T(2,128)S(1)}, u32[]{:S(2)}, u32[]{:S(2)}) collective-permute-start(f32[4,2,2,1024]{3,2,1,0:T(2,128)S(1)} %pack.1), channel_id=1, source_target_pairs={{0,8},{1,249},{2,10},{3,251},{4,12},{5,253},{6,14},{7,255},{8,16},... | collective-permute-start | bytes 196616 | tf_op jit(solution)/shard_map/ppermute | solution.py:513
  17.1 0.6 %deposit.3.own_ref = f32[2,128,128]{2,1,0:T(8,128)S(1)} custom-call(f32[2,2,2,1024]{3,2,1,0:T(2,128)S(1)} %collective-permute-done.2.refs_0_.yc_ref.pos_ref, f32[2,128,128]{2,1,0:T(8,128)S(1)} %get-tuple-element.33.refs_1_), custom_call_target="tpu_custom_call" | custom-call | flops 10000000 | tf_op jit(solution)/shard_map/deposit/pallas_call | solution.py:171
  17.6 0.9 %collective-permute-start.3 = (f32[2,128,128]{2,1,0:T(8,128)S(1)}, f32[2,128,128]{2,1,0:T(8,128)S(1)}, u32[]{:S(2)}, u32[]{:S(2)}) collective-permute-start(f32[2,128,128]{2,1,0:T(8,128)S(1)} %deposit.3.own_ref), channel_id=1, source_target_pairs={{0,4},{1,253},{2,6},{3,255},{4,8},{5,1},{6,10},{7,3},{8,12},{9,5},... | collective-permute-start | bytes 393224 | tf_op jit(solution)/shard_map/ppermute | solution.py:513
  18.6 0.0 collective-permute-done.4.pos_ref
  18.6 1.6 %deposit_packed.1.r2_ref = f32[2,128,128]{2,1,0:T(8,128)S(1)} custom-call(f32[4,2,2,1024]{3,2,1,0:T(2,128)S(1)} %collective-permute-done.4.pos_ref), custom_call_target="tpu_custom_call" | custom-call | flops 99999997952 | tf_op jit(solution)/shard_map/deposit_packed/pallas_call | solution.py:220
  20.2 1.4 %collective-permute-done.3.r1_ref = f32[2,128,128]{2,1,0:T(8,128)S(1)} collective-permute-done((f32[2,128,128]{2,1,0:T(8,128)S(1)}, f32[2,128,128]{2,1,0:T(8,128)S(1)}, u32[]{:S(2)}, u32[]{:S(2)}) %collective-permute-start.3) | collective-permute-done | bytes 131104 | tf_op jit(solution)/shard_map/ppermute | solution.py:513
  21.5 0.3 collective-permute-start.5
  21.8 0.2 collective-permute-start.6
  22.0 0.2 weight_tables.1
  22.2 0.7 %collective-permute-done.5.s1_ref = f32[2,128,128]{2,1,0:T(8,128)S(1)} collective-permute-done((f32[2,128,128]{2,1,0:T(8,128)S(1)}, f32[2,128,128]{2,1,0:T(8,128)S(1)}, u32[]{:S(2)}, u32[]{:S(2)}) %collective-permute-start.5) | collective-permute-done | bytes 131104 | tf_op jit(solution)/shard_map/ppermute | solution.py:502
  22.9 0.3 collective-permute-done.6.s2_ref
  23.1 2.1 %field.1 = (bf16[256,384]{1,0:T(8,128)(2,1)S(1)}, f32[2,1024]{1,0:T(2,128)S(1)}) custom-call(f32[2,128,128]{2,1,0:T(8,128)S(1)} %deposit.3.own_ref, f32[2,128,128]{2,1,0:T(8,128)S(1)} %collective-permute-done.3.r1_ref, f32[2,128,128]{2,1,0:T(8,128)S(1)} %deposit_packed.1.r2_ref, f32[2,128,128]{2,1,0:T(8,128)S(1)} %collective-permute-done.5.s1_ref, ...), custom_call_target="tpu_custom_call" | custom-call | tf_op jit(solution)/shard_map/field/pallas_call | solution.py:421
  25.2 0.3 %collective-permute-start.7 = (f32[2,1024]{1,0:T(2,128)S(1)}, f32[2,1024]{1,0:T(2,128)S(1)}, u32[]{:S(2)}, u32[]{:S(2)}) collective-permute-start(f32[2,1024]{1,0:T(2,128)S(1)} %get-tuple-element.51), channel_id=1, source_target_pairs={{0,1},{1,0},{2,3},{3,2},{4,5},{5,4},{6,7},{7,6},{8,9},{9,8},{10,11... | collective-permute-start | bytes 24584 | tf_op jit(solution)/shard_map/ppermute | solution.py:502
  25.5 1.0 %kick.1 = (f32[2,2,1024]{2,1,0:T(2,128)S(1)}, f32[2,1024]{1,0:T(2,128)S(1)}) custom-call(bf16[256,384]{1,0:T(8,128)(2,1)S(1)} %get-tuple-element.48.maps_ref, f32[2,2,2,1024]{3,2,1,0:T(2,128)S(1)} %get-tuple-element.49.pa_ref, f32[2,2,2,1024]{3,2,1,0:T(2,128)S(1)} %collective-permute-done.1.pc_ref, f32[2,2,2,1024]{3,2,1,0:T(2,128)S(1)} %collective-permute-done.refs_0_.py_ref), custom_call_target="tpu_custom_call" | custom-call | tf_op jit(solution)/shard_map/kick/pallas_call | solution.py:457
  26.6 0.0 copy-start
  26.6 0.0 collective-permute-done.7
  26.6 2.7 %collective-permute-start.9 = (f32[2,2,1024]{2,1,0:T(2,128)S(1)}, f32[2,2,1024]{2,1,0:T(2,128)S(1)}, u32[]{:S(2)}, u32[]{:S(2)}) collective-permute-start(f32[2,2,1024]{2,1,0:T(2,128)S(1)} %pad_maximum_fusion), channel_id=1, source_target_pairs={{0,2},{1,3},{2,0},{3,1},{4,6},{5,7},{6,4},{7,5},{8,10},{9,11},{10,... | collective-permute-start | bytes 49160 | tf_op jit(solution)/shard_map/ppermute | solution.py:505
  29.3 0.5 %collective-permute-start.8 = (f32[2,2,1024]{2,1,0:T(2,128)S(1)}, f32[2,2,1024]{2,1,0:T(2,128)S(1)}, u32[]{:S(2)}, u32[]{:S(2)}) collective-permute-start(f32[2,2,1024]{2,1,0:T(2,128)S(1)} %get-tuple-element.53.mine_ref), channel_id=1, source_target_pairs={{0,1},{1,0},{2,3},{3,2},{4,5},{5,4},{6,7},{7,6},{8,9},{9,8},{10,11... | collective-permute-start | bytes 49160 | tf_op jit(solution)/shard_map/ppermute | solution.py:502
  29.8 1.0 %collective-permute-done.9.chip_ref = f32[2,2,1024]{2,1,0:T(2,128)S(1)} collective-permute-done((f32[2,2,1024]{2,1,0:T(2,128)S(1)}, f32[2,2,1024]{2,1,0:T(2,128)S(1)}, u32[]{:S(2)}, u32[]{:S(2)}) %collective-permute-start.9) | collective-permute-done | bytes 16416 | tf_op jit(solution)/shard_map/ppermute | solution.py:505
  30.8 0.0 collective-permute-done.8.core_ref
  30.8 0.0 copy-done
  30.8 0.6 %finish.1 = f32[2,2,2,1024]{3,2,1,0:T(2,128)} custom-call(f32[2,2,1024]{2,1,0:T(2,128)S(1)} %get-tuple-element.53.mine_ref, f32[2,2,1024]{2,1,0:T(2,128)S(1)} %collective-permute-done.8.core_ref, f32[2,2,1024]{2,1,0:T(2,128)S(1)} %collective-permute-done.9.chip_ref, f32[2,2,2,1024]{3,2,1,0:T(2,128)S(1)} %copy-done), custom_call_target="tpu_custom_call" | custom-call | tf_op jit(solution)/shard_map/finish/pallas_call | solution.py:487
  (2 shorter events, 0.0 us)
Async XLA Ops:
  0.0 4.4 %collective-permute-start.1 = (f32[2,2,2,1024]{3,2,1,0:T(2,128)}, f32[2,2,2,1024]{3,2,1,0:T(2,128)S(1)}, u32[]{:S(2)}, u32[]{:S(2)}) collective-permute-start(f32[2,2,2,1024]{3,2,1,0:T(2,128)} %pa_hbm.1), channel_id=1, source_target_pairs={{0,1},{1,0},{2,3},{3,2},{4,5},{5,4},{6,7},{7,6},{8,9},{9,8},{10,11... | collective-permute-start | bytes 98312 | tf_op jit(solution)/shard_map/ppermute | solution.py:502
  3.2 4.5 %collective-permute-start = (f32[2,2,2,1024]{3,2,1,0:T(2,128)}, f32[2,2,2,1024]{3,2,1,0:T(2,128)S(1)}, u32[]{:S(2)}, u32[]{:S(2)}) collective-permute-start(f32[2,2,2,1024]{3,2,1,0:T(2,128)} %pa_hbm.1), channel_id=1, source_target_pairs={{0,2},{1,3},{2,0},{3,1},{4,6},{5,7},{6,4},{7,5},{8,10},{9,11},{10,... | collective-permute-start | bytes 98312 | tf_op jit(solution)/shard_map/ppermute | solution.py:505
  7.7 2.0 %collective-permute-start.2 = (f32[2,2,2,1024]{3,2,1,0:T(2,128)S(1)}, f32[2,2,2,1024]{3,2,1,0:T(2,128)S(1)}, u32[]{:S(2)}, u32[]{:S(2)}) collective-permute-start(f32[2,2,2,1024]{3,2,1,0:T(2,128)S(1)} %collective-permute-done.refs_0_.py_ref), channel_id=1, source_target_pairs={{0,1},{1,0},{2,3},{3,2},{4,5},{5,4},{6,7},{7,6},{8,9},{9,8},{10,11... | collective-permute-start | bytes 98312 | tf_op jit(solution)/shard_map/ppermute | solution.py:502
  9.7 8.8 %collective-permute-start.4 = (f32[4,2,2,1024]{3,2,1,0:T(2,128)S(1)}, f32[4,2,2,1024]{3,2,1,0:T(2,128)S(1)}, u32[]{:S(2)}, u32[]{:S(2)}) collective-permute-start(f32[4,2,2,1024]{3,2,1,0:T(2,128)S(1)} %pack.1), channel_id=1, source_target_pairs={{0,8},{1,249},{2,10},{3,251},{4,12},{5,253},{6,14},{7,255},{8,16},... | collective-permute-start | bytes 196616 | tf_op jit(solution)/shard_map/ppermute | solution.py:513
  17.6 3.9 %collective-permute-start.3 = (f32[2,128,128]{2,1,0:T(8,128)S(1)}, f32[2,128,128]{2,1,0:T(8,128)S(1)}, u32[]{:S(2)}, u32[]{:S(2)}) collective-permute-start(f32[2,128,128]{2,1,0:T(8,128)S(1)} %deposit.3.own_ref), channel_id=1, source_target_pairs={{0,4},{1,253},{2,6},{3,255},{4,8},{5,1},{6,10},{7,3},{8,12},{9,5},... | collective-permute-start | bytes 393224 | tf_op jit(solution)/shard_map/ppermute | solution.py:513
  21.5 1.3 %collective-permute-start.5 = (f32[2,128,128]{2,1,0:T(8,128)S(1)}, f32[2,128,128]{2,1,0:T(8,128)S(1)}, u32[]{:S(2)}, u32[]{:S(2)}) collective-permute-start(f32[2,128,128]{2,1,0:T(8,128)S(1)} %collective-permute-done.3.r1_ref), channel_id=1, source_target_pairs={{0,1},{1,0},{2,3},{3,2},{4,5},{5,4},{6,7},{7,6},{8,9},{9,8},{10,11... | collective-permute-start | bytes 393224 | tf_op jit(solution)/shard_map/ppermute | solution.py:502
  21.8 1.3 %collective-permute-start.6 = (f32[2,128,128]{2,1,0:T(8,128)S(1)}, f32[2,128,128]{2,1,0:T(8,128)S(1)}, u32[]{:S(2)}, u32[]{:S(2)}) collective-permute-start(f32[2,128,128]{2,1,0:T(8,128)S(1)} %deposit_packed.1.r2_ref), channel_id=1, source_target_pairs={{0,1},{1,0},{2,3},{3,2},{4,5},{5,4},{6,7},{7,6},{8,9},{9,8},{10,11... | collective-permute-start | bytes 393224 | tf_op jit(solution)/shard_map/ppermute | solution.py:502
  25.2 1.4 %collective-permute-start.7 = (f32[2,1024]{1,0:T(2,128)S(1)}, f32[2,1024]{1,0:T(2,128)S(1)}, u32[]{:S(2)}, u32[]{:S(2)}) collective-permute-start(f32[2,1024]{1,0:T(2,128)S(1)} %get-tuple-element.51), channel_id=1, source_target_pairs={{0,1},{1,0},{2,3},{3,2},{4,5},{5,4},{6,7},{7,6},{8,9},{9,8},{10,11... | collective-permute-start | bytes 24584 | tf_op jit(solution)/shard_map/ppermute | solution.py:502
  26.6 4.2 %copy-start = (f32[2,2,2,1024]{3,2,1,0:T(2,128)S(1)}, f32[2,2,2,1024]{3,2,1,0:T(2,128)}, u32[]{:S(2)}) copy-start(f32[2,2,2,1024]{3,2,1,0:T(2,128)} %momenta_ref.1) | copy-start | bytes 98308
  26.6 4.2 %collective-permute-start.9 = (f32[2,2,1024]{2,1,0:T(2,128)S(1)}, f32[2,2,1024]{2,1,0:T(2,128)S(1)}, u32[]{:S(2)}, u32[]{:S(2)}) collective-permute-start(f32[2,2,1024]{2,1,0:T(2,128)S(1)} %pad_maximum_fusion), channel_id=1, source_target_pairs={{0,2},{1,3},{2,0},{3,1},{4,6},{5,7},{6,4},{7,5},{8,10},{9,11},{10,... | collective-permute-start | bytes 49160 | tf_op jit(solution)/shard_map/ppermute | solution.py:505
  29.3 1.5 %collective-permute-start.8 = (f32[2,2,1024]{2,1,0:T(2,128)S(1)}, f32[2,2,1024]{2,1,0:T(2,128)S(1)}, u32[]{:S(2)}, u32[]{:S(2)}) collective-permute-start(f32[2,2,1024]{2,1,0:T(2,128)S(1)} %get-tuple-element.53.mine_ref), channel_id=1, source_target_pairs={{0,1},{1,0},{2,3},{3,2},{4,5},{5,4},{6,7},{7,6},{8,9},{9,8},{10,11... | collective-permute-start | bytes 49160 | tf_op jit(solution)/shard_map/ppermute | solution.py:502

commit v7 on v5

--- a/solution.py
+++ b/solution.py
@@ -344,7 +344,7 @@
 
 
 def field_body(
-    own_ref, r1_ref, r2_ref, s1_ref, s2_ref,
+    own_ref, r1_ref, r2_ref, both_ref,
     half_ref, slots_ref, rows_ref, cols_ref, bcols_ref, brows_ref, pyc_ref,
     maps_ref, out_ref,
     wx_ref, wy_ref, grids, source,
@@ -355,9 +355,12 @@
     for start in range(0, n, CHUNK):
         kick_tables(pyc_ref, start, CHUNK, wx_ref, wy_ref, start)
     places = (2, 1 + 2 * c, 4 * c, 3 - 2 * c, 4 - 4 * c)
-    for ref, place in zip((own_ref, r1_ref, r2_ref, s1_ref, s2_ref), places):
+    for ref, place in zip((own_ref, r1_ref, r2_ref), places):
         grids[2 * place] = ref[0]
         grids[2 * place + 1] = ref[1]
+    for i, place in enumerate(places[3:]):
+        grids[2 * place] = both_ref[2 * i]
+        grids[2 * place + 1] = both_ref[2 * i + 1]
     source[...] = jnp.zeros_like(source)
     lane = lax.broadcasted_iota(jnp.int32, (GRID, GRID), 1)
     for s in range(slots_ref.shape[0]):
@@ -409,7 +412,7 @@
             jax.ShapeDtypeStruct((2 * GRID, 3 * GRID), BF),
             jax.ShapeDtypeStruct((2, n), F32),
         ],
-        in_specs=[VM] * 12,
+        in_specs=[VM] * 11,
         out_specs=[VM] * 2,
         scratch_shapes=[
             pltpu.VMEM((GRID, n), F32),
@@ -513,9 +516,8 @@
     r1 = along_blocks(own, 1)
     r2 = deposit_packed(p2)
     r1, r2 = lax.optimization_barrier((r1, r2))
-    s2 = across_cores(r2)
-    s1 = across_cores(r1)
-    maps, diagonal = field((own, r1, r2, s1, s2), half, slots, tables, pos_yc)
+    both = across_cores(jnp.concatenate([r1, r2], 0))
+    maps, diagonal = field((own, r1, r2, both), half, slots, tables, pos_yc)
     from_core_far = across_cores(diagonal)
     near, far = kick(maps, (pos_own, pos_c, pos_y))
     message, mine = lax.optimization_barrier((jnp.stack([far, from_core_far]), near))

time: 31.5 us -> 31.5 us (level)
    ppermute x6 -> x5, waiting for transfers between devices: 1.43 us -> 1.66 us  [across_cores(): return lax.ppermute(x, 'dom', [(i, i ^ 1) for i in range(doms)])]
    ppermute x6 -> x5, starting transfers between devices: 5.73 us -> 5.61 us  [across_cores(): return lax.ppermute(x, 'dom', [(i, i ^ 1) for i in range(doms)])]
  transfers between devices with their start and end apart: 10 -> 9, of which waited for: 6 -> 5; matrix products, arithmetic and copies ran while one was open for 0% -> 0% of each run, Pallas kernels for 20% -> 20%
where the time goes in v7:
time: 31.5 us; the launch traced here: 31.4 us
  starting transfers between devices  17.7 us (56%)
  Pallas kernels  8.87 us (28%)
  waiting for transfers between devices  4.76 us (15%)
    ppermute x2, starting transfers between devices, along_blocks(): return lax.ppermute(x, ('bunch', 'dom'), pairs)  8.25 us
    ppermute x5, starting transfers between devices, across_cores(): return lax.ppermute(x, 'dom', [(i, i ^ 1) for i in range(doms)])  5.61 us
    ppermute x2, starting transfers between devices, across_chips(): return lax.ppermute(x, 'dom', [(i, i ^ 2) for i in range(doms)])  3.83 us
    pallas_call x1, Pallas kernels, first_deposit(): pl.pallas_call(first_body, out_shape=[jax.ShapeDtypeStruct((2, GRID, GRID...  2.42 us
    pallas_call x1, Pallas kernels, field(): pl.pallas_call(field_body, out_shape=[jax.ShapeDtypeStruct((2 * GRID, 3 *...  2.07 us
    ppermute x2, waiting for transfers between devices, across_chips(): return lax.ppermute(x, 'dom', [(i, i ^ 2) for i in range(doms)])  1.75 us
    ppermute x5, waiting for transfers between devices, across_cores(): return lax.ppermute(x, 'dom', [(i, i ^ 1) for i in range(doms)])  1.66 us
    pallas_call x1, Pallas kernels, deposit_packed(): pl.pallas_call(deposit_packed_body, out_shape=jax.ShapeDtypeStruct((2, GR...  1.59 us
  transfers between devices with their start and end apart: 9, of which 5 were waited for; matrix products, arithmetic and copies ran while one was open for 0% of the time, Pallas kernels for 20%

profile of v7, /device:TPU:1, one launch (start us, length us, event | category | flops | bytes accessed | tf_op | source)
XLA Modules:
  0.0 31.4 jit_solution(9532404209478482374)
XLA Ops:
  0.0 3.2 %collective-permute-start.1 = (f32[2,2,2,1024]{3,2,1,0:T(2,128)}, f32[2,2,2,1024]{3,2,1,0:T(2,128)S(1)}, u32[]{:S(2)}, u32[]{:S(2)}) collective-permute-start(f32[2,2,2,1024]{3,2,1,0:T(2,128)} %pa_hbm.1), channel_id=1, source_target_pairs={{0,1},{1,0},{2,3},{3,2},{4,5},{5,4},{6,7},{7,6},{8,9},{9,8},{10,11... | collective-permute-start | bytes 98312 | tf_op jit(solution)/shard_map/ppermute | solution.py:492
  3.2 1.2 %collective-permute-start = (f32[2,2,2,1024]{3,2,1,0:T(2,128)}, f32[2,2,2,1024]{3,2,1,0:T(2,128)S(1)}, u32[]{:S(2)}, u32[]{:S(2)}) collective-permute-start(f32[2,2,2,1024]{3,2,1,0:T(2,128)} %pa_hbm.1), channel_id=1, source_target_pairs={{0,2},{1,3},{2,0},{3,1},{4,6},{5,7},{6,4},{7,5},{8,10},{9,11},{10,... | collective-permute-start | bytes 98312 | tf_op jit(solution)/shard_map/ppermute | solution.py:495
  4.4 0.0 collective-permute-done.1.pc_ref
  4.4 2.4 %first_deposit.1 = (f32[2,128,128]{2,1,0:T(8,128)S(1)}, f32[2,2,2,1024]{3,2,1,0:T(2,128)S(1)}, f32[2,2,2,1024]{3,2,1,0:T(2,128)S(1)}, f32[2,2,136,256]{3,2,1,0:T...) custom-call(f32[2,2,2,1024]{3,2,1,0:T(2,128)S(1)} %collective-permut, ...), custom_call_target="tpu_custom_call" | custom-call | tf_op jit(solution)/shard_map/first_deposit/pallas_call | solution.py:301
  6.9 0.9 %collective-permute-done.refs_0_.py_ref = f32[2,2,2,1024]{3,2,1,0:T(2,128)S(1)} collective-permute-done((f32[2,2,2,1024]{3,2,1,0:T(2,128)}, f32[2,2,2,1024]{3,2,1,0:T(2,128)S(1)}, u32[]{:S(2)}, u32[]{:S(2)}) %collective-permute-start) | collective-permute-done | bytes 32800 | tf_op jit(solution)/shard_map/ppermute | solution.py:495
  7.7 1.2 %collective-permute-start.2 = (f32[2,2,2,1024]{3,2,1,0:T(2,128)S(1)}, f32[2,2,2,1024]{3,2,1,0:T(2,128)S(1)}, u32[]{:S(2)}, u32[]{:S(2)}) collective-permute-start(f32[2,2,2,1024]{3,2,1,0:T(2,128)S(1)} %collective-permute-done.refs_0_.py_ref), channel_id=1, source_target_pairs={{0,1},{1,0},{2,3},{3,2},{4,5},{5,4},{6,7},{7,6},{8,9},{9,8},{10,11... | collective-permute-start | bytes 98312 | tf_op jit(solution)/shard_map/ppermute | solution.py:492
  8.9 0.5 %deposit.2 = (f32[2,128,128]{2,1,0:T(8,128)S(1)}, f32[1,2,2,1024]{3,2,1,0:T(2,128)S(1)}) custom-call(f32[2,2,2,1024]{3,2,1,0:T(2,128)S(1)} %collective-permute-done.refs_0_.py_ref, f32[2,128,128]{2,1,0:T(8,128)S(1)} %get-tuple-element.28.refs_1_), custom_call_target="tpu_custom_call" | custom-call | flops 10000000 | tf_op jit(solution)/shard_map/deposit/pallas_call | solution.py:171
  9.4 0.3 collective-permute-done.2.refs_0_.yc_ref.pyc_ref
  9.7 7.3 %collective-permute-start.4 = (f32[4,2,2,1024]{3,2,1,0:T(2,128)S(1)}, f32[4,2,2,1024]{3,2,1,0:T(2,128)S(1)}, u32[]{:S(2)}, u32[]{:S(2)}) collective-permute-start(f32[4,2,2,1024]{3,2,1,0:T(2,128)S(1)} %pack.1), channel_id=1, source_target_pairs={{0,8},{1,249},{2,10},{3,251},{4,12},{5,253},{6,14},{7,255},{8,16},... | collective-permute-start | bytes 196616 | tf_op jit(solution)/shard_map/ppermute | solution.py:503
  17.1 0.6 %deposit.3.own_ref = f32[2,128,128]{2,1,0:T(8,128)S(1)} custom-call(f32[2,2,2,1024]{3,2,1,0:T(2,128)S(1)} %collective-permute-done.2.refs_0_.yc_ref.pyc_ref, f32[2,128,128]{2,1,0:T(8,128)S(1)} %get-tuple-element.29.refs_1_), custom_call_target="tpu_custom_call" | custom-call | flops 10000000 | tf_op jit(solution)/shard_map/deposit/pallas_call | solution.py:171
  17.6 0.9 %collective-permute-start.3 = (f32[2,128,128]{2,1,0:T(8,128)S(1)}, f32[2,128,128]{2,1,0:T(8,128)S(1)}, u32[]{:S(2)}, u32[]{:S(2)}) collective-permute-start(f32[2,128,128]{2,1,0:T(8,128)S(1)} %deposit.3.own_ref), channel_id=1, source_target_pairs={{0,4},{1,253},{2,6},{3,255},{4,8},{5,1},{6,10},{7,3},{8,12},{9,5},... | collective-permute-start | bytes 393224 | tf_op jit(solution)/shard_map/ppermute | solution.py:503
  18.6 0.0 collective-permute-done.4.pos_ref
  18.6 1.6 %deposit_packed.1.r2_ref = f32[2,128,128]{2,1,0:T(8,128)S(1)} custom-call(f32[4,2,2,1024]{3,2,1,0:T(2,128)S(1)} %collective-permute-done.4.pos_ref), custom_call_target="tpu_custom_call" | custom-call | flops 99999997952 | tf_op jit(solution)/shard_map/deposit_packed/pallas_call | solution.py:220
  20.2 1.4 %collective-permute-done.3.r1_ref = f32[2,128,128]{2,1,0:T(8,128)S(1)} collective-permute-done((f32[2,128,128]{2,1,0:T(8,128)S(1)}, f32[2,128,128]{2,1,0:T(8,128)S(1)}, u32[]{:S(2)}, u32[]{:S(2)}) %collective-permute-start.3) | collective-permute-done | bytes 131104 | tf_op jit(solution)/shard_map/ppermute | solution.py:503
  21.5 0.3 collective-permute-start.5
  21.8 1.3 %collective-permute-done.5.both_ref = f32[4,128,128]{2,1,0:T(8,128)S(1)} collective-permute-done((f32[4,128,128]{2,1,0:T(8,128)S(1)}, f32[4,128,128]{2,1,0:T(8,128)S(1)}, u32[]{:S(2)}, u32[]{:S(2)}) %collective-permute-start.5) | collective-permute-done | bytes 262176 | tf_op jit(solution)/shard_map/ppermute | solution.py:492
  23.2 2.1 %field.1 = (bf16[256,384]{1,0:T(8,128)(2,1)S(1)}, f32[2,1024]{1,0:T(2,128)S(1)}) custom-call(f32[2,128,128]{2,1,0:T(8,128)S(1)} %deposit.3.own_ref, f32[2,128,128]{2,1,0:T(8,128)S(1)} %collective-permute-done.3.r1_ref, f32[2,128,128]{2,1,0:T(8,128)S(1)} %deposit_packed.1.r2_ref, f32[4,128,128]{2,1,0:T(8,128)S(1)} %collective-permute-done.5.both_ref, ...), custom_call_target="tpu_custom_call" | custom-call | tf_op jit(solution)/shard_map/field/pallas_call | solution.py:409
  25.2 0.3 collective-permute-start.6
  25.5 1.0 %kick.1 = (f32[2,2,1024]{2,1,0:T(2,128)S(1)}, f32[2,1024]{1,0:T(2,128)S(1)}) custom-call(bf16[256,384]{1,0:T(8,128)(2,1)S(1)} %get-tuple-element.40.maps_ref, f32[2,2,2,1024]{3,2,1,0:T(2,128)S(1)} %get-tuple-element.41.pa_ref, f32[2,2,2,1024]{3,2,1,0:T(2,128)S(1)} %collective-permute-done.1.pc_ref, f32[2,2,2,1024]{3,2,1,0:T(2,128)S(1)} %collective-permute-done.refs_0_.py_ref), custom_call_target="tpu_custom_call" | custom-call | tf_op jit(solution)/shard_map/kick/pallas_call | solution.py:447
  26.6 0.0 copy-start
  26.6 0.0 collective-permute-done.6
  26.6 2.6 %collective-permute-start.8 = (f32[2,2,1024]{2,1,0:T(2,128)S(1)}, f32[2,2,1024]{2,1,0:T(2,128)S(1)}, u32[]{:S(2)}, u32[]{:S(2)}) collective-permute-start(f32[2,2,1024]{2,1,0:T(2,128)S(1)} %pad_maximum_fusion.1), channel_id=1, source_target_pairs={{0,2},{1,3},{2,0},{3,1},{4,6},{5,7},{6,4},{7,5},{8,10},{9,11},{10,... | collective-permute-start | bytes 49160 | tf_op jit(solution)/shard_map/ppermute | solution.py:495
  29.2 0.7 %collective-permute-start.7 = (f32[2,2,1024]{2,1,0:T(2,128)S(1)}, f32[2,2,1024]{2,1,0:T(2,128)S(1)}, u32[]{:S(2)}, u32[]{:S(2)}) collective-permute-start(f32[2,2,1024]{2,1,0:T(2,128)S(1)} %get-tuple-element.45.mine_ref), channel_id=1, source_target_pairs={{0,1},{1,0},{2,3},{3,2},{4,5},{5,4},{6,7},{7,6},{8,9},{9,8},{10,11... | collective-permute-start | bytes 49160 | tf_op jit(solution)/shard_map/ppermute | solution.py:492
  29.9 0.9 %collective-permute-done.8.chip_ref = f32[2,2,1024]{2,1,0:T(2,128)S(1)} collective-permute-done((f32[2,2,1024]{2,1,0:T(2,128)S(1)}, f32[2,2,1024]{2,1,0:T(2,128)S(1)}, u32[]{:S(2)}, u32[]{:S(2)}) %collective-permute-start.8) | collective-permute-done | bytes 16416 | tf_op jit(solution)/shard_map/ppermute | solution.py:495
  30.8 0.0 collective-permute-done.7.core_ref
  30.8 0.0 copy-done
  30.8 0.6 %finish.1 = f32[2,2,2,1024]{3,2,1,0:T(2,128)} custom-call(f32[2,2,1024]{2,1,0:T(2,128)S(1)} %get-tuple-element.45.mine_ref, f32[2,2,1024]{2,1,0:T(2,128)S(1)} %collective-permute-done.7.core_ref, f32[2,2,1024]{2,1,0:T(2,128)S(1)} %collective-permute-done.8.chip_ref, f32[2,2,2,1024]{3,2,1,0:T(2,128)S(1)} %copy-done), custom_call_target="tpu_custom_call" | custom-call | tf_op jit(solution)/shard_map/finish/pallas_call | solution.py:477
  (3 shorter events, 0.0 us)
Async XLA Ops:
  0.0 4.4 %collective-permute-start.1 = (f32[2,2,2,1024]{3,2,1,0:T(2,128)}, f32[2,2,2,1024]{3,2,1,0:T(2,128)S(1)}, u32[]{:S(2)}, u32[]{:S(2)}) collective-permute-start(f32[2,2,2,1024]{3,2,1,0:T(2,128)} %pa_hbm.1), channel_id=1, source_target_pairs={{0,1},{1,0},{2,3},{3,2},{4,5},{5,4},{6,7},{7,6},{8,9},{9,8},{10,11... | collective-permute-start | bytes 98312 | tf_op jit(solution)/shard_map/ppermute | solution.py:492
  3.2 4.5 %collective-permute-start = (f32[2,2,2,1024]{3,2,1,0:T(2,128)}, f32[2,2,2,1024]{3,2,1,0:T(2,128)S(1)}, u32[]{:S(2)}, u32[]{:S(2)}) collective-permute-start(f32[2,2,2,1024]{3,2,1,0:T(2,128)} %pa_hbm.1), channel_id=1, source_target_pairs={{0,2},{1,3},{2,0},{3,1},{4,6},{5,7},{6,4},{7,5},{8,10},{9,11},{10,... | collective-permute-start | bytes 98312 | tf_op jit(solution)/shard_map/ppermute | solution.py:495
  7.7 2.0 %collective-permute-start.2 = (f32[2,2,2,1024]{3,2,1,0:T(2,128)S(1)}, f32[2,2,2,1024]{3,2,1,0:T(2,128)S(1)}, u32[]{:S(2)}, u32[]{:S(2)}) collective-permute-start(f32[2,2,2,1024]{3,2,1,0:T(2,128)S(1)} %collective-permute-done.refs_0_.py_ref), channel_id=1, source_target_pairs={{0,1},{1,0},{2,3},{3,2},{4,5},{5,4},{6,7},{7,6},{8,9},{9,8},{10,11... | collective-permute-start | bytes 98312 | tf_op jit(solution)/shard_map/ppermute | solution.py:492
  9.7 8.8 %collective-permute-start.4 = (f32[4,2,2,1024]{3,2,1,0:T(2,128)S(1)}, f32[4,2,2,1024]{3,2,1,0:T(2,128)S(1)}, u32[]{:S(2)}, u32[]{:S(2)}) collective-permute-start(f32[4,2,2,1024]{3,2,1,0:T(2,128)S(1)} %pack.1), channel_id=1, source_target_pairs={{0,8},{1,249},{2,10},{3,251},{4,12},{5,253},{6,14},{7,255},{8,16},... | collective-permute-start | bytes 196616 | tf_op jit(solution)/shard_map/ppermute | solution.py:503
  17.6 3.9 %collective-permute-start.3 = (f32[2,128,128]{2,1,0:T(8,128)S(1)}, f32[2,128,128]{2,1,0:T(8,128)S(1)}, u32[]{:S(2)}, u32[]{:S(2)}) collective-permute-start(f32[2,128,128]{2,1,0:T(8,128)S(1)} %deposit.3.own_ref), channel_id=1, source_target_pairs={{0,4},{1,253},{2,6},{3,255},{4,8},{5,1},{6,10},{7,3},{8,12},{9,5},... | collective-permute-start | bytes 393224 | tf_op jit(solution)/shard_map/ppermute | solution.py:503
  21.5 1.6 %collective-permute-start.5 = (f32[4,128,128]{2,1,0:T(8,128)S(1)}, f32[4,128,128]{2,1,0:T(8,128)S(1)}, u32[]{:S(2)}, u32[]{:S(2)}) collective-permute-start(f32[4,128,128]{2,1,0:T(8,128)S(1)} %pad_maximum_fusion), channel_id=1, source_target_pairs={{0,1},{1,0},{2,3},{3,2},{4,5},{5,4},{6,7},{7,6},{8,9},{9,8},{10,11... | collective-permute-start | bytes 786440 | tf_op jit(solution)/shard_map/ppermute | solution.py:492
  25.2 1.3 %collective-permute-start.6 = (f32[2,1024]{1,0:T(2,128)S(1)}, f32[2,1024]{1,0:T(2,128)S(1)}, u32[]{:S(2)}, u32[]{:S(2)}) collective-permute-start(f32[2,1024]{1,0:T(2,128)S(1)} %get-tuple-element.43), channel_id=1, source_target_pairs={{0,1},{1,0},{2,3},{3,2},{4,5},{5,4},{6,7},{7,6},{8,9},{9,8},{10,11... | collective-permute-start | bytes 24584 | tf_op jit(solution)/shard_map/ppermute | solution.py:492
  26.6 4.2 %copy-start = (f32[2,2,2,1024]{3,2,1,0:T(2,128)S(1)}, f32[2,2,2,1024]{3,2,1,0:T(2,128)}, u32[]{:S(2)}) copy-start(f32[2,2,2,1024]{3,2,1,0:T(2,128)} %momenta_ref.1) | copy-start | bytes 98308
  26.6 4.2 %collective-permute-start.8 = (f32[2,2,1024]{2,1,0:T(2,128)S(1)}, f32[2,2,1024]{2,1,0:T(2,128)S(1)}, u32[]{:S(2)}, u32[]{:S(2)}) collective-permute-start(f32[2,2,1024]{2,1,0:T(2,128)S(1)} %pad_maximum_fusion.1), channel_id=1, source_target_pairs={{0,2},{1,3},{2,0},{3,1},{4,6},{5,7},{6,4},{7,5},{8,10},{9,11},{10,... | collective-permute-start | bytes 49160 | tf_op jit(solution)/shard_map/ppermute | solution.py:495
  29.2 1.5 %collective-permute-start.7 = (f32[2,2,1024]{2,1,0:T(2,128)S(1)}, f32[2,2,1024]{2,1,0:T(2,128)S(1)}, u32[]{:S(2)}, u32[]{:S(2)}) collective-permute-start(f32[2,2,1024]{2,1,0:T(2,128)S(1)} %get-tuple-element.45.mine_ref), channel_id=1, source_target_pairs={{0,1},{1,0},{2,3},{3,2},{4,5},{5,4},{6,7},{7,6},{8,9},{9,8},{10,11... | collective-permute-start | bytes 49160 | tf_op jit(solution)/shard_map/ppermute | solution.py:492
